TPU v7x, 32 devices: a whole 2x2x4 slice. The times are simulated.
32 devices in a mesh: dp: 8 (over y, x, core), tensor: 4 (over z).
Axes of the slice: x: 2, y: 2, z: 4, core: 2. Of those that a mesh axis runs over, the one named last changes fastest.
Arguments:
- image_in: bfloat16 [16, 1024, 1536], P('dp', None, 'tensor'), may hold values from -6 to 6
- text_in: bfloat16 [16, 154, 1536], P('dp', None, 'tensor'), may hold values from -6 to 6
- condition: bfloat16 [16, 1536], P('dp'), may hold values from -5 to 5
- image_cot: bfloat16 [16, 1024, 1536], P('dp', None, 'tensor'), may hold values from -6 to 6
- text_cot: bfloat16 [16, 154, 1536], P('dp', None, 'tensor'), may hold values from -6 to 6
- qkv_weight: bfloat16 [2, 1536, 3, 1536], P(None, 'dp', None, 'tensor'), may hold values from -0.15625 to 0.15625
- qv_bias: bfloat16 [2, 2, 1536], P(None, None, 'tensor'), may hold values from -3 to 3
- proj_weight: bfloat16 [2, 1536, 1536], P(None, 'tensor', 'dp'), may hold values from -2.5 to 2.5
- proj_bias: bfloat16 [2, 1536], P(None, 'tensor'), may hold values from -3 to 3
- up_weight: bfloat16 [2, 1536, 6144], P(None, 'dp', 'tensor'), may hold values from -0.15625 to 0.15625
- up_bias: bfloat16 [2, 6144], P(None, 'tensor'), may hold values from -3 to 3
- down_weight: bfloat16 [2, 6144, 1536], P(None, 'tensor', 'dp'), may hold values from -0.078125 to 0.078125
- down_bias: bfloat16 [2, 1536], P(None, 'tensor'), may hold values from -3 to 3
- mod_weight: bfloat16 [2, 1536, 6, 1536], P(None, 'dp', None, 'tensor'), may hold values from -0.15625 to 0.15625
- mod_bias: bfloat16 [2, 6, 1536], P(None, None, 'tensor'), may hold values from -3 to 3
Outputs:
- image_out: bfloat16 [16, 1024, 1536], P('dp', None, 'tensor')
- text_out: bfloat16 [16, 154, 1536], P('dp', None, 'tensor')
- image_grad: float32 [16, 1024, 1536], P('dp', None, 'tensor')
- text_grad: float32 [16, 154, 1536], P('dp', None, 'tensor')
- condition_grad: float32 [16, 1536], P('dp')
- qkv_weight_grad: float32 [2, 1536, 3, 1536], P(None, 'dp', None, 'tensor')
- qv_bias_grad: float32 [2, 2, 1536], P(None, None, 'tensor')
- proj_weight_grad: float32 [2, 1536, 1536], P(None, 'tensor', 'dp')
- proj_bias_grad: float32 [2, 1536], P(None, 'tensor')
- up_weight_grad: float32 [2, 1536, 6144], P(None, 'dp', 'tensor')
- up_bias_grad: float32 [2, 6144], P(None, 'tensor')
- down_weight_grad: float32 [2, 6144, 1536], P(None, 'tensor', 'dp')
- down_bias_grad: float32 [2, 1536], P(None, 'tensor')
- mod_weight_grad: float32 [2, 1536, 6, 1536], P(None, 'dp', None, 'tensor')
- mod_bias_grad: float32 [2, 6, 1536], P(None, None, 'tensor')
All inputs are finite; a program needn't handle non-finite values.
Results may differ from a plain program's by a relative error of at most 0.017.
The roundings to bfloat16 on the way count: a program that leaves them out, or rounds other values in their place, can miss the bound.
Values may be sent and summed in bfloat16 or wider, within the bound.
No kernel may reach another device: no remote copies, remote signals or barrier semaphores. Data moves between devices by JAX's collectives and lax.ppermute only.
A program may use at most 176 MiB of HBM per device.

v0:
```python
import jax
import jax.numpy as jnp
from jax import lax
from jax.sharding import PartitionSpec as P

D = 1536
HEAD_DIM = 64


norm_eps = 1e-06


def gelu_tanh(values):
    return jax.nn.gelu(values, approximate=True)


def feature_gather(first_part, second_part):
    return (
        lax.all_gather(first_part, "tensor", axis=1, tiled=True),
        lax.all_gather(second_part, "tensor", axis=1, tiled=True),
    )


def partial_reduce(first_part, second_part):
    return (
        lax.psum_scatter(
            first_part.astype(jnp.bfloat16), "tensor", scatter_dimension=1, tiled=True
        ).astype(jnp.float32),
        lax.psum_scatter(
            second_part.astype(jnp.bfloat16), "tensor", scatter_dimension=1, tiled=True
        ).astype(jnp.float32),
    )


def row_totals(sum_one, sum_two, sum_three, sum_four):
    return lax.psum((sum_one, sum_two, sum_three, sum_four), "tensor")


def norm_forward(shares):
    totals = row_totals(
        jnp.sum(shares[0], axis=1),
        jnp.sum(shares[0] * shares[0], axis=1),
        jnp.sum(shares[1], axis=1),
        jnp.sum(shares[1] * shares[1], axis=1),
    )
    normed, factors = ([], [])
    for modality in range(2):
        average = (totals[2 * modality] / D)[:, None]
        spread = (totals[2 * modality + 1] / D)[:, None] - average * average
        factor = lax.rsqrt(spread + norm_eps)
        normed.append((shares[modality] - average) * factor)
        factors.append(factor)
    return (normed, factors)


def norm_backward(grads, normed, factors):
    totals = row_totals(
        jnp.sum(grads[0], axis=1),
        jnp.sum(grads[0] * normed[0], axis=1),
        jnp.sum(grads[1], axis=1),
        jnp.sum(grads[1] * normed[1], axis=1),
    )
    result = []
    for modality in range(2):
        grad_mean = (totals[2 * modality] / D)[:, None]
        cross_mean = (totals[2 * modality + 1] / D)[:, None]
        result.append(
            factors[modality] * (grads[modality] - grad_mean - normed[modality] * cross_mean)
        )
    return result


def head_forward(operands):
    queries, keys_in, values_in = operands
    scores = jnp.einsum(
        "qd,kd->qk", queries, keys_in, preferred_element_type=jnp.float32
    ) * HEAD_DIM ** (-0.5)
    highest = jnp.max(scores, axis=1, keepdims=True)
    log_total = highest + jnp.log(jnp.sum(jnp.exp(scores - highest), axis=1, keepdims=True))
    soft_low = jnp.exp(scores - log_total).astype(jnp.bfloat16)
    attended = jnp.einsum("qk,kd->qd", soft_low, values_in, preferred_element_type=jnp.float32)
    return (attended, log_total[:, 0])


def head_backward(operands):
    queries, keys_in, values_in, log_total, upstream = operands
    score_scale = HEAD_DIM ** (-0.5)
    scores = (
        jnp.einsum("qd,kd->qk", queries, keys_in, preferred_element_type=jnp.float32) * score_scale
    )
    soft_full = jnp.exp(scores - log_total[:, None])
    soft_low = soft_full.astype(jnp.bfloat16)
    grad_soft = jnp.einsum("qd,kd->qk", upstream, values_in, preferred_element_type=jnp.float32)
    row_inner = jnp.sum(soft_full * grad_soft, axis=1, keepdims=True)
    grad_scores = (soft_full * (grad_soft - row_inner)).astype(jnp.bfloat16)
    grad_query = (
        jnp.einsum("qk,kd->qd", grad_scores, keys_in, preferred_element_type=jnp.float32)
        * score_scale
    ).astype(jnp.bfloat16)
    grad_key = (
        jnp.einsum("qk,qd->kd", grad_scores, queries, preferred_element_type=jnp.float32)
        * score_scale
    ).astype(jnp.bfloat16)
    grad_value = jnp.einsum(
        "qk,qd->kd", soft_low, upstream, preferred_element_type=jnp.float32
    ).astype(jnp.bfloat16)
    return (grad_query, grad_key, grad_value)


def split_heads(rows):
    return rows.reshape(rows.shape[0], -1, HEAD_DIM).transpose(1, 0, 2)


def join_heads(heads):
    return heads.transpose(1, 0, 2).reshape(heads.shape[1], -1)


def column_sum(values):
    return jnp.sum(values.astype(jnp.float32), axis=0)


def one_sample(inputs, cotangents, modulation, gathered, biases):
    qkv_full, proj_full, up_full, down_full = gathered
    qv_bias, proj_bias, up_bias, down_bias = biases
    image_count = inputs[0].shape[0]
    residual = [piece.astype(jnp.float32) for piece in inputs]
    normed_one, factors_one = norm_forward(residual)
    shifted = [
        (normed_one[modality] * (1.0 + modulation[modality, 1]) + modulation[modality, 0]).astype(
            jnp.bfloat16
        )
        for modality in range(2)
    ]
    attn_in = feature_gather(shifted[0], shifted[1])
    query_rows, key_rows, value_rows = ([], [], [])
    for modality in range(2):
        projected = jnp.einsum(
            "ni,icj->ncj", attn_in[modality], qkv_full[modality], preferred_element_type=jnp.float32
        )
        query_rows.append((projected[:, 0] + qv_bias[modality, 0]).astype(jnp.bfloat16))
        key_rows.append(projected[:, 1].astype(jnp.bfloat16))
        value_rows.append((projected[:, 2] + qv_bias[modality, 1]).astype(jnp.bfloat16))
    query_heads = split_heads(jnp.concatenate(query_rows, 0))
    key_heads = split_heads(jnp.concatenate(key_rows, 0))
    value_heads = split_heads(jnp.concatenate(value_rows, 0))
    attended_heads, log_total = lax.map(head_forward, (query_heads, key_heads, value_heads))
    attended = join_heads(attended_heads).astype(jnp.bfloat16)
    pieces = (attended[:image_count], attended[image_count:])
    reduced_one = partial_reduce(
        jnp.dot(pieces[0], proj_full[0], preferred_element_type=jnp.float32),
        jnp.dot(pieces[1], proj_full[1], preferred_element_type=jnp.float32),
    )
    branch_one = [reduced_one[modality] + proj_bias[modality] for modality in range(2)]
    middle = [
        residual[modality] + modulation[modality, 2] * branch_one[modality] for modality in range(2)
    ]
    normed_two, factors_two = norm_forward(middle)
    shifted_two = [
        (normed_two[modality] * (1.0 + modulation[modality, 4]) + modulation[modality, 3]).astype(
            jnp.bfloat16
        )
        for modality in range(2)
    ]
    mlp_in = feature_gather(shifted_two[0], shifted_two[1])
    pre_act = [
        jnp.dot(mlp_in[modality], up_full[modality], preferred_element_type=jnp.float32)
        + up_bias[modality]
        for modality in range(2)
    ]
    activated = [gelu_tanh(pre_act[modality]).astype(jnp.bfloat16) for modality in range(2)]
    reduced_two = partial_reduce(
        jnp.dot(activated[0], down_full[0], preferred_element_type=jnp.float32),
        jnp.dot(activated[1], down_full[1], preferred_element_type=jnp.float32),
    )
    branch_two = [reduced_two[modality] + down_bias[modality] for modality in range(2)]
    outputs = [
        (middle[modality] + modulation[modality, 5] * branch_two[modality]).astype(jnp.bfloat16)
        for modality in range(2)
    ]
    upstream = [piece.astype(jnp.float32) for piece in cotangents]
    grad_gate_two = [
        jnp.sum(upstream[modality] * branch_two[modality], axis=0) for modality in range(2)
    ]
    grad_two = [
        (modulation[modality, 5] * upstream[modality]).astype(jnp.bfloat16) for modality in range(2)
    ]
    grad_two_full = feature_gather(grad_two[0], grad_two[1])
    down_grad = jnp.stack(
        [
            jnp.einsum(
                "nf,nd->fd",
                activated[modality],
                grad_two_full[modality],
                preferred_element_type=jnp.float32,
            )
            for modality in range(2)
        ]
    )
    grad_pre = []
    for modality in range(2):
        grad_act = jnp.einsum(
            "nd,fd->nf",
            grad_two_full[modality],
            down_full[modality],
            preferred_element_type=jnp.float32,
        )
        grad_pre.append(jax.vjp(gelu_tanh, pre_act[modality])[1](grad_act)[0].astype(jnp.bfloat16))
    up_grad = jnp.stack(
        [
            jnp.einsum(
                "ni,nf->if",
                mlp_in[modality],
                grad_pre[modality],
                preferred_element_type=jnp.float32,
            )
            for modality in range(2)
        ]
    )
    grad_mlp = partial_reduce(
        jnp.einsum("nf,if->ni", grad_pre[0], up_full[0], preferred_element_type=jnp.float32),
        jnp.einsum("nf,if->ni", grad_pre[1], up_full[1], preferred_element_type=jnp.float32),
    )
    grad_shift_two = [jnp.sum(grad_mlp[modality], axis=0) for modality in range(2)]
    grad_scale_two = [
        jnp.sum(grad_mlp[modality] * normed_two[modality], axis=0) for modality in range(2)
    ]
    through_two = norm_backward(
        [grad_mlp[modality] * (1.0 + modulation[modality, 4]) for modality in range(2)],
        normed_two,
        factors_two,
    )
    grad_middle = [upstream[modality] + through_two[modality] for modality in range(2)]
    grad_gate_one = [
        jnp.sum(grad_middle[modality] * branch_one[modality], axis=0) for modality in range(2)
    ]
    grad_one = [
        (modulation[modality, 2] * grad_middle[modality]).astype(jnp.bfloat16)
        for modality in range(2)
    ]
    grad_one_full = feature_gather(grad_one[0], grad_one[1])
    proj_grad = jnp.stack(
        [
            jnp.einsum(
                "nc,nd->cd",
                pieces[modality],
                grad_one_full[modality],
                preferred_element_type=jnp.float32,
            )
            for modality in range(2)
        ]
    )
    grad_attended = jnp.concatenate(
        [
            jnp.einsum(
                "nd,cd->nc",
                grad_one_full[modality],
                proj_full[modality],
                preferred_element_type=jnp.float32,
            )
            for modality in range(2)
        ],
        0,
    ).astype(jnp.bfloat16)
    grad_queries, grad_keys, grad_values = lax.map(
        head_backward, (query_heads, key_heads, value_heads, log_total, split_heads(grad_attended))
    )
    grad_queries = join_heads(grad_queries)
    grad_keys = join_heads(grad_keys)
    grad_values = join_heads(grad_values)
    grad_qkv = [
        jnp.stack(
            [grad_queries[:image_count], grad_keys[:image_count], grad_values[:image_count]], axis=1
        ),
        jnp.stack(
            [grad_queries[image_count:], grad_keys[image_count:], grad_values[image_count:]], axis=1
        ),
    ]
    qkv_grad = jnp.stack(
        [
            jnp.einsum(
                "ni,ncj->icj",
                attn_in[modality],
                grad_qkv[modality],
                preferred_element_type=jnp.float32,
            )
            for modality in range(2)
        ]
    )
    qv_grad = jnp.stack(
        [
            jnp.stack([column_sum(grad_qkv[modality][:, 0]), column_sum(grad_qkv[modality][:, 2])])
            for modality in range(2)
        ]
    )
    grad_attn = partial_reduce(
        jnp.einsum("ncj,icj->ni", grad_qkv[0], qkv_full[0], preferred_element_type=jnp.float32),
        jnp.einsum("ncj,icj->ni", grad_qkv[1], qkv_full[1], preferred_element_type=jnp.float32),
    )
    grad_shift_one = [jnp.sum(grad_attn[modality], axis=0) for modality in range(2)]
    grad_scale_one = [
        jnp.sum(grad_attn[modality] * normed_one[modality], axis=0) for modality in range(2)
    ]
    through_one = norm_backward(
        [grad_attn[modality] * (1.0 + modulation[modality, 1]) for modality in range(2)],
        normed_one,
        factors_one,
    )
    input_grads = [grad_middle[modality] + through_one[modality] for modality in range(2)]
    grad_mod = jnp.stack(
        [
            jnp.stack(
                [
                    grad_shift_one[modality],
                    grad_scale_one[modality],
                    grad_gate_one[modality],
                    grad_shift_two[modality],
                    grad_scale_two[modality],
                    grad_gate_two[modality],
                ]
            )
            for modality in range(2)
        ]
    )
    bias_grads = (
        qv_grad,
        jnp.stack([column_sum(grad_one[modality]) for modality in range(2)]),
        jnp.stack([column_sum(grad_pre[modality]) for modality in range(2)]),
        jnp.stack([column_sum(grad_two[modality]) for modality in range(2)]),
    )
    return (outputs, input_grads, grad_mod, (qkv_grad, proj_grad, up_grad, down_grad), bias_grads)


def add_trees(current, update):
    if current is None:
        return update
    return jax.tree.map(jnp.add, current, update)


def per_device(
    image_in,
    text_in,
    condition,
    image_cot,
    text_cot,
    qkv_weight,
    qv_bias,
    proj_weight,
    proj_bias,
    up_weight,
    up_bias,
    down_weight,
    down_bias,
    mod_weight,
    mod_bias,
):
    micro = image_in.shape[0]
    cond_all = lax.all_gather(condition, "dp", axis=0, tiled=True)
    silu_all = jax.nn.silu(cond_all.astype(jnp.float32)).astype(jnp.bfloat16)
    row_count = mod_weight.shape[1]
    silu_rows = lax.dynamic_slice_in_dim(silu_all, lax.axis_index("dp") * row_count, row_count, 1)
    mod_terms = jnp.einsum(
        "bi,sicj->bscj", silu_rows, mod_weight, preferred_element_type=jnp.float32
    )
    modulation = (
        lax.psum_scatter(mod_terms, "dp", scatter_dimension=0, tiled=True)
        + mod_bias.astype(jnp.float32)[None]
    )
    biases = (
        qv_bias.astype(jnp.float32),
        proj_bias.astype(jnp.float32),
        up_bias.astype(jnp.float32),
        down_bias.astype(jnp.float32),
    )
    records = []
    bias_sums = None
    weight_sums = None
    for index in range(micro):
        record = one_sample(
            (image_in[index], text_in[index]),
            (image_cot[index], text_cot[index]),
            modulation[index],
            (
                lax.all_gather(qkv_weight, "dp", axis=1, tiled=True),
                lax.all_gather(proj_weight, "dp", axis=2, tiled=True),
                lax.all_gather(up_weight, "dp", axis=1, tiled=True),
                lax.all_gather(down_weight, "dp", axis=2, tiled=True),
            ),
            biases,
        )
        grads = record[3]
        weight_sums = add_trees(
            weight_sums,
            (
                lax.psum_scatter(grads[0], "dp", scatter_dimension=1, tiled=True),
                lax.psum_scatter(grads[1], "dp", scatter_dimension=2, tiled=True),
                lax.psum_scatter(grads[2], "dp", scatter_dimension=1, tiled=True),
                lax.psum_scatter(grads[3], "dp", scatter_dimension=2, tiled=True),
            ),
        )
        bias_sums = add_trees(bias_sums, record[4])
        records.append(record)
    image_out = jnp.stack([record[0][0] for record in records])
    text_out = jnp.stack([record[0][1] for record in records])
    image_grad = jnp.stack([record[1][0] for record in records])
    text_grad = jnp.stack([record[1][1] for record in records])
    grad_mod_low = jnp.stack([record[2] for record in records]).astype(jnp.bfloat16)
    mod_bias_local = jnp.sum(grad_mod_low.astype(jnp.float32), axis=0)
    grad_mod_all = lax.all_gather(grad_mod_low, "dp", axis=0, tiled=True)
    mod_weight_grad = jnp.einsum(
        "bi,bscj->sicj", silu_rows, grad_mod_all, preferred_element_type=jnp.float32
    )
    silu_grad_rows = jnp.einsum(
        "bscj,sicj->bi", grad_mod_all, mod_weight, preferred_element_type=jnp.float32
    )
    silu_grad_mine = lax.all_to_all(silu_grad_rows, "dp", split_axis=0, concat_axis=1, tiled=True)
    silu_grad = lax.psum(silu_grad_mine, "tensor")
    condition_grad = jax.vjp(jax.nn.silu, condition.astype(jnp.float32))[1](silu_grad)[0]
    qv_total, proj_bias_total, up_bias_total, down_bias_total, mod_bias_total = lax.psum(
        (bias_sums[0], bias_sums[1], bias_sums[2], bias_sums[3], mod_bias_local), "dp"
    )
    return (
        image_out,
        text_out,
        image_grad,
        text_grad,
        condition_grad,
        weight_sums[0],
        qv_total,
        weight_sums[1],
        proj_bias_total,
        weight_sums[2],
        up_bias_total,
        weight_sums[3],
        down_bias_total,
        mod_weight_grad,
        mod_bias_total,
    )


def solution(mesh):
    placed = (
        P("dp", None, "tensor"),
        P("dp", None, "tensor"),
        P("dp", None),
        P("dp", None, "tensor"),
        P("dp", None, "tensor"),
        P(None, "dp", None, "tensor"),
        P(None, None, "tensor"),
        P(None, "tensor", "dp"),
        P(None, "tensor"),
        P(None, "dp", "tensor"),
        P(None, "tensor"),
        P(None, "tensor", "dp"),
        P(None, "tensor"),
        P(None, "dp", None, "tensor"),
        P(None, None, "tensor"),
    )
    return jax.shard_map(
        per_device,
        mesh=mesh,
        in_specs=placed,
        out_specs=(
            P("dp", None, "tensor"),
            P("dp", None, "tensor"),
            P("dp", None, "tensor"),
            P("dp", None, "tensor"),
            P("dp", None),
            P(None, "dp", None, "tensor"),
            P(None, None, "tensor"),
            P(None, "tensor", "dp"),
            P(None, "tensor"),
            P(None, "dp", "tensor"),
            P(None, "tensor"),
            P(None, "tensor", "dp"),
            P(None, "tensor"),
            P(None, "dp", None, "tensor"),
            P(None, None, "tensor"),
        ),
        check_vma=False,
    )
```

profile of v0, /device:TPU:0, one launch (start us, length us, event | category | flops | bytes accessed | tf_op | source)
XLA Modules:
  0.0 2238.6 jit_solution(7022137310497590826)
XLA Ops:
  46.7 26.2 %all-reduce.12.cloned.1.call-done = f32[16,2,6,384]{3,0,2,1:T(8,128)} async-done(((f32[16,2,6,384]{3,0,2,1:T(8,128)}), f32[16,2,6,384]{3,0,2,1:T(8,128)}) %all-reduce.12.cloned.1.call-update) | async-done | bytes 294928
  161.3 28.6 %all-gather.14.cloned.1.call-done = bf16[1024,1536]{1,0:T(8,128)(2,1)} async-done(((bf16[1024,384]{1,0:T(8,128)(2,1)}), bf16[1024,1536]{1,0:T(8,128)(2,1)}) %all-gather.14.cloned.1.call-update) | async-done | bytes 3145744 | tf_op jit(solution)/shard_map/all_gather | solution.py:19
  202.3 51.6 %all-gather.26.cloned.1.call-done = bf16[1024,1536]{1,0:T(8,128)(2,1)} async-done(((bf16[1024,384]{1,0:T(8,128)(2,1)}), bf16[1024,1536]{1,0:T(8,128)(2,1)}) %all-gather.26.cloned.1.call-update) | async-done | bytes 3145744 | tf_op jit(solution)/shard_map/all_gather | solution.py:19
  315.6 38.1 %while.52 = (s32[]{:T(128)}, bf16[6,1178,64]{1,2,0:T(8,128)(2,1)}, f32[6,1178]{1,0:T(8,128)S(1)}, bf16[6,1178,64]{2,1,0:T(8,128)(2,1)}, bf16[6,1178,64]{2,1,0:T(...) while((s32[]{:T(128)}, bf16[6,1178,64]{1,2,0:T(8,128)(2,1)}, ...), condition=%wide.region_12.13_spmd, body=%wide.region_9.12_spmd.sunk | while | flops 363572032 | bytes 25695688 | solution.py:146
  366.8 30.8 %while.53 = (s32[]{:T(128)}, bf16[6,1178,64]{1,2,0:T(8,128)(2,1)S(1)}, f32[6,1178]{1,0:T(8,128)S(1)}, bf16[6,1178,64]{2,1,0:T(8,128)(2,1)}, bf16[6,1178,64]{2,1,...) while((s32[]{:T(128)}, bf16[6,1178,64]{1,2,0:T(8,128)(2,1)S(1)}, ...), condition=%wide.region_30.31_spmd, body=%wide.region_27.30_spmd.sunk | while | flops 363572032 | bytes 18458000 | solution.py:146
  430.4 55.7 %reduce-scatter.56.cloned.1.call-done = bf16[384,1024]{1,0:T(8,128)(2,1)} async-done(((bf16[1536,1024]{1,0:T(8,128)(2,1)}), bf16[384,1024]{1,0:T(8,128)(2,1)}) %reduce-scatter.56.cloned.1.call-update) | async-done | bytes 786448
  488.5 60.2 %reduce-scatter.60.cloned.1.call-done = bf16[384,1024]{1,0:T(8,128)(2,1)} async-done(((bf16[1536,1024]{1,0:T(8,128)(2,1)}), bf16[384,1024]{1,0:T(8,128)(2,1)}) %reduce-scatter.60.cloned.1.call-update) | async-done | bytes 786448
  638.9 31.3 %all-gather.24.cloned.1.call-done = bf16[2,1536,1536]{1,2,0:T(8,128)(2,1)} async-done(((bf16[2,1536,192]{1,2,0:T(8,128)(2,1)}), bf16[2,1536,1536]{1,2,0:T(8,128)(2,1)}) %all-gather.24.cloned.1.call-update) | async-done | bytes 9437200 | tf_op jit(solution)/shard_map/all_gather | solution.py:386
  680.5 23.8 %all_gather.82 = bf16[154,1536]{1,0:T(8,128)(2,1)} all-gather(bf16[154,384]{1,0:T(8,128)(2,1)} %get-tuple-element.595), channel_id=1, replica_groups=mesh['dp'=8,'tensor'=4] {'tensor'}, dimensions={1}, use_global_device_ids=true | all-gather | bytes 591360 | tf_op jit(solution)/shard_map/all_gather | solution.py:20
  718.9 24.5 %all-gather.20.cloned.1.call-done = bf16[1024,1536]{1,0:T(8,128)(2,1)} async-done(((bf16[1024,384]{1,0:T(8,128)(2,1)}), bf16[1024,1536]{1,0:T(8,128)(2,1)}) %all-gather.20.cloned.1.call-update) | async-done | bytes 3145744 | tf_op jit(solution)/shard_map/all_gather | solution.py:19
  753.0 54.5 %all-gather.30.cloned.1.call-done = bf16[1024,1536]{1,0:T(8,128)(2,1)} async-done(((bf16[1024,384]{1,0:T(8,128)(2,1)}), bf16[1024,1536]{1,0:T(8,128)(2,1)}) %all-gather.30.cloned.1.call-update) | async-done | bytes 3145744 | tf_op jit(solution)/shard_map/all_gather | solution.py:19
  835.8 35.7 %all-gather.28.cloned.1.call-done = bf16[1024,1536]{1,0:T(8,128)(2,1)} async-done(((bf16[1024,384]{1,0:T(8,128)(2,1)}), bf16[1024,1536]{1,0:T(8,128)(2,1)}) %all-gather.28.cloned.1.call-update) | async-done | bytes 3145744 | tf_op jit(solution)/shard_map/all_gather | solution.py:19
  881.2 53.6 %all-gather.34.cloned.1.call-done = bf16[1024,1536]{1,0:T(8,128)(2,1)} async-done(((bf16[1024,384]{1,0:T(8,128)(2,1)}), bf16[1024,1536]{1,0:T(8,128)(2,1)}) %all-gather.34.cloned.1.call-update) | async-done | bytes 3145744 | tf_op jit(solution)/shard_map/all_gather | solution.py:19
  1013.6 31.8 %reduce-scatter.72.cloned.1.call-done = bf16[384,1024]{1,0:T(8,128)(2,1)} async-done(((bf16[1536,1024]{1,0:T(8,128)(2,1)}), bf16[384,1024]{1,0:T(8,128)(2,1)}) %reduce-scatter.72.cloned.1.call-update) | async-done | bytes 786448
  1047.7 60.3 %reduce-scatter.78.cloned.1.call-done = bf16[384,1024]{1,0:T(8,128)(2,1)} async-done(((bf16[1536,1024]{1,0:T(8,128)(2,1)}), bf16[384,1024]{1,0:T(8,128)(2,1)}) %reduce-scatter.78.cloned.1.call-update) | async-done | bytes 786448
  1110.3 60.2 %reduce-scatter.62.cloned.1.call-done = bf16[384,1024]{1,0:T(8,128)(2,1)} async-done(((bf16[1536,1024]{1,0:T(8,128)(2,1)}), bf16[384,1024]{1,0:T(8,128)(2,1)}) %reduce-scatter.62.cloned.1.call-update) | async-done | bytes 786448
  1172.8 60.3 %reduce-scatter.58.cloned.1.call-done = bf16[384,1024]{1,0:T(8,128)(2,1)} async-done(((bf16[1536,1024]{1,0:T(8,128)(2,1)}), bf16[384,1024]{1,0:T(8,128)(2,1)}) %reduce-scatter.58.cloned.1.call-update) | async-done | bytes 786448
  1368.1 79.8 %while.55 = (s32[]{:T(128)}, bf16[6,1178,64]{1,2,0:T(8,128)(2,1)S(1)}, bf16[6,1178,64]{1,2,0:T(8,128)(2,1)}, bf16[6,1178,64]{1,2,0:T(8,128)(2,1)}, bf16[6,1178,6...) while((s32[]{:T(128)}, ...), condition=%wide.region_79.80_spmd, body=%wide.region_77.79_spmd.sunk | while | flops 899595008 | bytes 44249704 | solution.py:264
  1464.0 79.6 %while.54 = (s32[]{:T(128)}, bf16[6,1178,64]{1,2,0:T(8,128)(2,1)S(1)}, bf16[6,1178,64]{1,2,0:T(8,128)(2,1)}, bf16[6,1178,64]{1,2,0:T(8,128)(2,1)}, bf16[6,1178,6...) while((s32[]{:T(128)}, ...), condition=%wide.region_61.62_spmd, body=%wide.region_59.61_spmd.sunk | while | flops 899595008 | bytes 44249704 | solution.py:264
  1632.4 28.7 %copy.259 = f32[2,1536,1536]{1,0,2:T(2,128)} copy(f32[2,1536,1536]{2,1,0:T(8,128)} %maximum_add_fusion.1) | data formatting | bytes 37748736 | tf_op jit(solution)/shard_map/add | solution.py:336
  1809.0 27.6 %all-reduce.3 = (f32[2,2,384]{2,1,0:T(2,128)}, f32[2,384]{1,0:T(2,128)}, f32[2,1536]{1,0:T(2,128)}, f32[2,384]{1,0:T(2,128)}, f32[2,6,384]{2,0,1:T(2,128)}) all-reduce(f32[2,2,384]{2,1,0:T(2,128)} %maximum_add_fusion.5, f32[2,384]{1,0:T(2,128)} %maximum_add_fusion.6, ...), channel_id=1, replica_groups=mesh['dp'=8,'tensor'=4] {'dp'}, use_global_device_ids=true, to_apply=%region_130.131 | all-reduce | flops 10752 | bytes 86016 | tf_op jit(solution)/shard_map/psum | solution.py:418
  1865.8 130.6 %all-reduce.14.cloned.1.call-done = (f32[2,384,1536]{1,0,2:T(2,128)}, f32[2,1536,1536]{1,0,2:T(2,128)}) async-done(((f32[2,384,1536]{1,0,2:T(2,128)}, f32[2,1536,1536]{1,0,2:T(2,128)}), (f32[2,384,1536]{1,0,2:T(2,128)}, f32[2,1536,1536]{1,0,2:T(2,128)})) %all-reduce.14.cloned.1.call-update) | async-done | bytes 23592976
  2002.8 124.0 %reduce-scatter.54.cloned.1.call-done = f32[2,192,1536]{2,1,0:T(8,128)} async-done(((f32[2,1536,1536]{2,1,0:T(8,128)}), f32[2,192,1536]{2,1,0:T(8,128)}) %reduce-scatter.54.cloned.1.call-update) | async-done | bytes 2359312 | tf_op jit(solution)/shard_map/reduce_scatter | solution.py:396
  2126.9 105.0 %reduce-scatter.52.cloned.1.call-done = f32[2,192,3,384]{3,1,2,0:T(8,128)} async-done(((f32[2,1536,3,384]{3,1,2,0:T(8,128)}), f32[2,192,3,384]{3,1,2,0:T(8,128)}) %reduce-scatter.52.cloned.1.call-update) | async-done | bytes 1769488 | tf_op jit(solution)/shard_map/reduce_scatter | solution.py:394
  (1002 shorter events, 1145.4 us)
Async XLA Ops:
  77.5 277.8 %all-gather.18.cloned.1.call-start = ((), (), s32[]{:S(2)}) async-start(), calls=%async_computation.21 | async-start | bytes 2654208 | tf_op jit(solution)/shard_map/all_gather | solution.py:384
  78.1 347.7 %reduce-scatter.64.cloned.1.call-start = ((), (), s32[]{:S(2)}) async-start(), calls=%async_computation.37 | async-start | bytes 983040
  424.3 210.2 %all-gather.22.cloned.1.call-start = ((), (), s32[]{:S(2)}) async-start(), calls=%async_computation.23 | async-start | bytes 10616832 | tf_op jit(solution)/shard_map/all_gather | solution.py:385
  424.9 245.2 %all-gather.24.cloned.1.call-start = ((), (), s32[]{:S(2)}) async-start(), calls=%async_computation.24 | async-start | bytes 10616832 | tf_op jit(solution)/shard_map/all_gather | solution.py:386
  425.6 317.7 %all-gather.20.cloned.1.call-start = ((), (), s32[]{:S(2)}) async-start(), calls=%async_computation.22 | async-start | bytes 3932160 | tf_op jit(solution)/shard_map/all_gather | solution.py:19
  575.7 231.8 %all-gather.30.cloned.1.call-start = ((), (), s32[]{:S(2)}) async-start(), calls=%async_computation.27 | async-start | bytes 3932160 | tf_op jit(solution)/shard_map/all_gather | solution.py:19
  579.4 292.1 %all-gather.28.cloned.1.call-start = ((), (), s32[]{:S(2)}) async-start(), calls=%async_computation.26 | async-start | bytes 3932160 | tf_op jit(solution)/shard_map/all_gather | solution.py:19
  579.9 354.9 %all-gather.34.cloned.1.call-start = ((), (), s32[]{:S(2)}) async-start(), calls=%async_computation.29 | async-start | bytes 3932160 | tf_op jit(solution)/shard_map/all_gather | solution.py:19
  580.5 427.5 %reduce-scatter.74.cloned.1.call-start = ((), (), s32[]{:S(2)}) async-start(), calls=%async_computation.42 | async-start | bytes 983040
  704.3 305.4 %reduce-scatter.80.cloned.1.call-start = ((), (), s32[]{:S(2)}) async-start(), calls=%async_computation.45 | async-start | bytes 983040
  718.8 326.6 %reduce-scatter.72.cloned.1.call-start = ((), (), s32[]{:S(2)}) async-start(), calls=%async_computation.41 | async-start | bytes 3932160
  835.3 272.7 %reduce-scatter.78.cloned.1.call-start = ((), (), s32[]{:S(2)}) async-start(), calls=%async_computation.44 | async-start | bytes 3932160
  962.5 208.0 %reduce-scatter.62.cloned.1.call-start = ((), (), s32[]{:S(2)}) async-start(), calls=%async_computation.36 | async-start | bytes 3932160
  977.6 255.5 %reduce-scatter.58.cloned.1.call-start = ((), (), s32[]{:S(2)}) async-start(), calls=%async_computation.34 | async-start | bytes 3932160
  992.9 280.4 %reduce-scatter.70.cloned.1.call-start = ((), (), s32[]{:S(2)}) async-start(), calls=%async_computation.40 | async-start | bytes 983040
  1000.5 284.0 %reduce-scatter.66.cloned.1.call-start = ((), (), s32[]{:S(2)}) async-start(), calls=%async_computation.38 | async-start | bytes 983040
  1008.0 353.3 %all-gather.36.cloned.1.call-start = ((), (), s32[]{:S(2)}) async-start(), calls=%async_computation.30 | async-start | bytes 3932160 | tf_op jit(solution)/shard_map/all_gather | solution.py:19
  1338.7 426.8 %reduce-scatter.86.cloned.1.call-start = ((), (), s32[]{:S(2)}) async-start(), calls=%async_computation.48 | async-start | bytes 983040
  1456.8 310.4 %reduce-scatter.84.cloned.1.call-start = ((), (), s32[]{:S(2)}) async-start(), calls=%async_computation.47 | async-start | bytes 983040
  1552.5 223.7 %reduce-scatter.76.cloned.1.call-start = ((), (), s32[]{:S(2)}) async-start(), calls=%async_computation.43 | async-start | bytes 3932160
  1573.5 205.2 %reduce-scatter.82.cloned.1.call-start = ((), (), s32[]{:S(2)}) async-start(), calls=%async_computation.46 | async-start | bytes 3932160
  1595.3 401.1 %all-reduce.14.cloned.1.call-start = ((), (), s32[]{:S(2)}) async-start(), calls=%async_computation.50 | async-start | bytes 47185920
  1678.5 448.3 %reduce-scatter.54.cloned.1.call-start = ((), (), s32[]{:S(2)}) async-start(), calls=%async_computation.32 | async-start | bytes 21233664 | tf_op jit(solution)/shard_map/reduce_scatter | solution.py:396
  1712.4 519.4 %reduce-scatter.52.cloned.1.call-start = ((), (), s32[]{:S(2)}) async-start(), calls=%async_computation.31 | async-start | bytes 15925248 | tf_op jit(solution)/shard_map/reduce_scatter | solution.py:394
  (216 other events, 6974.8 us)
Sparse Core Ops, SparseCore 0:
  19.5 53.3 all-reduce.11
  75.3 49.0 all-gather.15
  126.5 63.3 all-gather.13
  191.9 61.8 all-gather.25
  255.6 27.5 all-gather.17
  426.6 59.5 reduce-scatter.55
  488.4 60.2 reduce-scatter.59
  550.5 58.8 all-gather.21
  611.3 58.8 all-gather.23
  672.1 71.1 all-gather.19
  745.5 61.9 all-gather.29
  809.5 61.9 all-gather.27
  872.9 61.9 all-gather.33
  985.9 59.4 reduce-scatter.71
  1047.7 60.2 reduce-scatter.77
  1110.2 60.2 reduce-scatter.61
  1172.8 60.2 reduce-scatter.57
  1286.0 75.2 all-gather.35
  1363.4 62.2 all-gather.31
  1577.7 59.5 reduce-scatter.75
  1639.6 60.2 reduce-scatter.81
  1703.8 292.6 all-reduce.13
  2000.6 126.2 reduce-scatter.53
  2131.0 100.7 reduce-scatter.51
  (8 shorter events, 179.5 us)
where the time goes:
time: 2250 us; the launch traced here: 2240 us
  waiting for transfers between devices  1040 us (46%)
  matrix products  432 us (19%)
  local copies, waits for them, and re-layouts  308 us (14%)
  blocking collectives  268 us (12%)
  other arithmetic  164 us (7%)
    unnamed x50, waiting for transfers between devices  499 us
    all_gather x8, waiting for transfers between devices, feature_gather(): lax.all_gather(first_part, 'tensor', axis=1, tiled=True)  271 us
    all_gather x8, blocking collectives, feature_gather(): lax.all_gather(second_part, 'tensor', axis=1, tiled=True)  144 us
    unnamed x432, local copies, waits for them, and re-layouts  137 us
    reduce_scatter x1, waiting for transfers between devices, per_device(): lax.psum_scatter(grads[2], 'dp', scatter_dimension=1, tiled=True)  124 us
    reduce_scatter x1, waiting for transfers between devices, per_device(): lax.psum_scatter(grads[0], 'dp', scatter_dimension=1, tiled=True)  105 us
    psum x4, blocking collectives, row_totals(): return lax.psum((sum_one, sum_two, sum_three, sum_four), 'tensor')  75.9 us
  transfers between devices with their start and end apart: 33, of which 20 were waited for; matrix products, arithmetic and copies ran while one was open for 39% of the time, Pallas kernels for 0%

commit v1 on v0

v1 whole, which is shorter than its diff:
```python
import functools

import jax
import jax.numpy as jnp
from jax import lax
from jax.experimental import pallas as pl
from jax.experimental.pallas import tpu as pltpu
from jax.sharding import Mesh
from jax.sharding import PartitionSpec as P

D = 1536
HEAD_DIM = 64
NORM_EPS = 1e-06
GELU_SLOPE = (2.0 / 3.141592653589793) ** 0.5
GELU_CUBE = 0.044715
LOW = jnp.bfloat16
FULL = jnp.float32
SWAP = [(0, 1), (1, 0)]
BLOCK = 256
LANES = 128


def place():
    return lax.axis_index("core"), lax.axis_index("zp"), lax.axis_index("zl")


def ordered(first_here, here, there, axis):
    return jnp.where(
        first_here,
        jnp.concatenate([here, there], axis),
        jnp.concatenate([there, here], axis),
    )


def nn(left, right):
    return lax.dot_general(left, right, (((1,), (0,)), ((), ())), preferred_element_type=FULL)


def nt(left, right):
    return lax.dot_general(left, right, (((1,), (1,)), ((), ())), preferred_element_type=FULL)


def tn(left, right):
    return lax.dot_general(left, right, (((0,), (0,)), ((), ())), preferred_element_type=FULL)


def rows_call(kernel, name, image, rows, tiles, tables, outs, flops):
    split = image // BLOCK

    def by_rows(i, _):
        return (i, 0)

    def by_modality(i, _):
        return (jnp.minimum(i // split, 1), 0, 0)

    core = lax.axis_index("core").astype(jnp.int32).reshape(1)
    moved = sum(t.size * t.dtype.itemsize for t in (*tiles, *tables))
    moved += sum(rows * width * jnp.dtype(kind).itemsize for width, kind in outs)
    return pl.pallas_call(
        kernel,
        grid_spec=pltpu.PrefetchScalarGridSpec(
            num_scalar_prefetch=1,
            grid=(pl.cdiv(rows, BLOCK),),
            in_specs=[pl.BlockSpec((BLOCK, t.shape[1]), by_rows) for t in tiles]
            + [pl.BlockSpec((1, *t.shape[1:]), by_modality) for t in tables],
            out_specs=[pl.BlockSpec((BLOCK, width), by_rows) for width, _ in outs],
        ),
        out_shape=[jax.ShapeDtypeStruct((rows, width), kind) for width, kind in outs],
        compiler_params=pltpu.CompilerParams(
            dimension_semantics=("arbitrary",), vmem_limit_bytes=56 << 20
        ),
        cost_estimate=pl.CostEstimate(flops=flops, transcendentals=0, bytes_accessed=moved),
        name=name,
    )(core, *tiles, *tables)


def halves(core_ref, width):
    mine = pl.multiple_of(core_ref[0] * width, width)
    theirs = pl.multiple_of((1 - core_ref[0]) * width, width)
    return pl.ds(mine, width), pl.ds(theirs, width)


def qkv_kernel(core_ref, x_ref, mod_ref, w_ref, bias_ref, in_ref, out_ref, stat_ref):
    values = x_ref[...].astype(FULL)
    average = jnp.mean(values, axis=1, keepdims=True)
    centred = values - average
    factor = lax.rsqrt(jnp.mean(centred * centred, axis=1, keepdims=True) + NORM_EPS)
    shifted = (centred * factor * (1.0 + mod_ref[0, 1:2, :]) + mod_ref[0, 0:1, :]).astype(LOW)
    in_ref[...] = shifted
    out_ref[...] = (nn(shifted, w_ref[0]) + bias_ref[0]).astype(LOW)
    lane = lax.broadcasted_iota(jnp.int32, stat_ref.shape, 1)
    stat_ref[...] = jnp.where(lane == 0, average, factor)


def spread_kernel(core_ref, a_ref, w_ref, mine_ref, theirs_ref):
    mine, theirs = halves(core_ref, w_ref.shape[1] // 2)
    theirs_ref[...] = nt(a_ref[...], w_ref[0, theirs, :]).astype(LOW)
    mine_ref[...] = nt(a_ref[...], w_ref[0, mine, :]).astype(LOW)


def gather_kernel(core_ref, a_ref, w_ref, out_ref):
    out_ref[...] = nn(a_ref[...], w_ref[0]).astype(LOW)


def mlp_kernel(core_ref, a_ref, up_ref, bias_ref, down_ref, pre_ref, act_ref, mine_ref, theirs_ref):
    mine, theirs = halves(core_ref, down_ref.shape[1] // 2)
    pre = nn(a_ref[...], up_ref[0]) + bias_ref[0]
    pre_ref[...] = pre
    bent = jnp.tanh(GELU_SLOPE * (pre + GELU_CUBE * (pre * pre * pre)))
    act = (0.5 * pre * (1.0 + bent)).astype(LOW)
    act_ref[...] = act
    theirs_ref[...] = nt(act, down_ref[0, theirs, :]).astype(LOW)
    mine_ref[...] = nt(act, down_ref[0, mine, :]).astype(LOW)


def mlp_back_kernel(core_ref, g_ref, pre_ref, up_ref, down_ref, grad_ref, mine_ref, theirs_ref):
    mine, theirs = halves(core_ref, up_ref.shape[1] // 2)
    grad_act = nn(g_ref[...], down_ref[0])
    pre = pre_ref[...]
    square = pre * pre
    bent = jnp.tanh(GELU_SLOPE * pre * (1.0 + GELU_CUBE * square))
    slope = 0.5 * (1.0 + bent) + (0.5 * GELU_SLOPE) * pre * (1.0 - bent * bent) * (
        1.0 + (3.0 * GELU_CUBE) * square
    )
    grad = (grad_act * slope).astype(LOW)
    grad_ref[...] = grad
    theirs_ref[...] = nt(grad, up_ref[0, theirs, :]).astype(LOW)
    mine_ref[...] = nt(grad, up_ref[0, mine, :]).astype(LOW)


def weight_kernel(image, left_zero, left_one, right_zero, right_one, out_ref):
    for m, rows in enumerate((slice(0, image), slice(image, None))):
        out_ref[m] = (
            tn(left_zero[rows, :], right_zero[rows, :]) + tn(left_one[rows, :], right_one[rows, :])
        ).astype(LOW)


def weight_grad(image, lefts, rights):
    rows, width = lefts[0].shape
    across = rights[0].shape[1]
    return pl.pallas_call(
        functools.partial(weight_kernel, image),
        grid=(width // BLOCK,),
        in_specs=[pl.BlockSpec((rows, BLOCK), lambda i: (0, i))] * 2
        + [pl.BlockSpec((rows, across), lambda i: (0, 0))] * 2,
        out_specs=pl.BlockSpec((2, BLOCK, across), lambda i: (0, i, 0)),
        out_shape=jax.ShapeDtypeStruct((2, width, across), LOW),
        compiler_params=pltpu.CompilerParams(
            dimension_semantics=("arbitrary",), vmem_limit_bytes=56 << 20
        ),
        cost_estimate=pl.CostEstimate(
            flops=4 * rows * width * across,
            transcendentals=0,
            bytes_accessed=4 * (rows * (width + across) + width * across),
        ),
        name="weight_grad",
    )(*lefts, *rights)


def head_mask(values, head):
    lane = lax.broadcasted_iota(jnp.int32, values.shape, 1)
    return jnp.where((lane // HEAD_DIM) == head, values, jnp.zeros_like(values))


def live_rows(values, length):
    row = lax.broadcasted_iota(jnp.int32, values.shape, 0) + pl.program_id(1) * BLOCK
    return jnp.where(row < length, values, jnp.zeros_like(values))


def attend_kernel(length, q_ref, k_ref, v_ref, out_ref, log_ref, turned):
    @pl.when(pl.program_id(1) == 0)
    def _():
        turned[...] = v_ref[...].T

    queries = live_rows(q_ref[...], length) * jnp.asarray(HEAD_DIM**-0.5, LOW)
    keys_in = k_ref[...]
    cut = length // 8 * 8
    scores = [nt(keys_in, head_mask(queries, head)) for head in range(2)]
    found = []
    for head in range(2):
        row = lax.broadcasted_iota(jnp.int32, (keys_in.shape[0] - cut, BLOCK), 0)
        body = scores[head][:cut]
        tail = jnp.where(row < length - cut, scores[head][cut:], -1e30)
        highest = jnp.maximum(
            jnp.max(body, axis=0, keepdims=True), jnp.max(tail, axis=0, keepdims=True)
        )
        body, tail = jnp.exp(body - highest), jnp.exp(tail - highest)
        total = jnp.sum(body, axis=0, keepdims=True) + jnp.sum(tail, axis=0, keepdims=True)
        scale = 1.0 / total
        soft = jnp.concatenate([(body * scale).astype(LOW), (tail * scale).astype(LOW)], 0)
        found.append(nn(turned[head * HEAD_DIM : (head + 1) * HEAD_DIM, :], soft))
        log_ref[0, head : head + 1, :] = highest + jnp.log(total)
    out_ref[...] = jnp.concatenate(found, 0).T.astype(LOW)


def attend(joint, length):
    rows, width = joint.shape[0], joint.shape[1] // 3
    pairs, blocks = width // LANES, pl.cdiv(rows, BLOCK)
    area = 2 * pairs * rows * rows
    return pl.pallas_call(
        functools.partial(attend_kernel, length),
        out_shape=(
            jax.ShapeDtypeStruct((rows, width), LOW),
            jax.ShapeDtypeStruct((pairs, 8, blocks * BLOCK), FULL),
        ),
        grid=(pairs, blocks),
        in_specs=[
            pl.BlockSpec((BLOCK, LANES), lambda p, i: (i, p)),
            pl.BlockSpec((rows, LANES), lambda p, i: (0, pairs + p)),
            pl.BlockSpec((rows, LANES), lambda p, i: (0, 2 * pairs + p)),
        ],
        out_specs=(
            pl.BlockSpec((BLOCK, LANES), lambda p, i: (i, p)),
            pl.BlockSpec((1, 8, BLOCK), lambda p, i: (p, 0, i)),
        ),
        scratch_shapes=[pltpu.VMEM((LANES, rows), LOW)],
        compiler_params=pltpu.CompilerParams(
            dimension_semantics=("arbitrary", "arbitrary"), vmem_limit_bytes=56 << 20
        ),
        cost_estimate=pl.CostEstimate(
            flops=area * HEAD_DIM * 40, transcendentals=area, bytes_accessed=joint.size * 3
        ),
        name="attend",
    )(joint, joint, joint)


def attend_back_kernel(
    length, q_ref, k_ref, v_ref, up_ref, log_ref, out_ref, turned, key_sum, value_sum
):
    pair, block = pl.program_id(0), pl.program_id(1)
    pairs = pl.num_programs(0)

    @pl.when(block == 0)
    def _():
        turned[...] = k_ref[...].T
        key_sum[...] = jnp.zeros_like(key_sum)
        value_sum[...] = jnp.zeros_like(value_sum)

    rows = k_ref.shape[0]
    cut = length // 8 * 8
    scale = HEAD_DIM**-0.5
    queries = live_rows(q_ref[...], length) * jnp.asarray(scale, LOW)
    upstream = live_rows(up_ref[...], length)
    keys_in, values_in = k_ref[...], v_ref[...]
    masked = [head_mask(queries, head) for head in range(2)]
    above = [head_mask(upstream, head) for head in range(2)]
    scores, grad_soft = [], []
    for head in range(2):
        scores.append(nt(keys_in, masked[head]))
        grad_soft.append(nt(values_in, above[head]))
    row = lax.broadcasted_iota(jnp.int32, (rows - cut, BLOCK), 0)
    found = []
    for head in range(2):
        raised = jnp.exp(scores[head] - log_ref[0, head : head + 1, :])
        tail = jnp.where(row < length - cut, raised[cut:], 0.0)
        soft = jnp.concatenate([raised[:cut], tail], 0)
        inner = jnp.sum(soft * grad_soft[head], axis=0, keepdims=True)
        grad_scores = (soft * (grad_soft[head] - inner)).astype(LOW)
        value_sum[...] += nn(soft.astype(LOW), above[head])
        key_sum[...] += nn(grad_scores, masked[head])
        found.append(nn(turned[head * HEAD_DIM : (head + 1) * HEAD_DIM, :], grad_scores))
    first = pl.multiple_of(pair * LANES, LANES)
    start = pl.multiple_of(block * BLOCK, BLOCK)
    grad_queries = (jnp.concatenate(found, 0).T * scale).astype(LOW)
    last = pl.num_programs(1) - 1
    left = rows - rows // BLOCK * BLOCK

    @pl.when((block < last) if left else (block <= last))
    def _():
        out_ref[pl.ds(start, BLOCK), pl.ds(first, LANES)] = grad_queries

    if left:

        @pl.when(block == last)
        def _():
            out_ref[rows - left :, pl.ds(first, LANES)] = grad_queries[:left]

    @pl.when(block == last)
    def _():
        second = pl.multiple_of((pairs + pair) * LANES, LANES)
        third = pl.multiple_of((2 * pairs + pair) * LANES, LANES)
        out_ref[:, pl.ds(second, LANES)] = key_sum[...].astype(LOW)
        out_ref[:, pl.ds(third, LANES)] = value_sum[...].astype(LOW)


def attend_back(joint, log_total, upstream, length):
    rows, width = joint.shape[0], joint.shape[1] // 3
    pairs, blocks = width // LANES, pl.cdiv(rows, BLOCK)
    area = 2 * pairs * rows * rows
    return pl.pallas_call(
        functools.partial(attend_back_kernel, length),
        out_shape=jax.ShapeDtypeStruct((rows, 3 * width), LOW),
        grid=(pairs, blocks),
        in_specs=[
            pl.BlockSpec((BLOCK, LANES), lambda p, i: (i, p)),
            pl.BlockSpec((rows, LANES), lambda p, i: (0, pairs + p)),
            pl.BlockSpec((rows, LANES), lambda p, i: (0, 2 * pairs + p)),
            pl.BlockSpec((BLOCK, LANES), lambda p, i: (i, p)),
            pl.BlockSpec((1, 8, BLOCK), lambda p, i: (p, 0, i)),
        ],
        out_specs=pl.BlockSpec((rows, 3 * width), lambda p, i: (0, 0)),
        scratch_shapes=[
            pltpu.VMEM((LANES, rows), LOW),
            pltpu.VMEM((rows, LANES), FULL),
            pltpu.VMEM((rows, LANES), FULL),
        ],
        compiler_params=pltpu.CompilerParams(
            dimension_semantics=("arbitrary", "arbitrary"), vmem_limit_bytes=56 << 20
        ),
        cost_estimate=pl.CostEstimate(
            flops=area * HEAD_DIM * 60, transcendentals=area, bytes_accessed=joint.size * 6
        ),
        name="attend_back",
    )(joint, joint, joint, upstream, log_total)


def rehome(values):
    return lax.ppermute(values, ("core", "zp"), [(0, 0), (1, 2), (2, 1), (3, 3)])


def group_gather(own):
    core, _, near = place()
    half = ordered(near == 0, own, lax.ppermute(own, "zl", SWAP), own.ndim - 1)
    return ordered(core == 0, half, lax.ppermute(half, "core", SWAP), own.ndim - 1)


def group_reduce(mine, theirs):
    _, _, near = place()
    half = mine.astype(FULL) + lax.ppermute(theirs, "core", SWAP).astype(FULL)
    width = half.shape[1] // 2
    send = lax.dynamic_slice_in_dim(half, (1 - near) * width, width, 1).astype(LOW)
    own = lax.dynamic_slice_in_dim(half, near * width, width, 1)
    return own + lax.ppermute(send, "zl", SWAP).astype(FULL)


def group_sum(values):
    values = values + lax.ppermute(values, "core", SWAP)
    return values + lax.ppermute(values, "zl", SWAP)


def row_means(first, second):
    packed = group_sum(jnp.stack([first.sum(axis=1), (first * second).sum(axis=1)])) / D
    return packed[0][:, None], packed[1][:, None]


def weight_gather(shard):
    core, pair, _ = place()
    other = lax.ppermute(shard, "zp", SWAP)
    stays = core == pair
    keep = jnp.where(stays, shard, other)
    sibling = lax.ppermute(jnp.where(stays, other, shard), "core", SWAP)
    return lax.all_gather(ordered(core == 0, keep, sibling, 1), "yx", axis=1, tiled=True)


def weight_reduce(grad):
    core, pair, _ = place()
    block = lax.psum_scatter(grad, "yx", scatter_dimension=1, tiled=True)
    rows = block.shape[1] // 2
    keep = lax.dynamic_slice_in_dim(block, core * rows, rows, 1)
    sibling = lax.ppermute(
        lax.dynamic_slice_in_dim(block, (1 - core) * rows, rows, 1), "core", SWAP
    )
    stays = core == pair
    own = jnp.where(stays, keep, sibling)
    other = lax.ppermute(jnp.where(stays, sibling, keep), "zp", SWAP)
    return own.astype(FULL) + other.astype(FULL)


def steps(count):
    return [1 << bit for bit in range(count.bit_length() - 1)]


def dp_gather(values, planes):
    core = lax.axis_index("core")
    plane = lax.axis_index("yx")
    values = ordered(core == 0, values, lax.ppermute(values, "core", SWAP), 0)
    for bit in steps(planes):
        other = lax.ppermute(values, "yx", [(i, i ^ bit) for i in range(planes)])
        values = ordered((plane & bit) == 0, values, other, 0)
    return values


def dp_scatter_sum(values, planes):
    core = lax.axis_index("core")
    plane = lax.axis_index("yx")

    def halve(values, high, axis, perm):
        rows = values.shape[0] // 2
        send = lax.dynamic_slice_in_dim(values, (1 - high) * rows, rows, 0)
        keep = lax.dynamic_slice_in_dim(values, high * rows, rows, 0)
        return keep + lax.ppermute(send, axis, perm)

    for bit in reversed(steps(planes)):
        high = jnp.where((plane & bit) == 0, 0, 1)
        values = halve(values, high, "yx", [(i, i ^ bit) for i in range(planes)])
    return halve(values, core, "core", SWAP)


def mm(equation, left, right):
    return jnp.einsum(equation, left, right, preferred_element_type=FULL)


def per_device(
    planes,
    image_in,
    text_in,
    condition,
    image_cot,
    text_cot,
    qkv_weight,
    qv_bias,
    proj_weight,
    proj_bias,
    up_weight,
    up_bias,
    down_weight,
    down_bias,
    mod_weight,
    mod_bias,
):
    micro, image, quarter = image_in.shape
    text = text_in.shape[1]
    length = image + text
    rows = -(-length // 16) * 16
    core, pair, _ = place()
    stays = core == pair
    is_image = lax.broadcasted_iota(jnp.int32, (rows, 1), 0) < image

    def own_quarter(bias):
        bias = bias.astype(FULL)
        return jnp.where(stays, bias, rehome(bias))

    def join(image_part, text_part):
        return jnp.concatenate(
            [image_part, text_part, jnp.zeros((rows - length, image_part.shape[1]), LOW)], 0
        )

    def by_row(table):
        return jnp.where(is_image, table[0][None], table[1][None])

    def sums(values):
        values = values.astype(FULL)
        return jnp.stack([values[:image].sum(axis=0), values[image:].sum(axis=0)])

    inputs = [rehome(join(image_in[s], text_in[s])) for s in range(micro)]
    cotangents = [rehome(join(image_cot[s], text_cot[s])) for s in range(micro)]

    row_count = mod_weight.shape[1]
    cond_all = dp_gather(condition, planes)
    silu_all = jax.nn.silu(cond_all.astype(FULL)).astype(LOW)
    dp_index = lax.axis_index(("yx", "core"))
    silu_rows = lax.dynamic_slice_in_dim(silu_all, dp_index * row_count, row_count, 1)
    mod_terms = mm("bi,sicj->bscj", silu_rows, mod_weight)
    modulation = rehome(dp_scatter_sum(mod_terms, planes) + mod_bias.astype(FULL)[None])
    wide_modulation = group_gather(modulation[:, :, :2])

    qkv = weight_gather(qkv_weight.reshape(2, row_count, -1))
    proj = weight_gather(proj_weight.transpose(0, 2, 1))
    up = weight_gather(up_weight)
    down = weight_gather(down_weight.transpose(0, 2, 1))
    qv_own, proj_own, up_own, down_own = [
        own_quarter(bias) for bias in (qv_bias, proj_bias, up_bias, down_bias)
    ]
    qkv_own = jnp.concatenate([qv_own[:, 0], jnp.zeros_like(qv_own[:, 0]), qv_own[:, 1]], 1)
    call = functools.partial(rows_call, image=image, rows=rows)
    dense = 2 * rows * D

    outputs, input_grads, grad_mods, factors, bias_sums = [], [], [], [], []
    for s in range(micro):
        mod = modulation[s]
        wide = group_gather(inputs[s])
        residual = inputs[s].astype(FULL)
        attn_in, joint, stats = call(
            qkv_kernel,
            "qkv",
            tiles=[wide],
            tables=[wide_modulation[s], qkv, qkv_own[:, None]],
            outs=[(D, LOW), (3 * quarter, LOW), (LANES, FULL)],
            flops=dense * 3 * quarter,
        )
        normed_one = (residual - stats[:, 0:1]) * stats[:, 1:2]
        attended, log_total = attend(joint, length)
        reduced = group_reduce(
            *call(
                spread_kernel,
                "proj",
                tiles=[attended],
                tables=[proj],
                outs=[(D // 2, LOW), (D // 2, LOW)],
                flops=dense * quarter,
            )
        )
        branch_one = reduced + by_row(proj_own)
        middle = residual + by_row(mod[:, 2]) * branch_one
        average, square = row_means(middle, middle)
        factor_two = lax.rsqrt(square - average * average + NORM_EPS)
        normed_two = (middle - average) * factor_two
        mlp_in = group_gather(
            (normed_two * (1.0 + by_row(mod[:, 4])) + by_row(mod[:, 3])).astype(LOW)
        )
        hidden = up.shape[2]
        pre_act, activated, mine, theirs = call(
            mlp_kernel,
            "mlp",
            tiles=[mlp_in],
            tables=[up, up_own[:, None], down],
            outs=[(hidden, FULL), (hidden, LOW), (D // 2, LOW), (D // 2, LOW)],
            flops=dense * hidden * 2,
        )
        branch_two = group_reduce(mine, theirs) + by_row(down_own)
        outputs.append(rehome((middle + by_row(mod[:, 5]) * branch_two).astype(LOW)))

        upstream = cotangents[s].astype(FULL)
        grad_gate_two = sums(upstream * branch_two)
        grad_two = (by_row(mod[:, 5]) * upstream).astype(LOW)
        grad_two_full = group_gather(grad_two)
        grad_pre, mine, theirs = call(
            mlp_back_kernel,
            "mlp_back",
            tiles=[grad_two_full, pre_act],
            tables=[up, down],
            outs=[(hidden, LOW), (D // 2, LOW), (D // 2, LOW)],
            flops=dense * hidden * 2,
        )
        grad_mlp = group_reduce(mine, theirs)
        grad_shift_two = sums(grad_mlp)
        grad_scale_two = sums(grad_mlp * normed_two)
        scaled = grad_mlp * (1.0 + by_row(mod[:, 4]))
        grad_mean, cross_mean = row_means(scaled, normed_two)
        grad_middle = upstream + factor_two * (scaled - grad_mean - normed_two * cross_mean)
        grad_gate_one = sums(grad_middle * branch_one)
        grad_one = (by_row(mod[:, 2]) * grad_middle).astype(LOW)
        grad_one_full = group_gather(grad_one)
        (grad_attended,) = call(
            gather_kernel,
            "proj_back",
            tiles=[grad_one_full],
            tables=[proj],
            outs=[(quarter, LOW)],
            flops=dense * quarter,
        )
        grad_joint = attend_back(joint, log_total, grad_attended, length)
        grad_attn = group_reduce(
            *call(
                spread_kernel,
                "qkv_back",
                tiles=[grad_joint],
                tables=[qkv],
                outs=[(D // 2, LOW), (D // 2, LOW)],
                flops=dense * 3 * quarter,
            )
        )
        grad_shift_one = sums(grad_attn)
        grad_scale_one = sums(grad_attn * normed_one)
        scaled = grad_attn * (1.0 + by_row(mod[:, 1]))
        grad_mean, cross_mean = row_means(scaled, normed_one)
        grad_in = grad_middle + stats[:, 1:2] * (scaled - grad_mean - normed_one * cross_mean)
        input_grads.append(
            jnp.where(stays, grad_in, rehome(grad_in.astype(LOW)).astype(FULL))
        )
        grad_mods.append(
            jnp.stack(
                [
                    grad_shift_one,
                    grad_scale_one,
                    grad_gate_one,
                    grad_shift_two,
                    grad_scale_two,
                    grad_gate_two,
                ],
                1,
            )
        )
        grad_qkv_sums = sums(grad_joint)
        bias_sums.append(
            (
                jnp.stack([grad_qkv_sums[:, :quarter], grad_qkv_sums[:, 2 * quarter :]], 1),
                sums(grad_one),
                sums(grad_pre),
                sums(grad_two),
            )
        )
        factors.append(
            (
                (attn_in, grad_joint),
                (grad_one_full, attended),
                (mlp_in, grad_pre),
                (grad_two_full, activated),
            )
        )

    def reduced_grad(index):
        lefts, rights = zip(*[factor[index] for factor in factors])
        return weight_reduce(weight_grad(image, lefts, rights))

    down_grad = reduced_grad(3).transpose(0, 2, 1)
    up_grad = reduced_grad(2)
    proj_grad = reduced_grad(1).transpose(0, 2, 1)
    qkv_grad = reduced_grad(0).reshape(qkv_weight.shape)

    image_out = jnp.stack([output[:image] for output in outputs])
    text_out = jnp.stack([output[image:length] for output in outputs])
    image_grad = jnp.stack([grad[:image] for grad in input_grads])
    text_grad = jnp.stack([grad[image:length] for grad in input_grads])

    grad_mod_low = rehome(jnp.stack(grad_mods).astype(LOW))
    grad_mod_all = dp_gather(grad_mod_low, planes)
    mod_bias_grad = jnp.sum(grad_mod_all.astype(FULL), axis=0)
    mod_weight_grad = mm("bi,bscj->sicj", silu_rows, grad_mod_all)
    silu_grad_rows = mm("bscj,sicj->bi", grad_mod_all, mod_weight)
    silu_grad = lax.all_to_all(
        silu_grad_rows, ("yx", "core"), split_axis=0, concat_axis=1, tiled=True
    )
    silu_grad = silu_grad + lax.ppermute(silu_grad, "zp", SWAP)
    silu_grad = silu_grad + lax.ppermute(silu_grad, "zl", SWAP)
    condition_grad = jax.vjp(jax.nn.silu, condition.astype(FULL))[1](silu_grad)[0]

    totals = [sum(parts[1:], parts[0]) for parts in zip(*bias_sums)]
    packed = jnp.concatenate([total.reshape(-1) for total in totals])
    packed = packed + lax.ppermute(packed, "zp", SWAP)
    for bit in steps(planes):
        packed = packed + lax.ppermute(packed, "yx", [(i, i ^ bit) for i in range(planes)])
    packed = jnp.where(stays, packed, lax.ppermute(packed, "core", SWAP))
    bias_grads, start = [], 0
    for total in totals:
        bias_grads.append(packed[start : start + total.size].reshape(total.shape))
        start += total.size
    return (
        image_out,
        text_out,
        image_grad,
        text_grad,
        condition_grad,
        qkv_grad,
        bias_grads[0],
        proj_grad,
        bias_grads[1],
        up_grad,
        bias_grads[2],
        down_grad,
        bias_grads[3],
        mod_weight_grad,
        mod_bias_grad,
    )


def solution(mesh):
    planes = mesh.shape["dp"] // 2
    split = Mesh(mesh.devices.reshape(planes, 2, 2, 2), ("yx", "core", "zp", "zl"))
    dp, tensor = ("yx", "core"), ("zp", "zl")
    tokens = P(dp, None, tensor)
    placed = (
        tokens,
        tokens,
        P(dp, None),
        tokens,
        tokens,
        P(None, dp, None, tensor),
        P(None, None, tensor),
        P(None, tensor, dp),
        P(None, tensor),
        P(None, dp, tensor),
        P(None, tensor),
        P(None, tensor, dp),
        P(None, tensor),
        P(None, dp, None, tensor),
        P(None, None, tensor),
    )
    return jax.shard_map(
        functools.partial(per_device, planes),
        mesh=split,
        in_specs=placed,
        out_specs=(tokens,) * 4 + (P(dp, None),) + placed[5:],
        check_vma=False,
    )
```

time: 2250 us -> 1310 us (0.58)
  waiting for transfers between devices: 1040 us -> 542 us
  matrix products: 432 us -> 4.36 us
  Pallas kernels: 0 us -> 334 us
  blocking collectives: 268 us -> 0 us
  local copies, waits for them, and re-layouts: 308 us -> 84.1 us
  starting transfers between devices: 6.87 us -> 168 us
    ppermute x0 -> x91, waiting for transfers between devices: none -> 539 us  [the longest x4 144 us: weight_gather(): other = lax.ppermute(shard, 'zp', SWAP)]
    unnamed x50 -> x8, waiting for transfers between devices: 499 us -> 0.13 us
    dot_general x135 -> x3, matrix products: 432 us -> 4.36 us  [mm(): return jnp.einsum(equation, left, right, preferred_element_type=FULL)]
    pallas_call x0 -> x20, Pallas kernels: none -> 334 us  [the longest x12 165 us: rows_call(): pl.pallas_call(kernel, grid_spec=pltpu.PrefetchScalarGridSpec(num_scalar_...]
    all_gather x12 -> x4, waiting for transfers between devices: 314 us -> 0.01 us  [weight_gather(): lax.all_gather(ordered(core == 0, keep, sibling, 1), 'yx', axis=1, tiled=...]
    reduce_scatter x2 -> x4, waiting for transfers between devices: 229 us -> 0.01 us  [weight_reduce(): block = lax.psum_scatter(grad, 'yx', scatter_dimension=1, tiled=True)]
    all_gather x10 -> x0, blocking collectives: 165 us -> none  [the longest x8 144 us: feature_gather(): lax.all_gather(second_part, 'tensor', axis=1, tiled=True)]
    ppermute x0 -> x91, starting transfers between devices: none -> 164 us  [the longest x14 43.3 us: rehome(): lax.ppermute(values, ('core', 'zp'), [(0, 0), (1, 2), (2, 1), (3, 3)])]
  transfers between devices with their start and end apart: 33 -> 100, of which waited for: 20 -> 47; matrix products, arithmetic and copies ran while one was open for 39% -> 16% of each run, Pallas kernels for 0% -> 26%
where the time goes in v1:
time: 1310 us; the launch traced here: 1300 us
  waiting for transfers between devices  542 us (41%)
  Pallas kernels  334 us (25%)
  starting transfers between devices  168 us (13%)
  other arithmetic  147 us (11%)
  local copies, waits for them, and re-layouts  84.1 us (6%)
  between operations  16.6 us (1%)
    pallas_call x12, Pallas kernels, rows_call(): pl.pallas_call(kernel, grid_spec=pltpu.PrefetchScalarGridSpec(num_scalar_...  165 us
    ppermute x4, waiting for transfers between devices, weight_gather(): other = lax.ppermute(shard, 'zp', SWAP)  144 us
    ppermute x4, waiting for transfers between devices, weight_reduce(): other = lax.ppermute(jnp.where(stays, sibling, keep), 'zp', SWAP)  141 us
    ppermute x8, waiting for transfers between devices, group_reduce(): return own + lax.ppermute(send, 'zl', SWAP).astype(FULL)  89.7 us
    ppermute x9, waiting for transfers between devices, group_gather(): half = ordered(near == 0, own, lax.ppermute(own, 'zl', SWAP), own.ndim - 1)  89.4 us
    pallas_call x2, Pallas kernels, attend_back(): pl.pallas_call(functools.partial(attend_back_kernel, length), out_shape=j...  62.4 us
    pallas_call x4, Pallas kernels, weight_grad(): pl.pallas_call(functools.partial(weight_kernel, image), grid=(width // BL...  61.7 us
    select_n x26, other arithmetic, ordered(): jnp.where(first_here, jnp.concatenate([here, there], axis), jnp.concatena...  52.9 us
  transfers between devices with their start and end apart: 100, of which 47 were waited for; matrix products, arithmetic and copies ran while one was open for 16% of the time, Pallas kernels for 26%

profile of v1, /device:TPU:0, one launch (start us, length us, event | category | flops | bytes accessed | tf_op | source)
XLA Modules:
  0.0 1296.7 jit_solution(17569782209667646912)
XLA Ops:
  12.7 38.7 %collective-permute-done.12 = bf16[2,192,1152]{2,1,0:T(8,128)(2,1)} collective-permute-done((bf16[2,192,1152]{2,1,0:T(8,128)(2,1)S(1)}, bf16[2,192,1152]{2,1,0:T(8,128)(2,1)}, u32[]{:S(2)}, u32[]{:S(2)}) %collective-permute-start.12) | collective-permute-done | bytes 884768 | tf_op jit(solution)/shard_map/ppermute | solution.py:348
  77.7 52.7 %collective-permute-done.27 = bf16[2,192,1536]{2,1,0:T(8,128)(2,1)S(1)} collective-permute-done((bf16[2,192,1536]{2,1,0:T(8,128)(2,1)S(1)}, bf16[2,192,1536]{2,1,0:T(8,128)(2,1)S(1)}, u32[]{:S(2)}, u32[]{:S(2)}) %collective-permute-start.27) | collective-permute-done | bytes 1179680 | tf_op jit(solution)/shard_map/ppermute | solution.py:348
  176.8 35.7 %collective-permute-done.24 = bf16[2,192,1536]{2,1,0:T(8,128)(2,1)} collective-permute-done((bf16[2,192,1536]{2,1,0:T(8,128)(2,1)}, bf16[2,192,1536]{2,1,0:T(8,128)(2,1)}, u32[]{:S(2)}, u32[]{:S(2)}) %collective-permute-start.24) | collective-permute-done | bytes 1179680 | tf_op jit(solution)/shard_map/ppermute | solution.py:348
  214.3 23.6 %collective-permute-start.25 = (bf16[2,192,1536]{2,1,0:T(8,128)(2,1)S(1)}, bf16[2,192,1536]{2,1,0:T(8,128)(2,1)S(1)}, u32[]{:S(2)}, u32[]{:S(2)}) collective-permute-start(bf16[2,192,1536]{2,1,0:T(8,128)(2,1)S(1)} %get-tuple-element.202), channel_id=1, source_target_pairs={{0,4},{4,0},{1,5},{5,1},{2,6},{6,2},{3,7},{7,3},{8,12},{12,8},{9,1... | collective-permute-start | bytes 3538952 | tf_op jit(solution)/shard_map/ppermute | solution.py:351
  289.1 22.6 %attend.2 = (bf16[1184,384]{1,0:T(8,128)(2,1)}, f32[3,8,1280]{2,1,0:T(8,128)}) custom-call(bf16[1184,1152]{1,0:T(8,128)(2,1)} %get-tuple-element.47.q_ref.k_ref.v_ref, bf16[1184,1152]{1,0:T(8,128)(2,1)} %get-tuple-element.47.q_ref.k_ref.v_ref, bf16[1184,1152]{1,0:T(8,128)(2,1)} %get-tuple-element.47.q_ref.k_ref.v_ref), custom_call_target="tpu_custom_call" | custom-call | flops 21532508160 | bytes 4091904 | tf_op jit(solution)/shard_map/attend/pallas_call | solution.py:200
  331.3 22.5 %attend.3 = (bf16[1184,384]{1,0:T(8,128)(2,1)}, f32[3,8,1280]{2,1,0:T(8,128)}) custom-call(bf16[1184,1152]{1,0:T(8,128)(2,1)} %get-tuple-element.53.q_ref.k_ref.v_ref, bf16[1184,1152]{1,0:T(8,128)(2,1)} %get-tuple-element.53.q_ref.k_ref.v_ref, bf16[1184,1152]{1,0:T(8,128)(2,1)} %get-tuple-element.53.q_ref.k_ref.v_ref), custom_call_target="tpu_custom_call" | custom-call | flops 21532508160 | bytes 4091904 | tf_op jit(solution)/shard_map/attend/pallas_call | solution.py:200
  407.1 20.2 %collective-permute-done.37 = bf16[1184,384]{1,0:T(8,128)(2,1)} collective-permute-done((bf16[1184,384]{1,0:T(8,128)(2,1)}, bf16[1184,384]{1,0:T(8,128)(2,1)}, u32[]{:S(2)}, u32[]{:S(2)}) %collective-permute-start.37) | collective-permute-done | bytes 909344 | tf_op jit(solution)/shard_map/ppermute | solution.py:333
  482.8 17.5 %collective-permute-done.40 = bf16[1184,384]{1,0:T(8,128)(2,1)S(1)} collective-permute-done((bf16[1184,384]{1,0:T(8,128)(2,1)S(1)}, bf16[1184,384]{1,0:T(8,128)(2,1)S(1)}, u32[]{:S(2)}, u32[]{:S(2)}) %collective-permute-start.40) | collective-permute-done | bytes 909344 | tf_op jit(solution)/shard_map/ppermute | solution.py:323
  522.0 22.7 %mlp.2 = (f32[1184,1536]{1,0:T(8,128)}, bf16[1184,1536]{1,0:T(8,128)(2,1)}, bf16[1184,768]{1,0:T(8,128)(2,1)}, bf16[1184,768]{1,0:T(8,128)(2,1)}) custom-call(s32[1]{0:T(128)} %bitcast.5.core_ref, bf16[1184,1536]{1,0:T(8,128)(2,1)} %maximum_select_fusion.1.a_ref.left_zero, bf16[2,1536,1536]{2,1,0:T(8,128)(2,1)} %all-gather.9.cloned.1.call-done.up_ref, ...), custom_call_target="tpu_custom_call" | custom-call | flops 11173625856 | bytes 37072896 | tf_op jit(solution)/shard_map/mlp/pallas_call | solution.py:59
  550.3 22.0 %mlp_back.2 = (bf16[1184,1536]{1,0:T(8,128)(2,1)}, bf16[1184,768]{1,0:T(8,128)(2,1)}, bf16[1184,768]{1,0:T(8,128)(2,1)}) custom-call(s32[1]{0:T(128)} %bitcast.5.core_ref, bf16[1184,1536]{1,0:T(8,128)(2,1)} %maximum_select_fusion.4.g_ref.left_zero, f32[1184,1536]{1,0:T(8,128)} %get-tuple-element.59.pre_ref, ...), custom_call_target="tpu_custom_call" | custom-call | flops 11173625856 | bytes 37060608 | tf_op jit(solution)/shard_map/mlp_back/pallas_call | solution.py:59
  577.7 22.6 %mlp.3 = (f32[1184,1536]{1,0:T(8,128)}, bf16[1184,1536]{1,0:T(8,128)(2,1)}, bf16[1184,768]{1,0:T(8,128)(2,1)}, bf16[1184,768]{1,0:T(8,128)(2,1)}) custom-call(s32[1]{0:T(128)} %bitcast.5.core_ref, bf16[1184,1536]{1,0:T(8,128)(2,1)} %maximum_select_fusion.3.a_ref.left_one, bf16[2,1536,1536]{2,1,0:T(8,128)(2,1)} %all-gather.9.cloned.1.call-done.up_ref, ...), custom_call_target="tpu_custom_call" | custom-call | flops 11173625856 | bytes 37072896 | tf_op jit(solution)/shard_map/mlp/pallas_call | solution.py:59
  629.1 22.4 %mlp_back.3 = (bf16[1184,1536]{1,0:T(8,128)(2,1)}, bf16[1184,768]{1,0:T(8,128)(2,1)}, bf16[1184,768]{1,0:T(8,128)(2,1)}) custom-call(s32[1]{0:T(128)} %bitcast.5.core_ref, bf16[1184,1536]{1,0:T(8,128)(2,1)} %maximum_select_fusion.6.g_ref.left_one, f32[1184,1536]{1,0:T(8,128)} %get-tuple-element.66.pre_ref, ...), custom_call_target="tpu_custom_call" | custom-call | flops 11173625856 | bytes 37060608 | tf_op jit(solution)/shard_map/mlp_back/pallas_call | solution.py:59
  658.6 18.3 %weight_grad.6 = bf16[2,1536,1536]{2,1,0:T(8,128)(2,1)} custom-call(bf16[1184,1536]{1,0:T(8,128)(2,1)} %maximum_select_fusion.1.a_ref.left_zero, bf16[1184,1536]{1,0:T(8,128)(2,1)} %maximum_select_fusion.3.a_ref.left_one, bf16[1184,1536]{1,0:T(8,128)(2,1)} %get-tuple-element.75.right_zero, bf16[1184,1536]{1,0:T(8,128)(2,1)} %get-tuple-element.76.right_one), custom_call_target="tpu_custom_call" | custom-call | flops 11173625856 | bytes 23986176 | tf_op jit(solution)/shard_map/weight_grad/pallas_call | solution.py:141
  696.2 31.2 %attend_back.2.a_ref.right_zero = bf16[1184,1152]{1,0:T(8,128)(2,1)} custom-call(bf16[1184,1152]{1,0:T(8,128)(2,1)} %get-tuple-element.47.q_ref.k_ref.v_ref, bf16[1184,1152]{1,0:T(8,128)(2,1)} %get-tuple-element.47.q_ref.k_ref.v_ref, bf16[1184,1152]{1,0:T(8,128)(2,1)} %get-tuple-element.47.q_ref.k_ref.v_ref, bf16[1184,384]{1,0:T(8,128)(2,1)} %proj_back.2.up_ref, ...), custom_call_target="tpu_custom_call" | custom-call | flops 32298762240 | bytes 8183808 | tf_op jit(solution)/shard_map/attend_back/pallas_call | solution.py:290
  745.5 17.5 %collective-permute-done.63 = bf16[1184,384]{1,0:T(8,128)(2,1)S(1)} collective-permute-done((bf16[1184,384]{1,0:T(8,128)(2,1)S(1)}, bf16[1184,384]{1,0:T(8,128)(2,1)S(1)}, u32[]{:S(2)}, u32[]{:S(2)}) %collective-permute-start.63) | collective-permute-done | bytes 909344 | tf_op jit(solution)/shard_map/ppermute | solution.py:333
  764.7 17.4 %collective-permute-done.55 = bf16[1184,384]{1,0:T(8,128)(2,1)S(1)} collective-permute-done((bf16[1184,384]{1,0:T(8,128)(2,1)S(1)}, bf16[1184,384]{1,0:T(8,128)(2,1)S(1)}, u32[]{:S(2)}, u32[]{:S(2)}) %collective-permute-start.55) | collective-permute-done | bytes 909344 | tf_op jit(solution)/shard_map/ppermute | solution.py:333
  791.0 20.7 %collective-permute-done.65 = f32[2,1184]{1,0:T(2,128)S(1)} collective-permute-done((f32[2,1184]{1,0:T(2,128)S(1)}, f32[2,1184]{1,0:T(2,128)S(1)}, u32[]{:S(2)}, u32[]{:S(2)}) %collective-permute-start.65) | collective-permute-done | bytes 9504 | tf_op jit(solution)/shard_map/ppermute | solution.py:338
  817.4 21.2 %collective-permute-done.66 = bf16[1184,384]{1,0:T(8,128)(2,1)S(1)} collective-permute-done((bf16[1184,384]{1,0:T(8,128)(2,1)S(1)}, bf16[1184,384]{1,0:T(8,128)(2,1)S(1)}, u32[]{:S(2)}, u32[]{:S(2)}) %collective-permute-start.66) | collective-permute-done | bytes 909344 | tf_op jit(solution)/shard_map/ppermute | solution.py:323
  854.5 18.5 %weight_grad.7 = bf16[2,1536,1536]{2,1,0:T(8,128)(2,1)} custom-call(bf16[1184,1536]{1,0:T(8,128)(2,1)} %maximum_select_fusion.4.g_ref.left_zero, bf16[1184,1536]{1,0:T(8,128)(2,1)} %maximum_select_fusion.6.g_ref.left_one, bf16[1184,1536]{1,0:T(8,128)(2,1)} %get-tuple-element.77.right_zero, bf16[1184,1536]{1,0:T(8,128)(2,1)} %get-tuple-element.78.right_one), custom_call_target="tpu_custom_call" | custom-call | flops 11173625856 | bytes 23986176 | tf_op jit(solution)/shard_map/weight_grad/pallas_call | solution.py:141
  931.8 31.2 %attend_back.3.a_ref.right_one = bf16[1184,1152]{1,0:T(8,128)(2,1)} custom-call(bf16[1184,1152]{1,0:T(8,128)(2,1)} %get-tuple-element.53.q_ref.k_ref.v_ref, bf16[1184,1152]{1,0:T(8,128)(2,1)} %get-tuple-element.53.q_ref.k_ref.v_ref, bf16[1184,1152]{1,0:T(8,128)(2,1)} %get-tuple-element.53.q_ref.k_ref.v_ref, bf16[1184,384]{1,0:T(8,128)(2,1)} %proj_back.3.up_ref, ...), custom_call_target="tpu_custom_call" | custom-call | flops 32298762240 | bytes 8183808 | tf_op jit(solution)/shard_map/attend_back/pallas_call | solution.py:290
  1020.4 17.9 %collective-permute-done.69 = bf16[1184,384]{1,0:T(8,128)(2,1)} collective-permute-done((bf16[1184,384]{1,0:T(8,128)(2,1)}, bf16[1184,384]{1,0:T(8,128)(2,1)}, u32[]{:S(2)}, u32[]{:S(2)}) %collective-permute-start.69) | collective-permute-done | bytes 909344 | tf_op jit(solution)/shard_map/ppermute | solution.py:333
  1141.8 58.5 %collective-permute-done.86 = bf16[2,192,384]{2,1,0:T(8,128)(2,1)S(1)} collective-permute-done((bf16[2,192,384]{2,1,0:T(8,128)(2,1)S(1)}, bf16[2,192,384]{2,1,0:T(8,128)(2,1)S(1)}, u32[]{:S(2)}, u32[]{:S(2)}) %collective-permute-start.86) | collective-permute-done | bytes 294944 | tf_op jit(solution)/shard_map/ppermute | solution.py:365
  1202.1 42.5 %collective-permute-done.88 = bf16[2,192,1536]{2,1,0:T(8,128)(2,1)S(1)} collective-permute-done((bf16[2,192,1536]{2,1,0:T(8,128)(2,1)S(1)}, bf16[2,192,1536]{2,1,0:T(8,128)(2,1)S(1)}, u32[]{:S(2)}, u32[]{:S(2)}) %collective-permute-start.88) | collective-permute-done | bytes 1179680 | tf_op jit(solution)/shard_map/ppermute | solution.py:365
  1246.4 23.4 %collective-permute-done.90 = bf16[2,192,1536]{2,1,0:T(8,128)(2,1)S(1)} collective-permute-done((bf16[2,192,1536]{2,1,0:T(8,128)(2,1)S(1)}, bf16[2,192,1536]{2,1,0:T(8,128)(2,1)S(1)}, u32[]{:S(2)}, u32[]{:S(2)}) %collective-permute-start.90) | collective-permute-done | bytes 1179680 | tf_op jit(solution)/shard_map/ppermute | solution.py:365
  (676 shorter events, 638.5 us)
Async XLA Ops:
  7.2 268.8 %all-gather.5.cloned.1.call-start = ((), (), s32[]{:S(2)}) async-start(), calls=%async_computation.5 | async-start | bytes 8847360 | tf_op jit(solution)/shard_map/all_gather | solution.py:352
  58.2 253.5 %all-gather.7.cloned.1.call-start = ((), (), s32[]{:S(2)}) async-start(), calls=%async_computation.6 | async-start | bytes 2949120 | tf_op jit(solution)/shard_map/all_gather | solution.py:352
  77.5 444.4 %all-gather.11.cloned.1.call-start = ((), (), s32[]{:S(2)}) async-start(), calls=%async_computation.8 | async-start | bytes 11796480 | tf_op jit(solution)/shard_map/all_gather | solution.py:352
  135.2 386.8 %all-gather.9.cloned.1.call-start = ((), (), s32[]{:S(2)}) async-start(), calls=%async_computation.7 | async-start | bytes 11796480 | tf_op jit(solution)/shard_map/all_gather | solution.py:352
  138.7 73.9 %collective-permute-start.24 = (bf16[2,192,1536]{2,1,0:T(8,128)(2,1)}, bf16[2,192,1536]{2,1,0:T(8,128)(2,1)}, u32[]{:S(2)}, u32[]{:S(2)}) collective-permute-start(bf16[2,192,1536]{2,1,0:T(8,128)(2,1)} %param.24), channel_id=1, source_target_pairs={{0,2},{2,0},{1,3},{3,1},{4,6},{6,4},{5,7},{7,5},{8,10},{10,8},{9,1... | collective-permute-start | bytes 3538952 | tf_op jit(solution)/shard_map/ppermute | solution.py:348
  172.8 65.1 %collective-permute-start.8 = (bf16[1184,384]{1,0:T(8,128)(2,1)}, bf16[1184,384]{1,0:T(8,128)(2,1)S(1)}, u32[]{:S(2)}, u32[]{:S(2)}) collective-permute-start(bf16[1184,384]{1,0:T(8,128)(2,1)} %collective-permute-done), channel_id=1, source_target_pairs={{0,1},{1,0},{2,3},{3,2},{4,5},{5,4},{6,7},{7,6},{8,9},{9,8},{10,11... | collective-permute-start | bytes 2727944 | tf_op jit(solution)/shard_map/ppermute | solution.py:323
  174.7 79.7 %collective-permute-start.10 = (f32[2,2,2,384]{3,2,1,0:T(2,128)S(1)}, f32[2,2,2,384]{3,2,1,0:T(2,128)S(1)}, u32[]{:S(2)}, u32[]{:S(2)}) collective-permute-start(f32[2,2,2,384]{3,2,1,0:T(2,128)S(1)} %slice.554), channel_id=1, source_target_pairs={{0,1},{1,0},{2,3},{3,2},{4,5},{5,4},{6,7},{7,6},{8,9},{9,8},{10,11... | collective-permute-start | bytes 36872 | tf_op jit(solution)/shard_map/ppermute | solution.py:323
  175.7 78.8 %collective-permute-start.34 = (bf16[1184,384]{1,0:T(8,128)(2,1)S(1)}, bf16[1184,384]{1,0:T(8,128)(2,1)S(1)}, u32[]{:S(2)}, u32[]{:S(2)}) collective-permute-start(bf16[1184,384]{1,0:T(8,128)(2,1)S(1)} %collective-permute-done.33), channel_id=1, source_target_pairs={{0,1},{1,0},{2,3},{3,2},{4,5},{5,4},{6,7},{7,6},{8,9},{9,8},{10,11... | collective-permute-start | bytes 2727944 | tf_op jit(solution)/shard_map/ppermute | solution.py:323
  264.6 857.1 %reduce-scatter.9.cloned.1.call-start = ((), (), s32[]{:S(2)}) async-start(), calls=%async_computation.11 | async-start | bytes 11796480 | tf_op jit(solution)/shard_map/reduce_scatter | solution.py:357
  383.0 55.1 %collective-permute-start.45 = (bf16[1184,384]{1,0:T(8,128)(2,1)}, bf16[1184,384]{1,0:T(8,128)(2,1)}, u32[]{:S(2)}, u32[]{:S(2)}) collective-permute-start(bf16[1184,384]{1,0:T(8,128)(2,1)} %concatenate.223), channel_id=1, source_target_pairs={{0,0},{2,4},{4,2},{6,6},{1,1},{3,5},{5,3},{7,7},{8,8},{10,12},{12,... | collective-permute-start | bytes 2727944 | tf_op jit(solution)/shard_map/ppermute | solution.py:318
  461.5 57.9 %collective-permute-start.23 = (bf16[1184,768]{1,0:T(8,128)(2,1)S(1)}, bf16[1184,768]{1,0:T(8,128)(2,1)S(1)}, u32[]{:S(2)}, u32[]{:S(2)}) collective-permute-start(bf16[1184,768]{1,0:T(8,128)(2,1)S(1)} %maximum_select_fusion.11), channel_id=1, source_target_pairs={{0,4},{4,0},{1,5},{5,1},{2,6},{6,2},{3,7},{7,3},{8,12},{12,8},{9,1... | collective-permute-start | bytes 5455880 | tf_op jit(solution)/shard_map/ppermute | solution.py:324
  482.4 62.8 %collective-permute-start.47 = (bf16[1184,768]{1,0:T(8,128)(2,1)}, bf16[1184,768]{1,0:T(8,128)(2,1)}, u32[]{:S(2)}, u32[]{:S(2)}) collective-permute-start(bf16[1184,768]{1,0:T(8,128)(2,1)} %maximum_select_fusion.14), channel_id=1, source_target_pairs={{0,4},{4,0},{1,5},{5,1},{2,6},{6,2},{3,7},{7,3},{8,12},{12,8},{9,1... | collective-permute-start | bytes 5455880 | tf_op jit(solution)/shard_map/ppermute | solution.py:324
  501.9 70.5 %collective-permute-start.41 = (bf16[1184,768]{1,0:T(8,128)(2,1)}, bf16[1184,768]{1,0:T(8,128)(2,1)}, u32[]{:S(2)}, u32[]{:S(2)}) collective-permute-start(bf16[1184,768]{1,0:T(8,128)(2,1)} %maximum_select_fusion.13), channel_id=1, source_target_pairs={{0,4},{4,0},{1,5},{5,1},{2,6},{6,2},{3,7},{7,3},{8,12},{12,8},{9,1... | collective-permute-start | bytes 5455880 | tf_op jit(solution)/shard_map/ppermute | solution.py:324
  519.4 81.9 %collective-permute-start.61 = (bf16[1184,768]{1,0:T(8,128)(2,1)}, bf16[1184,768]{1,0:T(8,128)(2,1)}, u32[]{:S(2)}, u32[]{:S(2)}) collective-permute-start(bf16[1184,768]{1,0:T(8,128)(2,1)} %maximum_select_fusion.16), channel_id=1, source_target_pairs={{0,4},{4,0},{1,5},{5,1},{2,6},{6,2},{3,7},{7,3},{8,12},{12,8},{9,1... | collective-permute-start | bytes 5455880 | tf_op jit(solution)/shard_map/ppermute | solution.py:324
  544.6 62.0 %collective-permute-start.29 = (bf16[1184,768]{1,0:T(8,128)(2,1)}, bf16[1184,768]{1,0:T(8,128)(2,1)S(1)}, u32[]{:S(2)}, u32[]{:S(2)}) collective-permute-start(bf16[1184,768]{1,0:T(8,128)(2,1)} %get-tuple-element.52), channel_id=1, source_target_pairs={{0,4},{4,0},{1,5},{5,1},{2,6},{6,2},{3,7},{7,3},{8,12},{12,8},{9,1... | collective-permute-start | bytes 5455880 | tf_op jit(solution)/shard_map/ppermute | solution.py:329
  676.8 448.4 %reduce-scatter.7.cloned.1.call-start = ((), (), s32[]{:S(2)}) async-start(), calls=%async_computation.10 | async-start | bytes 2949120 | tf_op jit(solution)/shard_map/reduce_scatter | solution.py:357
  681.6 57.9 %collective-permute-start.62 = (bf16[1184,768]{1,0:T(8,128)(2,1)}, bf16[1184,768]{1,0:T(8,128)(2,1)S(1)}, u32[]{:S(2)}, u32[]{:S(2)}) collective-permute-start(bf16[1184,768]{1,0:T(8,128)(2,1)} %get-tuple-element.68), channel_id=1, source_target_pairs={{0,4},{4,0},{1,5},{5,1},{2,6},{6,2},{3,7},{7,3},{8,12},{12,8},{9,1... | collective-permute-start | bytes 5455880 | tf_op jit(solution)/shard_map/ppermute | solution.py:329
  854.4 273.1 %reduce-scatter.11.cloned.1.call-start = ((), (), s32[]{:S(2)}) async-start(), calls=%async_computation.12 | async-start | bytes 11796480 | tf_op jit(solution)/shard_map/reduce_scatter | solution.py:357
  873.0 261.5 %reduce-scatter.5.cloned.1.call-start = ((), (), s32[]{:S(2)}) async-start(), calls=%async_computation.9 | async-start | bytes 8847360 | tf_op jit(solution)/shard_map/reduce_scatter | solution.py:357
  1132.9 67.4 %collective-permute-start.86 = (bf16[2,192,384]{2,1,0:T(8,128)(2,1)S(1)}, bf16[2,192,384]{2,1,0:T(8,128)(2,1)S(1)}, u32[]{:S(2)}, u32[]{:S(2)}) collective-permute-start(bf16[2,192,384]{2,1,0:T(8,128)(2,1)S(1)} %broadcast_select_fusion.10), channel_id=1, source_target_pairs={{0,2},{2,0},{1,3},{3,1},{4,6},{6,4},{5,7},{7,5},{8,10},{10,8},{9,1... | collective-permute-start | bytes 884744 | tf_op jit(solution)/shard_map/ppermute | solution.py:365
  1135.7 65.5 %collective-permute-start.79 = (bf16[2,192,1152]{2,1,0:T(8,128)(2,1)S(1)}, bf16[2,192,1152]{2,1,0:T(8,128)(2,1)S(1)}, u32[]{:S(2)}, u32[]{:S(2)}) collective-permute-start(bf16[2,192,1152]{2,1,0:T(8,128)(2,1)S(1)} %constant_dynamic-slice_fusion.3), channel_id=1, source_target_pairs={{0,4},{4,0},{1,5},{5,1},{2,6},{6,2},{3,7},{7,3},{8,12},{12,8},{9,1... | collective-permute-start | bytes 2654216 | tf_op jit(solution)/shard_map/ppermute | solution.py:360
  1138.4 106.2 %collective-permute-start.88 = (bf16[2,192,1536]{2,1,0:T(8,128)(2,1)S(1)}, bf16[2,192,1536]{2,1,0:T(8,128)(2,1)S(1)}, u32[]{:S(2)}, u32[]{:S(2)}) collective-permute-start(bf16[2,192,1536]{2,1,0:T(8,128)(2,1)S(1)} %broadcast_select_fusion.1), channel_id=1, source_target_pairs={{0,2},{2,0},{1,3},{3,1},{4,6},{6,4},{5,7},{7,5},{8,10},{10,8},{9,1... | collective-permute-start | bytes 3538952 | tf_op jit(solution)/shard_map/ppermute | solution.py:365
  1140.7 129.2 %collective-permute-start.90 = (bf16[2,192,1536]{2,1,0:T(8,128)(2,1)S(1)}, bf16[2,192,1536]{2,1,0:T(8,128)(2,1)S(1)}, u32[]{:S(2)}, u32[]{:S(2)}) collective-permute-start(bf16[2,192,1536]{2,1,0:T(8,128)(2,1)S(1)} %broadcast_select_fusion), channel_id=1, source_target_pairs={{0,2},{2,0},{1,3},{3,1},{4,6},{6,4},{5,7},{7,5},{8,10},{10,8},{9,1... | collective-permute-start | bytes 3538952 | tf_op jit(solution)/shard_map/ppermute | solution.py:365
  1201.5 86.5 %collective-permute-start.80 = (bf16[2,192,1152]{2,1,0:T(8,128)(2,1)S(1)}, bf16[2,192,1152]{2,1,0:T(8,128)(2,1)S(1)}, u32[]{:S(2)}, u32[]{:S(2)}) collective-permute-start(bf16[2,192,1152]{2,1,0:T(8,128)(2,1)S(1)} %broadcast_select_fusion.6), channel_id=1, source_target_pairs={{0,2},{2,0},{1,3},{3,1},{4,6},{6,4},{5,7},{7,5},{8,10},{10,8},{9,1... | collective-permute-start | bytes 2654216 | tf_op jit(solution)/shard_map/ppermute | solution.py:365
  (164 other events, 2544.8 us)
Sparse Core Ops, SparseCore 0:
  58.3 77.8 all-gather.4
  138.6 40.6 all-gather.6
  181.7 95.2 all-gather.10
  279.3 96.3 all-gather.8
  677.0 93.1 reduce-scatter.8
  854.5 35.3 reduce-scatter.6
  893.1 95.0 reduce-scatter.10
  991.2 76.7 reduce-scatter.4

commit v2 on v1

v2 whole, which is shorter than its diff:
```python
import functools

import jax
import jax.numpy as jnp
from jax import lax
from jax.experimental import pallas as pl
from jax.experimental.pallas import tpu as pltpu
from jax.sharding import Mesh
from jax.sharding import PartitionSpec as P

D = 1536
HEAD_DIM = 64
NORM_EPS = 1e-06
GELU_SLOPE = (2.0 / 3.141592653589793) ** 0.5
GELU_CUBE = 0.044715
LOW = jnp.bfloat16
FULL = jnp.float32
SWAP = [(0, 1), (1, 0)]
BLOCK = 256
ROWS = 512
LANES = 128


def place():
    return lax.axis_index("core"), lax.axis_index("zp"), lax.axis_index("zl")


def ordered(first_here, here, there, axis):
    return jnp.where(
        first_here,
        jnp.concatenate([here, there], axis),
        jnp.concatenate([there, here], axis),
    )


def nn(left, right):
    return lax.dot_general(left, right, (((1,), (0,)), ((), ())), preferred_element_type=FULL)


def nt(left, right):
    return lax.dot_general(left, right, (((1,), (1,)), ((), ())), preferred_element_type=FULL)


def tn(left, right):
    return lax.dot_general(left, right, (((0,), (0,)), ((), ())), preferred_element_type=FULL)


def rows_kernel(body, split, text, count, here_ref, *refs):
    def view(size):
        def cut(ref):
            return ref.at[pl.ds(0, size), :]

        tiles, tables, outs = refs[: count[0]], refs[count[0] : count[1]], refs[count[1] :]
        return (*map(cut, tiles), *tables, *map(cut, outs))

    @pl.when(pl.program_id(0) < split)
    def _():
        body(here_ref, *view(ROWS))

    @pl.when(pl.program_id(0) == split)
    def _():
        body(here_ref, *view(text))


def rows_call(kernel, name, image, rows, tiles, tables, outs, flops, scratch=()):
    split = image // ROWS

    def by_rows(i, _):
        return (i, 0)

    def by_modality(i, _):
        return (jnp.minimum(i // split, 1), 0, 0)

    here = jnp.stack([lax.axis_index("core"), lax.axis_index("zl")]).astype(jnp.int32)
    moved = sum(t.size * t.dtype.itemsize for t in (*tiles, *tables))
    moved += sum(rows * width * jnp.dtype(kind).itemsize for width, kind in outs)
    count = (len(tiles), len(tiles) + len(tables))
    return pl.pallas_call(
        functools.partial(rows_kernel, kernel, split, rows - image, count),
        grid_spec=pltpu.PrefetchScalarGridSpec(
            num_scalar_prefetch=1,
            grid=(split + 1,),
            in_specs=[pl.BlockSpec((ROWS, t.shape[1]), by_rows) for t in tiles]
            + [pl.BlockSpec((1, *t.shape[1:]), by_modality) for t in tables],
            out_specs=[pl.BlockSpec((ROWS, width), by_rows) for width, _ in outs],
            scratch_shapes=[pltpu.VMEM((ROWS, width), kind) for width, kind in scratch],
        ),
        out_shape=[jax.ShapeDtypeStruct((rows, width), kind) for width, kind in outs],
        compiler_params=pltpu.CompilerParams(
            dimension_semantics=("arbitrary",), vmem_limit_bytes=56 << 20
        ),
        cost_estimate=pl.CostEstimate(flops=flops, transcendentals=0, bytes_accessed=moved),
        name=name,
    )(here, *tiles, *tables)


def halves(here_ref, width):
    mine = pl.multiple_of(here_ref[0] * width, width)
    theirs = pl.multiple_of((1 - here_ref[0]) * width, width)
    return pl.ds(mine, width), pl.ds(theirs, width)


def gather_pieces(here_ref, pieces, full_ref):
    width = pieces[0].shape[1]
    for k, piece in enumerate(pieces):
        core = here_ref[0] if k < 2 else 1 - here_ref[0]
        near = here_ref[1] if k % 2 == 0 else 1 - here_ref[1]
        start = pl.multiple_of((2 * core + near) * width, LANES)
        full_ref[:, pl.ds(start, width)] = piece[...]


def spread(here_ref, value, read, outs):
    for refs, half in zip((outs[2:], outs[:2]), halves(here_ref, read.shape[1] // 2)[::-1]):
        found = nt(value, read[0, half, :]).astype(LOW)
        width = found.shape[1] // 2
        first, second = found[:, :width], found[:, width:]
        low = here_ref[1] == 0
        refs[0][...] = jnp.where(low, first, second)
        refs[1][...] = jnp.where(low, second, first)


def join_kernel(length, image_ref, text_ref, *outs):
    image, rows = image_ref.shape[1], outs[0].shape[0]
    start = length // 8 * 8
    for sample, out_ref in enumerate(outs):
        out_ref[:image, :] = image_ref[sample]
        out_ref[start:rows, :] = jnp.zeros((rows - start, out_ref.shape[1]), LOW)
        out_ref[image:length, :] = text_ref[sample]


def join(rows, image_part, text_part):
    samples, image, width = image_part.shape
    return pl.pallas_call(
        functools.partial(join_kernel, image + text_part.shape[1]),
        out_shape=[jax.ShapeDtypeStruct((rows, width), LOW)] * samples,
        compiler_params=pltpu.CompilerParams(vmem_limit_bytes=32 << 20),
        cost_estimate=pl.CostEstimate(
            flops=0, transcendentals=0, bytes_accessed=4 * samples * rows * width
        ),
        name="join",
    )(image_part, text_part)


def qkv_kernel(here_ref, *refs):
    pieces, (mod_ref, w_ref, bias_ref, in_ref, out_ref, stat_ref, full) = refs[:4], refs[4:]
    gather_pieces(here_ref, pieces, full)
    values = full[...].astype(FULL)
    average = jnp.mean(values, axis=1, keepdims=True)
    centred = values - average
    factor = lax.rsqrt(jnp.mean(centred * centred, axis=1, keepdims=True) + NORM_EPS)
    shifted = (centred * factor * (1.0 + mod_ref[0, 1:2, :]) + mod_ref[0, 0:1, :]).astype(LOW)
    in_ref[...] = shifted
    out_ref[...] = (nn(shifted, w_ref[0]) + bias_ref[0]).astype(LOW)
    lane = lax.broadcasted_iota(jnp.int32, stat_ref.shape, 1)
    stat_ref[...] = jnp.where(lane == 0, average, factor)


def spread_kernel(here_ref, a_ref, w_ref, *outs):
    spread(here_ref, a_ref[...], w_ref, outs)


def proj_back_kernel(here_ref, *refs):
    pieces, (w_ref, in_ref, out_ref) = refs[:4], refs[4:]
    gather_pieces(here_ref, pieces, in_ref)
    out_ref[...] = nn(in_ref[...], w_ref[0]).astype(LOW)


def gather_kernel(here_ref, *refs):
    gather_pieces(here_ref, refs[:4], refs[4])


def up_kernel(here_ref, *refs):
    pieces, (up_ref, bias_ref, in_ref, pre_ref, act_ref) = refs[:4], refs[4:]
    gather_pieces(here_ref, pieces, in_ref)
    values = in_ref[...]
    width = up_ref.shape[2] // 3
    for j in range(3):
        part = slice(j * width, (j + 1) * width)
        pre = nn(values, up_ref[0, :, part]) + bias_ref[0, :, part]
        pre_ref[:, part] = pre
        bent = jnp.tanh(GELU_SLOPE * (pre + GELU_CUBE * (pre * pre * pre)))
        act_ref[:, part] = (0.5 * pre * (1.0 + bent)).astype(LOW)


def mlp_back_kernel(here_ref, g_ref, pre_ref, up_ref, down_ref, grad_ref, *outs):
    values = g_ref[...]
    width = down_ref.shape[2] // 3
    for j in range(3):
        part = slice(j * width, (j + 1) * width)
        grad_act = nn(values, down_ref[0, :, part])
        pre = pre_ref[:, part]
        square = pre * pre
        bent = jnp.tanh(GELU_SLOPE * pre * (1.0 + GELU_CUBE * square))
        slope = 0.5 * (1.0 + bent) + (0.5 * GELU_SLOPE) * pre * (1.0 - bent * bent) * (
            1.0 + (3.0 * GELU_CUBE) * square
        )
        grad_ref[:, part] = (grad_act * slope).astype(LOW)
    spread(here_ref, grad_ref[...], up_ref, outs)


def weight_kernel(image, left_zero, left_one, right_zero, right_one, out_ref, sum_ref):
    for m, rows in enumerate((slice(0, image), slice(image, None))):
        out_ref[m] = (
            tn(left_zero[rows, :], right_zero[rows, :]) + tn(left_one[rows, :], right_one[rows, :])
        ).astype(LOW)

        @pl.when(pl.program_id(0) == 0)
        def _():
            sum_ref[m] = sum(
                jnp.sum(right[rows, :].astype(FULL), axis=0, keepdims=True)
                for right in (right_zero, right_one)
            )


def weight_grad(image, lefts, rights):
    rows, width = lefts[0].shape
    across = rights[0].shape[1]
    return pl.pallas_call(
        functools.partial(weight_kernel, image),
        grid=(width // BLOCK,),
        in_specs=[pl.BlockSpec((rows, BLOCK), lambda i: (0, i))] * 2
        + [pl.BlockSpec((rows, across), lambda i: (0, 0))] * 2,
        out_specs=[
            pl.BlockSpec((2, BLOCK, across), lambda i: (0, i, 0)),
            pl.BlockSpec((2, 1, across), lambda i: (0, 0, 0)),
        ],
        out_shape=[
            jax.ShapeDtypeStruct((2, width, across), LOW),
            jax.ShapeDtypeStruct((2, 1, across), FULL),
        ],
        compiler_params=pltpu.CompilerParams(
            dimension_semantics=("arbitrary",), vmem_limit_bytes=56 << 20
        ),
        cost_estimate=pl.CostEstimate(
            flops=4 * rows * width * across,
            transcendentals=0,
            bytes_accessed=4 * (rows * (width + across) + width * across),
        ),
        name="weight_grad",
    )(*lefts, *rights)


def head_mask(values, head):
    lane = lax.broadcasted_iota(jnp.int32, values.shape, 1)
    return jnp.where((lane // HEAD_DIM) == head, values, jnp.zeros_like(values))


def live_rows(values, length):
    row = lax.broadcasted_iota(jnp.int32, values.shape, 0) + pl.program_id(1) * BLOCK
    return jnp.where(row < length, values, jnp.zeros_like(values))


def attend_kernel(length, q_ref, k_ref, v_ref, out_ref, log_ref, turned):
    @pl.when(pl.program_id(1) == 0)
    def _():
        turned[...] = v_ref[...].T

    queries = live_rows(q_ref[...], length) * jnp.asarray(HEAD_DIM**-0.5, LOW)
    keys_in = k_ref[...]
    cut = length // 8 * 8
    scores = [nt(keys_in, head_mask(queries, head)) for head in range(2)]
    found = []
    for head in range(2):
        row = lax.broadcasted_iota(jnp.int32, (keys_in.shape[0] - cut, BLOCK), 0)
        body = scores[head][:cut]
        tail = jnp.where(row < length - cut, scores[head][cut:], -1e30)
        highest = jnp.maximum(
            jnp.max(body, axis=0, keepdims=True), jnp.max(tail, axis=0, keepdims=True)
        )
        body, tail = jnp.exp(body - highest), jnp.exp(tail - highest)
        total = jnp.sum(body, axis=0, keepdims=True) + jnp.sum(tail, axis=0, keepdims=True)
        scale = 1.0 / total
        soft = jnp.concatenate([(body * scale).astype(LOW), (tail * scale).astype(LOW)], 0)
        found.append(nn(turned[head * HEAD_DIM : (head + 1) * HEAD_DIM, :], soft))
        log_ref[0, head : head + 1, :] = highest + jnp.log(total)
    out_ref[...] = jnp.concatenate(found, 0).T.astype(LOW)


def attend(joint, length):
    rows, width = joint.shape[0], joint.shape[1] // 3
    pairs, blocks = width // LANES, pl.cdiv(rows, BLOCK)
    area = 2 * pairs * rows * rows
    return pl.pallas_call(
        functools.partial(attend_kernel, length),
        out_shape=(
            jax.ShapeDtypeStruct((rows, width), LOW),
            jax.ShapeDtypeStruct((pairs, 8, blocks * BLOCK), FULL),
        ),
        grid=(pairs, blocks),
        in_specs=[
            pl.BlockSpec((BLOCK, LANES), lambda p, i: (i, p)),
            pl.BlockSpec((rows, LANES), lambda p, i: (0, pairs + p)),
            pl.BlockSpec((rows, LANES), lambda p, i: (0, 2 * pairs + p)),
        ],
        out_specs=(
            pl.BlockSpec((BLOCK, LANES), lambda p, i: (i, p)),
            pl.BlockSpec((1, 8, BLOCK), lambda p, i: (p, 0, i)),
        ),
        scratch_shapes=[pltpu.VMEM((LANES, rows), LOW)],
        compiler_params=pltpu.CompilerParams(
            dimension_semantics=("arbitrary", "arbitrary"), vmem_limit_bytes=56 << 20
        ),
        cost_estimate=pl.CostEstimate(
            flops=area * HEAD_DIM * 40, transcendentals=area, bytes_accessed=joint.size * 3
        ),
        name="attend",
    )(joint, joint, joint)


def attend_back_kernel(
    length, q_ref, k_ref, v_ref, up_ref, log_ref, out_ref, turned, key_sum, value_sum
):
    pair, block = pl.program_id(0), pl.program_id(1)
    pairs = pl.num_programs(0)

    @pl.when(block == 0)
    def _():
        turned[...] = k_ref[...].T
        key_sum[...] = jnp.zeros_like(key_sum)
        value_sum[...] = jnp.zeros_like(value_sum)

    rows = k_ref.shape[0]
    cut = length // 8 * 8
    scale = HEAD_DIM**-0.5
    queries = live_rows(q_ref[...], length) * jnp.asarray(scale, LOW)
    upstream = live_rows(up_ref[...], length)
    keys_in, values_in = k_ref[...], v_ref[...]
    masked = [head_mask(queries, head) for head in range(2)]
    above = [head_mask(upstream, head) for head in range(2)]
    scores, grad_soft = [], []
    for head in range(2):
        scores.append(nt(keys_in, masked[head]))
        grad_soft.append(nt(values_in, above[head]))
    row = lax.broadcasted_iota(jnp.int32, (rows - cut, BLOCK), 0)
    found = []
    for head in range(2):
        raised = jnp.exp(scores[head] - log_ref[0, head : head + 1, :])
        tail = jnp.where(row < length - cut, raised[cut:], 0.0)
        soft = jnp.concatenate([raised[:cut], tail], 0)
        inner = jnp.sum(soft * grad_soft[head], axis=0, keepdims=True)
        grad_scores = (soft * (grad_soft[head] - inner)).astype(LOW)
        value_sum[...] += nn(soft.astype(LOW), above[head])
        key_sum[...] += nn(grad_scores, masked[head])
        found.append(nn(turned[head * HEAD_DIM : (head + 1) * HEAD_DIM, :], grad_scores))
    first = pl.multiple_of(pair * LANES, LANES)
    start = pl.multiple_of(block * BLOCK, BLOCK)
    grad_queries = (jnp.concatenate(found, 0).T * scale).astype(LOW)
    last = pl.num_programs(1) - 1
    left = rows - rows // BLOCK * BLOCK

    @pl.when((block < last) if left else (block <= last))
    def _():
        out_ref[pl.ds(start, BLOCK), pl.ds(first, LANES)] = grad_queries

    if left:

        @pl.when(block == last)
        def _():
            out_ref[rows - left :, pl.ds(first, LANES)] = grad_queries[:left]

    @pl.when(block == last)
    def _():
        second = pl.multiple_of((pairs + pair) * LANES, LANES)
        third = pl.multiple_of((2 * pairs + pair) * LANES, LANES)
        out_ref[:, pl.ds(second, LANES)] = key_sum[...].astype(LOW)
        out_ref[:, pl.ds(third, LANES)] = value_sum[...].astype(LOW)


def attend_back(joint, log_total, upstream, length):
    rows, width = joint.shape[0], joint.shape[1] // 3
    pairs, blocks = width // LANES, pl.cdiv(rows, BLOCK)
    area = 2 * pairs * rows * rows
    return pl.pallas_call(
        functools.partial(attend_back_kernel, length),
        out_shape=jax.ShapeDtypeStruct((rows, 3 * width), LOW),
        grid=(pairs, blocks),
        in_specs=[
            pl.BlockSpec((BLOCK, LANES), lambda p, i: (i, p)),
            pl.BlockSpec((rows, LANES), lambda p, i: (0, pairs + p)),
            pl.BlockSpec((rows, LANES), lambda p, i: (0, 2 * pairs + p)),
            pl.BlockSpec((BLOCK, LANES), lambda p, i: (i, p)),
            pl.BlockSpec((1, 8, BLOCK), lambda p, i: (p, 0, i)),
        ],
        out_specs=pl.BlockSpec((rows, 3 * width), lambda p, i: (0, 0)),
        scratch_shapes=[
            pltpu.VMEM((LANES, rows), LOW),
            pltpu.VMEM((rows, LANES), FULL),
            pltpu.VMEM((rows, LANES), FULL),
        ],
        compiler_params=pltpu.CompilerParams(
            dimension_semantics=("arbitrary", "arbitrary"), vmem_limit_bytes=56 << 20
        ),
        cost_estimate=pl.CostEstimate(
            flops=area * HEAD_DIM * 60, transcendentals=area, bytes_accessed=joint.size * 6
        ),
        name="attend_back",
    )(joint, joint, joint, upstream, log_total)


def settle_kernel(planes, plane_ref, *refs):
    *parts, out_ref = refs
    plane = plane_ref[0]
    blocks = planes // 2
    rows = parts[0].shape[0] // blocks
    for turned in range(2):
        high = (plane // blocks + turned) % 2
        start = pl.multiple_of(high * (blocks * rows), 8)
        out_ref[0, pl.ds(start, blocks * rows), :] = parts[turned][...]
        low = (plane + turned) % 2
        for b in range(blocks):
            turn = int(f"{b:0{max(blocks.bit_length() - 1, 1)}b}"[::-1], 2)
            start = pl.multiple_of((2 * turn + low) * rows, 8)
            out_ref[1, pl.ds(start, rows), :] = parts[2 + turned][b * rows : (b + 1) * rows, :]


def settle(planes, parts, there):
    rows, width = parts[0].shape
    plane = lax.axis_index("yx").astype(jnp.int32).reshape(1)
    return pl.pallas_call(
        functools.partial(settle_kernel, planes),
        in_specs=[pl.BlockSpec(memory_space=pltpu.SMEM)]
        + [pl.BlockSpec(memory_space=pltpu.VMEM)] * 4,
        out_specs=pl.BlockSpec(memory_space=pltpu.VMEM),
        out_shape=jax.ShapeDtypeStruct((2, 2 * rows, width), LOW),
        compiler_params=pltpu.CompilerParams(vmem_limit_bytes=40 << 20),
        cost_estimate=pl.CostEstimate(
            flops=0, transcendentals=0, bytes_accessed=16 * rows * width
        ),
        name="settle",
    )(plane, parts[0], there[0], parts[1], there[1])


class Line:
    def __init__(self):
        self.held, self.pending = (), []

    def due(self, steps_between, *values):
        self.pending.append((steps_between, values))

    def wait(self, *values):
        self.due(0, *values)

    def run(self, step, *operands):
        waits = [values for count, values in self.pending if count <= 0]
        self.pending = [(count - 1, values) for count, values in self.pending if count > 0]
        operands, _ = lax.optimization_barrier((operands, (self.held, waits)))
        results = step(*operands)
        self.held = tuple(jax.tree.leaves(results)[:1])
        return results


def apart(flag, step, *operands):
    shapes = jax.eval_shape(step, *operands)

    def skip(_):
        return jax.tree.map(lambda shape: jnp.zeros(shape.shape, shape.dtype), shapes)

    return lax.cond(flag, lambda values: step(*values), skip, operands)


def after(value, earlier):
    return lax.optimization_barrier((value, earlier))[0]


def away(values):
    return lax.ppermute(values, ("core", "zp"), [(1, 2), (2, 1)])


def rehome(values):
    core, pair, _ = place()
    return jnp.where(core == pair, values, away(values))


def over(axis, values):
    return lax.ppermute(values, axis, SWAP)


def over_planes(values, bit, planes):
    return lax.ppermute(values, "yx", [(i, i ^ bit) for i in range(planes)])


def group_gather(own):
    core, _, near = place()
    half = ordered(near == 0, own, over("zl", own), own.ndim - 1)
    return ordered(core == 0, half, over("core", half), own.ndim - 1)


def group_sum(values):
    values = values + over("core", values)
    return values + over("zl", values)


def steps(count):
    return [1 << bit for bit in range(count.bit_length() - 1)]


def dp_gather(values, planes):
    core = lax.axis_index("core")
    plane = lax.axis_index("yx")
    values = ordered(core == 0, values, over("core", values), 0)
    for bit in steps(planes):
        values = ordered((plane & bit) == 0, values, over_planes(values, bit, planes), 0)
    return values


def dp_scatter_sum(values, planes):
    core = lax.axis_index("core")
    plane = lax.axis_index("yx")

    def halve(values, high):
        rows = values.shape[0] // 2
        send = lax.dynamic_slice_in_dim(values, (1 - high) * rows, rows, 0)
        return lax.dynamic_slice_in_dim(values, high * rows, rows, 0), send

    for bit in reversed(steps(planes)):
        keep, send = halve(values, jnp.where((plane & bit) == 0, 0, 1))
        values = keep + over_planes(send, bit, planes)
    keep, send = halve(values, core)
    return keep + over("core", send)


class WeightGather:
    def __init__(self, line, shard, planes):
        self.line, self.shard, self.planes = line, shard, planes
        self.other = over("zp", shard)

    def swap(self):
        core, pair, _ = place()
        stays = core == pair
        self.keep, send = self.line.run(
            lambda a, b: (jnp.where(stays, a, b), jnp.where(stays, b, a)), self.shard, self.other
        )
        self.sibling = over("core", send)

    @staticmethod
    def whole(shard, other):
        core, pair, _ = place()
        keep = jnp.where(core == pair, shard, other)
        sibling = over("core", jnp.where(core == pair, other, shard))
        return ordered(core == 0, keep, sibling, 1)

    def block(self):
        core = lax.axis_index("core")
        return self.line.run(lambda a, b: ordered(core == 0, a, b, 1), self.keep, self.sibling)

    def offload(self):
        return lax.all_gather(self.block(), "yx", axis=1, tiled=True)

    def split(self):
        core = lax.axis_index("core")
        self.parts = self.line.run(
            lambda a, b: tuple(ordered(core == 0, a[m], b[m], 0) for m in range(2)),
            self.keep,
            self.sibling,
        )
        self.turn = 0
        self.send()

    def send(self):
        bits = steps(self.planes)
        self.bits = (bits[self.turn], bits[-1 - self.turn])
        self.there = [over_planes(p, b, self.planes) for p, b in zip(self.parts, self.bits)]
        self.turn += 1

    def grow(self):
        plane = lax.axis_index("yx")
        bits, count = self.bits, len(steps(self.planes))

        def step(here, there):
            return tuple(
                ordered((plane & b) == 0, h, t, 0) for h, t, b in zip(here, there, bits)
            )

        if self.turn == count:
            return self.line.run(
                functools.partial(settle, self.planes), self.parts, tuple(self.there)
            )
        self.parts = self.line.run(step, self.parts, self.there)
        self.send()

    def most(self):
        for _ in steps(self.planes)[1:]:
            self.grow()


class WeightReduce:
    def __init__(self, line, planes):
        self.line, self.planes = line, planes

    def offload(self, grad):
        self.part = lax.psum_scatter(grad, "yx", scatter_dimension=1, tiled=True)

    def split(self, grad):
        plane = lax.axis_index("yx")
        bits = steps(self.planes)
        count = len(bits)
        self.left = [bits[::-1], bits]

        def cut(values):
            return tuple(
                v.reshape(*[2] * count, v.shape[0] >> count, v.shape[1]) for v in values
            )

        self.cut = lambda values: tuple(
            self.halves(v, plane, m, self.left[m]) for m, v in enumerate(values)
        )
        self.kept = self.line.run(lambda g: self.cut(cut((g[0], g[1]))), grad)
        self.send()

    def halves(self, values, plane, m, left):
        axis = 0 if m == 0 else len(left) - 1
        high = jnp.where((plane & left[0]) == 0, 0, 1)
        return (
            lax.dynamic_index_in_dim(values, high, axis, keepdims=False),
            lax.dynamic_index_in_dim(values, 1 - high, axis, keepdims=False).astype(LOW),
        )

    def send(self):
        self.there = [
            over_planes(self.kept[m][1], self.left[m][0], self.planes) for m in range(2)
        ]

    def shrink(self):
        self.left = [left[1:] for left in self.left]

        def add(kept, there):
            return tuple(k[0].astype(FULL) + t.astype(FULL) for k, t in zip(kept, there))

        if self.left[0]:
            self.kept = self.line.run(lambda k, t: self.cut(add(k, t)), self.kept, self.there)
            self.send()
        else:
            self.part = (self.kept, self.there, add)

    def most(self):
        for _ in steps(self.planes)[1:]:
            self.shrink()

    def swap(self):
        core = lax.axis_index("core")

        def step(part):
            if isinstance(part, tuple):
                part = jnp.stack(part)
            part = part.astype(LOW)
            rows = part.shape[1] // 2
            return (
                lax.dynamic_slice_in_dim(part, core * rows, rows, 1),
                lax.dynamic_slice_in_dim(part, (1 - core) * rows, rows, 1),
            )

        if isinstance(self.part, tuple):
            kept, there, add = self.part
            self.keep, send = self.line.run(lambda k, t: step(add(k, t)), kept, there)
        else:
            self.keep, send = self.line.run(step, self.part)
        self.sibling = over("core", send)

    def hop(self):
        core, pair, _ = place()
        stays = core == pair
        self.own, send = self.line.run(
            lambda a, b: (jnp.where(stays, a, b), jnp.where(stays, b, a)), self.keep, self.sibling
        )
        self.other = over("zp", send)

    def cross(self):
        core = lax.axis_index("core")
        both = self.line.run(
            lambda a, b: jnp.where(core == 0, jnp.stack([a, b]), jnp.stack([b, a])),
            self.keep,
            self.sibling,
        )
        self.total = lax.psum_scatter(both, "zp", scatter_dimension=0, tiled=False)


def mm(equation, left, right):
    return jnp.einsum(equation, left, right, preferred_element_type=FULL)


def per_device(
    planes,
    image_in,
    text_in,
    condition,
    image_cot,
    text_cot,
    qkv_weight,
    qv_bias,
    proj_weight,
    proj_bias,
    up_weight,
    up_bias,
    down_weight,
    down_bias,
    mod_weight,
    mod_bias,
):
    micro, image, quarter = image_in.shape
    length = image + text_in.shape[1]
    rows = -(-length // 16) * 16
    both = range(micro)
    core, pair, near = place()
    stays = core == pair
    is_image = lax.broadcasted_iota(jnp.int32, (rows, 1), 0) < image
    line = Line()

    def own_quarter(bias):
        return rehome(bias.astype(FULL))

    def by_row(table):
        return jnp.where(is_image, table[0][None], table[1][None])

    def sums(values):
        values = values.astype(FULL)
        return jnp.stack([values[:image].sum(axis=0), values[image:].sum(axis=0)])

    def gather(own):
        other, far = over("zl", own), over("core", own)
        return own, other, far, over("core", other)

    def fold(parts):
        own, near, (own_there, near_there) = parts
        line.wait(own_there)
        send = line.run(
            lambda a, b: (a.astype(FULL) + b.astype(FULL)).astype(LOW), near, near_there
        )
        return own, own_there, over("zl", send)

    def total(part):
        return part[0].astype(FULL) + part[1].astype(FULL) + part[2].astype(FULL)

    def row_sums(first, second):
        return jnp.stack([first.sum(axis=1), (first * second).sum(axis=1)])

    def columns(totals):
        return totals[0][:, None] / D, totals[1][:, None] / D

    row_count = mod_weight.shape[1]
    shards = [
        qkv_weight.reshape(2, row_count, -1),
        proj_weight.transpose(0, 2, 1),
        up_weight,
        down_weight.transpose(0, 2, 1),
    ]
    qkv_way = WeightGather(line, shards[0], planes)

    cond_all = dp_gather(condition, planes)
    silu_all = jax.nn.silu(cond_all.astype(FULL)).astype(LOW)
    dp_index = lax.axis_index(("yx", "core"))
    silu_rows = lax.dynamic_slice_in_dim(silu_all, dp_index * row_count, row_count, 1)
    mod_terms = mm("bi,sicj->bscj", silu_rows, mod_weight)
    mod_local = dp_scatter_sum(mod_terms, planes) + mod_bias.astype(FULL)[None]
    modulation = rehome(mod_local)
    wide_modulation = group_gather(modulation[:, :, :2])
    qv_own, proj_own, up_own, down_own = [
        own_quarter(bias) for bias in (qv_bias, proj_bias, up_bias, down_bias)
    ]
    qkv_own = jnp.concatenate([qv_own[:, 0], jnp.zeros_like(qv_own[:, 0]), qv_own[:, 1]], 1)

    call = functools.partial(rows_call, image=image, rows=rows)
    dense = 2 * rows * D
    hidden = up_weight.shape[2]

    def qkv_step(s, pieces):
        return line.run(
            lambda a, b, c, d: call(
                qkv_kernel,
                "qkv",
                tiles=a,
                tables=[b, c, d],
                outs=[(D, LOW), (3 * quarter, LOW), (LANES, FULL)],
                flops=dense * 3 * quarter,
                scratch=[(D, LOW)],
            ),
            pieces,
            wide_modulation[s],
            qkv,
            qkv_own[:, None],
        )

    def parts_of(outs):
        own, near, own_theirs, near_theirs = outs
        far = over("core", near_theirs)
        return own, near, (over("core", own_theirs), far)

    def spread_step(name, value, weight):
        return parts_of(
            line.run(
                lambda a, b: call(
                    spread_kernel,
                    name,
                    tiles=[a],
                    tables=[b],
                    outs=[(quarter, LOW)] * 4,
                    flops=dense * value.shape[1],
                ),
                value,
                weight,
            )
        )

    def up_step(pieces):
        return line.run(
            lambda a, b, c: call(
                up_kernel,
                "up",
                tiles=a,
                tables=[b, c],
                outs=[(D, LOW), (hidden, FULL), (hidden, LOW)],
                flops=dense * hidden,
            ),
            pieces,
            up,
            up_own[:, None],
        )

    def gather_step(pieces):
        return line.run(
            lambda a: call(gather_kernel, "gather", tiles=a, tables=[], outs=[(D, LOW)], flops=0),
            pieces,
        )[0]

    def mlp_back_step(value, pre):
        grad, *outs = line.run(
            lambda a, b, c, d: call(
                mlp_back_kernel,
                "mlp_back",
                tiles=[a, b],
                tables=[c, d],
                outs=[(hidden, LOW)] + [(quarter, LOW)] * 4,
                flops=dense * hidden * 2,
            ),
            value,
            pre,
            up,
            down,
        )
        return grad, parts_of(outs)

    def proj_back_step(pieces):
        return line.run(
            lambda a, b: call(
                proj_back_kernel,
                "proj_back",
                tiles=a,
                tables=[b],
                outs=[(D, LOW), (quarter, LOW)],
                flops=dense * quarter,
            ),
            pieces,
            proj,
        )

    def grad_step(lefts, rights):
        return line.run(lambda a, b: weight_grad(image, a, b), tuple(lefts), tuple(rights))

    def middle_step(s, part):
        def step(part, x, mod, bias):
            branch = total(part) + by_row(bias)
            value = x.astype(FULL) + by_row(mod[:, 2]) * branch
            return row_sums(value, value), value, branch

        totals, value, branch = line.run(step, part, inputs[s], modulation[s], proj_own)
        return group_sum(totals), value, branch

    def second_norm(s, totals, value):
        def step(totals, value, mod):
            average, square = columns(totals)
            factor = lax.rsqrt(square - average * average + NORM_EPS)
            normed = (value - average) * factor
            shifted = (normed * (1.0 + by_row(mod[:, 4])) + by_row(mod[:, 3])).astype(LOW)
            return shifted, normed, factor

        shifted, normed, factor = line.run(step, totals, value, modulation[s])
        return gather(shifted), normed, factor

    def cot_step(s):
        def step(cot, mod):
            low = (by_row(mod[:, 5]) * cot.astype(FULL)).astype(LOW)
            return low, sums(low)

        low, bias = line.run(step, cotangents[s], modulation[s])
        return gather(low), bias

    def scaled_step(s, part, normed, which):
        def step(part, normed, mod):
            grad = total(part)
            scaled = grad * (1.0 + by_row(mod[:, which]))
            return row_sums(scaled, normed), scaled, sums(grad), sums(grad * normed)

        totals, scaled, shift, scale = line.run(step, part, normed, modulation[s])
        return group_sum(totals), scaled, shift, scale

    def middle_back(s, totals, scaled, normed, factor, branch):
        def step(totals, scaled, normed, factor, branch, cot, mod):
            grad_mean, cross_mean = columns(totals)
            grad = cot.astype(FULL) + factor * (scaled - grad_mean - normed * cross_mean)
            low = (by_row(mod[:, 2]) * grad).astype(LOW)
            return low, grad, sums(grad * branch), sums(low)

        low, grad, gate, bias = line.run(
            step, totals, scaled, normed, factor, branch, cotangents[s], modulation[s]
        )
        return gather(low), grad, gate, bias

    def first_back(totals, scaled, normed, stats, grad_middle):
        def step(totals, scaled, normed, stats, grad_middle):
            grad_mean, cross_mean = columns(totals)
            grad = grad_middle + stats[:, 1:2] * (scaled - grad_mean - normed * cross_mean)
            return grad.astype(LOW), grad

        low, grad = line.run(step, totals, scaled, normed, stats, grad_middle)
        return grad, away(low)

    def output_step(s, part, value):
        def step(part, value, cot, mod, bias):
            branch = total(part) + by_row(bias)
            out = (value + by_row(mod[:, 5]) * branch).astype(LOW)
            return out, sums(cot.astype(FULL) * branch)

        out, gate = line.run(step, part, value, cotangents[s], modulation[s], down_own)
        return (out, away(out)), gate

    def first_norm(s, stats):
        return line.run(
            lambda x, t: (x.astype(FULL) - t[:, 0:1]) * t[:, 1:2], inputs[s], stats
        )

    none = [None] * micro
    wide, attn_in, joint, stats, attended, log_total = (list(none) for _ in range(6))
    branch_one, middle, totals, normed_two, factor_two = (list(none) for _ in range(5))
    mlp_in, pre_act, activated, grad_two, grad_two_full = (list(none) for _ in range(5))
    grad_pre, part_a, part_b, part_c = (list(none) for _ in range(4))
    shift_two, scale_two, gate_two, shift_one, scale_one, gate_one = (list(none) for _ in range(6))
    scaled, grad_middle, one_bias, grad_one_full, grad_joint = (list(none) for _ in range(5))
    normed_one, outs, grad_in = (list(none) for _ in range(3))

    def settle_in(own, moved):
        return line.run(lambda a, b: jnp.where(stays, a, b), own, moved)

    two_bias, pieces, parts = list(none), list(none), list(none)

    raw = line.run(functools.partial(join, rows), image_in, text_in)
    qkv_way.swap()
    moved = away(after(raw[0], qkv_way.keep))
    qkv_way.split()
    line.wait(mod_local)
    inputs = [settle_in(raw[0], moved)]
    wide[0] = gather(inputs[0])
    proj_way = WeightGather(line, after(shards[1], inputs[0]), planes)
    qkv_way.most()
    proj_way.swap()
    up_way = WeightGather(line, after(shards[2], proj_way.keep), planes)
    proj_way.split()
    cot_raw = line.run(functools.partial(join, rows), image_cot, text_cot)
    line.wait(wide[0][1])
    qkv = qkv_way.grow()
    attn_in[0], joint[0], stats[0] = qkv_step(0, wide[0])
    up_way.swap()
    moved = away(after(raw[1], up_way.keep))
    up = up_way.offload()
    proj_way.most()
    attended[0], log_total[0] = line.run(lambda a: attend(a, length), joint[0])
    inputs.append(settle_in(raw[1], moved))
    wide[1] = gather(inputs[1])
    moved = away(after(cot_raw[0], inputs[1]))
    proj = proj_way.grow()
    part_a[0] = spread_step("proj", attended[0], proj)
    part_a[0] = fold(part_a[0])
    cotangents = [settle_in(cot_raw[0], moved)]
    down_way = WeightGather(line, after(shards[3], cotangents[0]), planes)
    attn_in[1], joint[1], stats[1] = qkv_step(1, wide[1])
    totals[0], middle[0], branch_one[0] = middle_step(0, part_a[0])
    attended[1], log_total[1] = line.run(lambda a: attend(a, length), joint[1])
    down_way.swap()
    down = down_way.offload()
    pieces[0], normed_two[0], factor_two[0] = second_norm(0, totals[0], middle[0])
    part_a[1] = spread_step("proj", attended[1], proj)
    normed_one[0] = first_norm(0, stats[0])
    normed_one[1] = first_norm(1, stats[1])
    line.wait(pieces[0][1])
    part_a[1] = fold(part_a[1])
    mlp_in[0], pre_act[0], activated[0] = up_step(pieces[0])
    totals[1], middle[1], branch_one[1] = middle_step(1, part_a[1])
    pieces[1], normed_two[1], factor_two[1] = second_norm(1, totals[1], middle[1])
    line.wait(pieces[1][1])
    grad_two[0], two_bias[0] = cot_step(0)
    moved = away(after(cot_raw[1], grad_two[0][0]))
    mlp_in[1], pre_act[1], activated[1] = up_step(pieces[1])
    cotangents.append(settle_in(cot_raw[1], moved))
    line.wait(grad_two[0][1])
    grad_two[1], two_bias[1] = cot_step(1)
    grad_two_full[0] = gather_step(grad_two[0])
    line.wait(grad_two[1][1])
    grad_two_full[1] = gather_step(grad_two[1])

    down_sum = WeightReduce(line, planes)
    down_sum.offload(grad_step(grad_two_full, activated)[0])
    grad_pre[0], part_b[0] = mlp_back_step(grad_two_full[0], pre_act[0])
    part_b[0] = fold(part_b[0])
    grad_pre[1], part_b[1] = mlp_back_step(grad_two_full[1], pre_act[1])
    totals[0], scaled[0], shift_two[0], scale_two[0] = scaled_step(0, part_b[0], normed_two[0], 4)
    up_sum = WeightReduce(line, planes)
    grad, up_rows = grad_step(mlp_in, grad_pre)
    up_sum.offload(grad)
    part_b[1] = fold(part_b[1])
    part_c[0] = spread_step("down", activated[0], down)
    pieces[0], grad_middle[0], gate_one[0], one_bias[0] = middle_back(
        0, totals[0], scaled[0], normed_two[0], factor_two[0], branch_one[0]
    )
    part_c[1] = spread_step("down", activated[1], down)
    line.wait(pieces[0][1])
    totals[1], scaled[1], shift_two[1], scale_two[1] = scaled_step(1, part_b[1], normed_two[1], 4)
    part_c[0] = fold(part_c[0])
    pieces[1], grad_middle[1], gate_one[1], one_bias[1] = middle_back(
        1, totals[1], scaled[1], normed_two[1], factor_two[1], branch_one[1]
    )
    down_sum.swap()
    grad_one_full[0], grad_attended = proj_back_step(pieces[0])
    outs[0], gate_two[0] = output_step(0, part_c[0], middle[0])
    line.wait(pieces[1][1])
    part_c[1] = fold(part_c[1])
    down_sum.cross()
    grad_joint[0] = line.run(
        lambda a, b, c: attend_back(a, b, c, length), joint[0], log_total[0], grad_attended
    )
    up_sum.swap()
    grad_one_full[1], grad_attended = proj_back_step(pieces[1])
    up_sum.cross()
    part_a[0] = spread_step("qkv_back", grad_joint[0], qkv)
    proj_sum = WeightReduce(line, planes)
    proj_sum.offload(grad_step(grad_one_full, attended)[0])
    part_a[0] = fold(part_a[0])
    grad_joint[1] = line.run(
        lambda a, b, c: attend_back(a, b, c, length), joint[1], log_total[1], grad_attended
    )
    down_grad = line.run(lambda a: a.astype(FULL).transpose(0, 2, 1), down_sum.total)
    part_a[1] = spread_step("qkv_back", grad_joint[1], qkv)
    totals[0], scaled[0], shift_one[0], scale_one[0] = scaled_step(0, part_a[0], normed_one[0], 1)
    part_a[1] = fold(part_a[1])
    qkv_sum = WeightReduce(line, planes)
    grad, qkv_rows = grad_step(attn_in, grad_joint)
    qkv_sum.split(grad)
    grad_in[0] = first_back(totals[0], scaled[0], normed_one[0], stats[0], grad_middle[0])
    outs[1], gate_two[1] = output_step(1, part_c[1], middle[1])

    def pack():
        qv = jnp.concatenate([qkv_rows[:, 0, :quarter], qkv_rows[:, 0, 2 * quarter :]], 1)
        return jnp.concatenate(
            [qv, one_bias[0] + one_bias[1], two_bias[0] + two_bias[1], up_rows[:, 0]], 1
        )

    def mod_rows(s):
        return jnp.concatenate(
            [shift_one[s], scale_one[s], gate_one[s], shift_two[s], scale_two[s], gate_two[s]], 1
        )

    packed = line.run(pack)
    up_grad = line.run(lambda a: a.astype(FULL), up_sum.total)
    line.wait(grad_in[0][1])
    qkv_sum.most()
    totals[1], scaled[1], shift_one[1], scale_one[1] = scaled_step(1, part_a[1], normed_one[1], 1)
    proj_sum.swap()
    grad_in[1] = first_back(totals[1], scaled[1], normed_one[1], stats[1], grad_middle[1])
    grad_mods = line.run(lambda: jnp.stack([mod_rows(s) for s in both]).astype(LOW))
    line.wait(outs[1][1])
    grad_mods = line.run(rehome, grad_mods)
    qkv_sum.shrink()
    qkv_sum.swap()
    qkv_sum.hop()
    proj_sum.hop()

    def late(outs):
        outs = [jnp.where(stays, own, home) for own, home in outs]
        return (
            jnp.stack([out[:image] for out in outs]),
            jnp.stack([out[image:length] for out in outs]),
        )

    image_out, text_out = line.run(late, outs)

    def last_sums(grad_mods, packed, silu_rows, mod_weight, condition):
        every = dp_gather(grad_mods, planes)
        every = every.reshape(*every.shape[:2], 6, quarter)
        silu_grad = mm("bscj,sicj->bi", every, mod_weight)
        silu_grad = lax.all_to_all(
            silu_grad, ("yx", "core"), split_axis=0, concat_axis=1, tiled=True
        )
        for bit in steps(planes):
            packed = packed + over_planes(packed, bit, planes)
        packed = after(packed, silu_grad)
        packed = packed + over("zp", packed)
        packed = jnp.where(stays, packed, over("core", packed))
        silu_grad = silu_grad + over("zp", silu_grad)
        silu_grad = silu_grad + over("zl", silu_grad)
        return (
            jax.vjp(jax.nn.silu, condition.astype(FULL))[1](silu_grad)[0],
            mm("bi,bscj->sicj", silu_rows, every),
            jnp.sum(every.astype(FULL), axis=0),
            packed,
        )

    flag = condition[0, 0] == condition[0, 0]
    condition_grad, mod_weight_grad, mod_bias_grad, packed = line.run(
        functools.partial(apart, flag, last_sums),
        grad_mods,
        packed,
        silu_rows,
        mod_weight,
        condition,
    )
    qkv_grad, proj_grad = line.run(
        lambda sums: [own.astype(FULL) + other.astype(FULL) for own, other in sums],
        [(one.own, one.other) for one in (qkv_sum, proj_sum)],
    )
    qkv_grad = qkv_grad.reshape(qkv_weight.shape)
    bias_grads = [
        packed[:, : 2 * quarter].reshape(qv_bias.shape),
        packed[:, 2 * quarter : 3 * quarter],
        packed[:, 4 * quarter :],
        packed[:, 3 * quarter : 4 * quarter],
    ]

    grad_in = [jnp.where(stays, own, home.astype(FULL)) for own, home in grad_in]
    image_grad = jnp.stack([grad[:image] for grad in grad_in])
    text_grad = jnp.stack([grad[image:length] for grad in grad_in])
    proj_grad = proj_grad.transpose(0, 2, 1)
    return (
        image_out,
        text_out,
        image_grad,
        text_grad,
        condition_grad,
        qkv_grad,
        bias_grads[0],
        proj_grad,
        bias_grads[1],
        up_grad,
        bias_grads[2],
        down_grad,
        bias_grads[3],
        mod_weight_grad,
        mod_bias_grad,
    )


def solution(mesh):
    planes = mesh.shape["dp"] // 2
    split = Mesh(mesh.devices.reshape(planes, 2, 2, 2), ("yx", "core", "zp", "zl"))
    dp, tensor = ("yx", "core"), ("zp", "zl")
    tokens = P(dp, None, tensor)
    placed = (
        tokens,
        tokens,
        P(dp, None),
        tokens,
        tokens,
        P(None, dp, None, tensor),
        P(None, None, tensor),
        P(None, tensor, dp),
        P(None, tensor),
        P(None, dp, tensor),
        P(None, tensor),
        P(None, tensor, dp),
        P(None, tensor),
        P(None, dp, None, tensor),
        P(None, None, tensor),
    )
    return jax.shard_map(
        functools.partial(per_device, planes),
        mesh=split,
        in_specs=placed,
        out_specs=(tokens,) * 4 + (P(dp, None),) + placed[5:],
        check_vma=False,
    )
```

time: 1310 us -> 1060 us (0.81)
  waiting for transfers between devices: 542 us -> 338 us
  other arithmetic: 147 us -> 109 us
  local copies, waits for them, and re-layouts: 84.1 us -> 53.4 us
  Pallas kernels: 334 us -> 360 us
    ppermute x91 -> x117, waiting for transfers between devices: 539 us -> 338 us  [the longest x83 238 us: over(): return lax.ppermute(values, axis, SWAP)]
    select_n x26 -> x18, other arithmetic: 52.9 us -> 6.94 us  [ordered(): jnp.where(first_here, jnp.concatenate([here, there], axis), jnp.concatena...]
    concatenate x5, local copies, waits for them, and re-layouts: 21.2 us -> 0.19 us  [the longest x4 0.17 us: ordered(): jnp.concatenate([here, there], axis)]
    pallas_call x12 -> x20, Pallas kernels: 165 us -> 181 us  [the longest x16 180 us: rows_call(): pl.pallas_call(functools.partial(rows_kernel, kernel, split, rows - image...]
    convert_element_type x7 -> x17, other arithmetic: 9.73 us -> 22.9 us  [the longest x8 12.4 us: fold(): (a.astype(FULL) + b.astype(FULL)).astype(LOW)]
    mul x6 -> x10, other arithmetic: 18.9 us -> 28.1 us  [the longest x4 8.29 us: step(): return (row_sums(scaled, normed), scaled, sums(grad), sums(grad * normed))]
    ppermute x91 -> x117, starting transfers between devices: 164 us -> 159 us  [the longest x83 122 us: over(): return lax.ppermute(values, axis, SWAP)]
  transfers between devices with their start and end apart: 100 -> 124, of which waited for: 47 -> 48; matrix products, arithmetic and copies ran while one was open for 16% -> 13% of each run, Pallas kernels for 26% -> 34%
where the time goes in v2:
time: 1060 us; the launch traced here: 1050 us
  Pallas kernels  360 us (34%)
  waiting for transfers between devices  338 us (32%)
  starting transfers between devices  160 us (15%)
  other arithmetic  109 us (10%)
  local copies, waits for them, and re-layouts  53.4 us (5%)
  between operations  17.6 us (2%)
    ppermute x83, waiting for transfers between devices, over(): return lax.ppermute(values, axis, SWAP)  238 us
    pallas_call x16, Pallas kernels, rows_call(): pl.pallas_call(functools.partial(rows_kernel, kernel, split, rows - image...  180 us
    ppermute x83, starting transfers between devices, over(): return lax.ppermute(values, axis, SWAP)  122 us
    ppermute x20, waiting for transfers between devices, over_planes(): return lax.ppermute(values, 'yx', [(i, i ^ bit) for i in range(planes)])  100 us
    pallas_call x4, Pallas kernels, weight_grad(): pl.pallas_call(functools.partial(weight_kernel, image), grid=(width // BL...  71 us
    pallas_call x2, Pallas kernels, attend_back(): pl.pallas_call(functools.partial(attend_back_kernel, length), out_shape=j...  62.6 us
    pallas_call x2, Pallas kernels, attend(): pl.pallas_call(functools.partial(attend_kernel, length), out_shape=(jax.S...  45 us
    ppermute x20, starting transfers between devices, over_planes(): return lax.ppermute(values, 'yx', [(i, i ^ bit) for i in range(planes)])  26.1 us
  transfers between devices with their start and end apart: 124, of which 48 were waited for; matrix products, arithmetic and copies ran while one was open for 13% of the time, Pallas kernels for 34%

profile of v2, /device:TPU:0, one launch (start us, length us, event | category | flops | bytes accessed | tf_op | source)
XLA Modules:
  0.0 1052.0 jit_solution(14370043538930078516)
XLA Ops:
  30.7 32.0 %collective-permute-done.9 = bf16[2,192,1152]{2,1,0:T(8,128)(2,1)} collective-permute-done((bf16[2,192,1152]{2,1,0:T(8,128)(2,1)}, bf16[2,192,1152]{2,1,0:T(8,128)(2,1)}, u32[]{:S(2)}, u32[]{:S(2)}) %collective-permute-start.9) | collective-permute-done | bytes 884768 | tf_op jit(solution)/shard_map/ppermute | solution.py:475
  82.5 21.2 %collective-permute-start.28 = (bf16[2,192,384]{2,1,0:T(8,128)(2,1)S(1)}, bf16[2,192,384]{2,1,0:T(8,128)(2,1)S(1)}, u32[]{:S(2)}, u32[]{:S(2)}) collective-permute-start(bf16[2,192,384]{2,1,0:T(8,128)(2,1)S(1)} %bitcast.142), channel_id=1, source_target_pairs={{0,2},{2,0},{1,3},{3,1},{4,6},{6,4},{5,7},{7,5},{8,10},{10,8},{9,1... | collective-permute-start | bytes 884744 | tf_op jit(solution)/shard_map/ppermute | solution.py:475
  124.8 29.1 %collective-permute-done.27.refs_3_ = bf16[768,1152]{1,0:T(8,128)(2,1)S(1)} collective-permute-done((bf16[768,1152]{1,0:T(8,128)(2,1)S(1)}, bf16[768,1152]{1,0:T(8,128)(2,1)S(1)}, u32[]{:S(2)}, u32[]{:S(2)}) %collective-permute-start.27) | collective-permute-done | bytes 1769504 | tf_op jit(solution)/shard_map/ppermute | solution.py:479
  192.3 22.5 %attend.2 = (bf16[1184,384]{1,0:T(8,128)(2,1)}, f32[3,8,1280]{2,1,0:T(8,128)}) custom-call(bf16[1184,1152]{1,0:T(8,128)(2,1)} %get-tuple-element.618.q_ref.k_ref.v_ref, bf16[1184,1152]{1,0:T(8,128)(2,1)} %get-tuple-element.618.q_ref.k_ref.v_ref, bf16[1184,1152]{1,0:T(8,128)(2,1)} %get-tuple-element.618.q_ref.k_ref.v_ref), custom_call_target="tpu_custom_call" | custom-call | flops 21532508160 | bytes 4091904 | tf_op jit(solution)/shard_map/attend/pallas_call | solution.py:283
  285.8 22.5 %attend.3 = (bf16[1184,384]{1,0:T(8,128)(2,1)}, f32[3,8,1280]{2,1,0:T(8,128)}) custom-call(bf16[1184,1152]{1,0:T(8,128)(2,1)} %get-tuple-element.645.q_ref.k_ref.v_ref, bf16[1184,1152]{1,0:T(8,128)(2,1)} %get-tuple-element.645.q_ref.k_ref.v_ref, bf16[1184,1152]{1,0:T(8,128)(2,1)} %get-tuple-element.645.q_ref.k_ref.v_ref), custom_call_target="tpu_custom_call" | custom-call | flops 21532508160 | bytes 4091904 | tf_op jit(solution)/shard_map/attend/pallas_call | solution.py:283
  344.5 15.2 %up.2 = (bf16[1184,1536]{1,0:T(8,128)(2,1)}, f32[1184,1536]{1,0:T(8,128)}, bf16[1184,1536]{1,0:T(8,128)(2,1)}) custom-call(s32[2]{0:T(128)} %pad_add_fusion.here_ref, bf16[1184,384]{1,0:T(8,128)(2,1)} %copy-done.64, bf16[1184,384]{1,0:T(8,128)(2,1)} %copy-done.95, bf16[1184,384]{1,0:T(8,128)(2,1)} %copy-done.94, ...), custom_call_target="tpu_custom_call" | custom-call | flops 5586812928 | bytes 27635712 | tf_op jit(solution)/shard_map/up/pallas_call | solution.py:78
  377.3 20.9 %collective-permute-done.59.refs_1_ = bf16[1184,384]{1,0:T(8,128)(2,1)S(1)} collective-permute-done((bf16[1184,384]{1,0:T(8,128)(2,1)S(1)}, bf16[1184,384]{1,0:T(8,128)(2,1)S(1)}, u32[]{:S(2)}, u32[]{:S(2)}) %collective-permute-start.59) | collective-permute-done | bytes 909344 | tf_op jit(solution)/shard_map/ppermute | solution.py:475
  402.3 15.1 %up.3 = (bf16[1184,1536]{1,0:T(8,128)(2,1)}, f32[1184,1536]{1,0:T(8,128)}, bf16[1184,1536]{1,0:T(8,128)(2,1)}) custom-call(s32[2]{0:T(128)} %pad_add_fusion.here_ref, bf16[1184,384]{1,0:T(8,128)(2,1)} %copy-done.67, bf16[1184,384]{1,0:T(8,128)(2,1)} %copy-done.99, bf16[1184,384]{1,0:T(8,128)(2,1)} %copy-done.100, ...), custom_call_target="tpu_custom_call" | custom-call | flops 5586812928 | bytes 27635712 | tf_op jit(solution)/shard_map/up/pallas_call | solution.py:78
  417.5 13.8 %collective-permute-done.63.refs_1_ = bf16[1184,384]{1,0:T(8,128)(2,1)S(1)} collective-permute-done((bf16[1184,384]{1,0:T(8,128)(2,1)S(1)}, bf16[1184,384]{1,0:T(8,128)(2,1)S(1)}, u32[]{:S(2)}, u32[]{:S(2)}) %collective-permute-start.63) | collective-permute-done | bytes 909344 | tf_op jit(solution)/shard_map/ppermute | solution.py:475
  435.8 19.1 %collective-permute-done.64.refs_1_ = bf16[1184,384]{1,0:T(8,128)(2,1)S(1)} collective-permute-done((bf16[1184,384]{1,0:T(8,128)(2,1)S(1)}, bf16[1184,384]{1,0:T(8,128)(2,1)S(1)}, u32[]{:S(2)}, u32[]{:S(2)}) %collective-permute-start.64) | collective-permute-done | bytes 909344 | tf_op jit(solution)/shard_map/ppermute | solution.py:475
  466.7 20.6 %weight_grad.4 = (bf16[2,1536,1536]{2,1,0:T(8,128)(2,1)}, f32[2,1,1536]{2,1,0:T(1,128)}) custom-call(bf16[1184,1536]{1,0:T(8,128)(2,1)} %gather.2.left_zero.refs_0_, bf16[1184,1536]{1,0:T(8,128)(2,1)} %gather.3.left_one.refs_0_, bf16[1184,1536]{1,0:T(8,128)(2,1)} %get-tuple-element.567.right_zero.refs_0_, bf16[1184,1536]{1,0:T(8,128)(2,1)} %get-tuple-element.580.right_one.refs_0_), custom_call_target="tpu_custom_call" | custom-call | flops 11173625856 | bytes 23986176 | tf_op jit(solution)/shard_map/weight_grad/pallas_call | solution.py:218
  487.4 22.3 %mlp_back.2 = (bf16[1184,1536]{1,0:T(8,128)(2,1)}, bf16[1184,384]{1,0:T(8,128)(2,1)}, bf16[1184,384]{1,0:T(8,128)(2,1)}, bf16[1184,384]{1,0:T(8,128)(2,1)}, bf16[1184,384]{1,0:T(8,128)(2,1)}) custom-call(s32[2]{0:T(128)} %pad_add_fusion.here_ref, bf16[1184,1536]{1,0:T(8,128)(2,1)} %gather.2.left_zero.refs_0_, f32[1184,1536]{1,0:T(8,128)} %get-tuple-element.537.refs_1_, ...), custom_call_target="tpu_custom_call" | custom-call | flops 11173625856 | bytes 37060608 | tf_op jit(solution)/shard_map/mlp_back/pallas_call | solution.py:78
  515.2 22.6 %mlp_back.3 = (bf16[1184,1536]{1,0:T(8,128)(2,1)}, bf16[1184,384]{1,0:T(8,128)(2,1)}, bf16[1184,384]{1,0:T(8,128)(2,1)}, bf16[1184,384]{1,0:T(8,128)(2,1)}, bf16[1184,384]{1,0:T(8,128)(2,1)}) custom-call(s32[2]{0:T(128)} %pad_add_fusion.here_ref, bf16[1184,1536]{1,0:T(8,128)(2,1)} %gather.3.left_one.refs_0_, f32[1184,1536]{1,0:T(8,128)} %get-tuple-element.547.refs_1_, ...), custom_call_target="tpu_custom_call" | custom-call | flops 11173625856 | bytes 37060608 | tf_op jit(solution)/shard_map/mlp_back/pallas_call | solution.py:78
  541.5 20.8 %weight_grad.5 = (bf16[2,1536,1536]{2,1,0:T(8,128)(2,1)}, f32[2,1,1536]{2,1,0:T(1,128)}) custom-call(bf16[1184,1536]{1,0:T(8,128)(2,1)} %get-tuple-element.559.left_zero, bf16[1184,1536]{1,0:T(8,128)(2,1)} %get-tuple-element.560.left_one, bf16[1184,1536]{1,0:T(8,128)(2,1)} %get-tuple-element.561.right_zero, bf16[1184,1536]{1,0:T(8,128)(2,1)} %get-tuple-element.562.right_one), custom_call_target="tpu_custom_call" | custom-call | flops 11173625856 | bytes 23986176 | tf_op jit(solution)/shard_map/weight_grad/pallas_call | solution.py:218
  656.1 14.1 %collective-permute-done.89.refs_1_ = bf16[1184,384]{1,0:T(8,128)(2,1)} collective-permute-done((bf16[1184,384]{1,0:T(8,128)(2,1)}, bf16[1184,384]{1,0:T(8,128)(2,1)}, u32[]{:S(2)}, u32[]{:S(2)}) %collective-permute-start.89) | collective-permute-done | bytes 909344 | tf_op jit(solution)/shard_map/ppermute | solution.py:475
  674.5 31.4 %attend_back.2.refs_0_.right_zero = bf16[1184,1152]{1,0:T(8,128)(2,1)} custom-call(bf16[1184,1152]{1,0:T(8,128)(2,1)} %get-tuple-element.618.q_ref.k_ref.v_ref, bf16[1184,1152]{1,0:T(8,128)(2,1)} %get-tuple-element.618.q_ref.k_ref.v_ref, bf16[1184,1152]{1,0:T(8,128)(2,1)} %get-tuple-element.618.q_ref.k_ref.v_ref, ...), custom_call_target="tpu_custom_call" | custom-call | flops 32298762240 | bytes 8183808 | tf_op jit(solution)/shard_map/attend_back/pallas_call | solution.py:373
  762.2 31.2 %attend_back.3.refs_0_.right_one = bf16[1184,1152]{1,0:T(8,128)(2,1)} custom-call(bf16[1184,1152]{1,0:T(8,128)(2,1)} %get-tuple-element.645.q_ref.k_ref.v_ref, bf16[1184,1152]{1,0:T(8,128)(2,1)} %get-tuple-element.645.q_ref.k_ref.v_ref, bf16[1184,1152]{1,0:T(8,128)(2,1)} %get-tuple-element.645.q_ref.k_ref.v_ref, ...), custom_call_target="tpu_custom_call" | custom-call | flops 32298762240 | bytes 8183808 | tf_op jit(solution)/shard_map/attend_back/pallas_call | solution.py:373
  806.5 17.5 %collective-permute-done.97 = bf16[1184,384]{1,0:T(8,128)(2,1)S(1)} collective-permute-done((bf16[1184,384]{1,0:T(8,128)(2,1)S(1)}, bf16[1184,384]{1,0:T(8,128)(2,1)S(1)}, u32[]{:S(2)}, u32[]{:S(2)}) %collective-permute-start.97) | collective-permute-done | bytes 909344 | tf_op jit(solution)/shard_map/ppermute | solution.py:475
  833.2 18.9 %weight_grad.7 = (bf16[2,1536,1152]{2,1,0:T(8,128)(2,1)}, f32[2,1,1152]{2,1,0:T(1,128)}) custom-call(bf16[1184,1536]{1,0:T(8,128)(2,1)} %get-tuple-element.662.left_zero, bf16[1184,1536]{1,0:T(8,128)(2,1)} %get-tuple-element.663.left_one, bf16[1184,1152]{1,0:T(8,128)(2,1)} %attend_back.2.refs_0_.right_zero, bf16[1184,1152]{1,0:T(8,128)(2,1)} %attend_back.3.refs_0_.right_one), custom_call_target="tpu_custom_call" | custom-call | flops 8380219392 | bytes 19808256 | tf_op jit(solution)/shard_map/weight_grad/pallas_call | solution.py:218
  869.9 33.6 %collective-permute-done.105 = bf16[2,384,1152]{2,1,0:T(8,128)(2,1)} collective-permute-done((bf16[2,384,1152]{2,1,0:T(8,128)(2,1)}, bf16[2,384,1152]{2,1,0:T(8,128)(2,1)}, u32[]{:S(2)}, u32[]{:S(2)}) %collective-permute-start.105) | collective-permute-done | bytes 1769504 | tf_op jit(solution)/shard_map/ppermute | solution.py:479
  930.9 15.8 %collective-permute-done.108 = bf16[384,1152]{1,0:T(8,128)(2,1)S(1)} collective-permute-done((bf16[384,1152]{1,0:T(8,128)(2,1)S(1)}, bf16[384,1152]{1,0:T(8,128)(2,1)S(1)}, u32[]{:S(2)}, u32[]{:S(2)}) %collective-permute-start.108) | collective-permute-done | bytes 884768 | tf_op jit(solution)/shard_map/ppermute | solution.py:479
  960.3 20.5 %collective-permute-start.115 = (bf16[2,192,1152]{2,1,0:T(8,128)(2,1)S(1)}, bf16[2,192,1152]{2,1,0:T(8,128)(2,1)S(1)}, u32[]{:S(2)}, u32[]{:S(2)}) collective-permute-start(bf16[2,192,1152]{2,1,0:T(8,128)(2,1)S(1)} %get-tuple-element.961), channel_id=1, source_target_pairs={{0,2},{2,0},{1,3},{3,1},{4,6},{6,4},{5,7},{7,5},{8,10},{10,8},{9,1... | collective-permute-start | bytes 2654216 | tf_op jit(solution)/shard_map/ppermute | solution.py:475
  983.2 58.3 %conditional.1 = (f32[2,1536]{1,0:T(2,128)S(1)}, f32[2,192,6,384]{3,1,2,0:T(8,128)}, f32[2,3072]{1,0:T(2,128)}, f32[2,768]{1,0:T(2,128)}, f32[2,384]{1,0:T(2,128...) conditional(s32[]{:T(128)} %bitcast.61, () %tuple.203, ...), branch_computations={%region_49.50_spmd, %region_50.52_spmd} | conditional | flops 58154508 | bytes 8399401 | solution.py:458
  1008.9 23.4 %collective-permute-done.3 = f32[2,1536]{1,0:T(2,128)S(1)} collective-permute-done((f32[2,1536]{1,0:T(2,128)S(1)}, f32[2,1536]{1,0:T(2,128)S(1)}, u32[]{:S(2)}, u32[]{:S(2)}) %collective-permute-start.3) | collective-permute-done | bytes 12320 | tf_op jit(solution)/shard_map/cond/branch_1_fun/ppermute | solution.py:475
  (770 shorter events, 530.3 us)
Async XLA Ops:
  7.2 337.3 %all-gather.3.cloned.1.call-start = ((), (), s32[]{:S(2)}) async-start(), calls=%async_computation.6 | async-start | bytes 11796480 | tf_op jit(solution)/shard_map/all_gather | solution.py:547
  23.2 39.4 %collective-permute-start.9 = (bf16[2,192,1152]{2,1,0:T(8,128)(2,1)}, bf16[2,192,1152]{2,1,0:T(8,128)(2,1)}, u32[]{:S(2)}, u32[]{:S(2)}) collective-permute-start(bf16[2,192,1152]{2,1,0:T(8,128)(2,1)} %bitcast.74), channel_id=1, source_target_pairs={{0,2},{2,0},{1,3},{3,1},{4,6},{6,4},{5,7},{7,5},{8,10},{10,8},{9,1... | collective-permute-start | bytes 2654216 | tf_op jit(solution)/shard_map/ppermute | solution.py:475
  28.0 39.9 %collective-permute-start.30 = (f32[2,2,384]{2,0,1:T(2,128)S(1)}, f32[2,2,384]{2,0,1:T(2,128)S(1)}, u32[]{:S(2)}, u32[]{:S(2)}) collective-permute-start(f32[2,2,384]{2,0,1:T(2,128)S(1)} %copy_convert_fusion), channel_id=1, source_target_pairs={{2,4},{4,2},{3,5},{5,3},{10,12},{12,10},{11,13},{13,11},{18,20},{2... | collective-permute-start | bytes 18440 | tf_op jit(solution)/shard_map/ppermute | solution.py:466
  72.4 47.9 %collective-permute-start.23 = (f32[2,2,2,768]{3,2,1,0:T(2,128)S(1)}, f32[2,2,2,768]{3,2,1,0:T(2,128)S(1)}, u32[]{:S(2)}, u32[]{:S(2)}) collective-permute-start(f32[2,2,2,768]{3,2,1,0:T(2,128)S(1)} %maximum_select_fusion.20), channel_id=1, source_target_pairs={{0,4},{4,0},{1,5},{5,1},{2,6},{6,2},{3,7},{7,3},{8,12},{12,8},{9,1... | collective-permute-start | bytes 73736 | tf_op jit(solution)/shard_map/ppermute | solution.py:475
  104.3 49.6 %collective-permute-start.26 = (bf16[768,1152]{1,0:T(8,128)(2,1)S(1)}, bf16[768,1152]{1,0:T(8,128)(2,1)S(1)}, u32[]{:S(2)}, u32[]{:S(2)}) collective-permute-start(bf16[768,1152]{1,0:T(8,128)(2,1)S(1)} %maximum_select_fusion.9.refs_0_), channel_id=1, source_target_pairs={{0,16},{8,24},{16,0},{24,8},{1,17},{9,25},{17,1},{25,9},{2,18},{10... | collective-permute-start | bytes 5308424 | tf_op jit(solution)/shard_map/ppermute | solution.py:479
  120.5 55.0 %collective-permute-start.33 = (bf16[2,192,1536]{2,1,0:T(8,128)(2,1)S(1)}, bf16[2,192,1536]{2,1,0:T(8,128)(2,1)S(1)}, u32[]{:S(2)}, u32[]{:S(2)}) collective-permute-start(bf16[2,192,1536]{2,1,0:T(8,128)(2,1)S(1)} %copy-done.46), channel_id=1, source_target_pairs={{0,2},{2,0},{1,3},{3,1},{4,6},{6,4},{5,7},{7,5},{8,10},{10,8},{9,1... | collective-permute-start | bytes 3538952 | tf_op jit(solution)/shard_map/ppermute | solution.py:475
  180.3 307.1 %all-gather.5.cloned.1.call-start = ((), (), s32[]{:S(2)}) async-start(), calls=%async_computation.7 | async-start | bytes 11796480 | tf_op jit(solution)/shard_map/all_gather | solution.py:547
  241.7 40.2 %collective-permute-start.40 = (bf16[1184,384]{1,0:T(8,128)(2,1)}, bf16[1184,384]{1,0:T(8,128)(2,1)}, u32[]{:S(2)}, u32[]{:S(2)}) collective-permute-start(bf16[1184,384]{1,0:T(8,128)(2,1)} %add_convert_fusion.11), channel_id=1, source_target_pairs={{0,1},{1,0},{2,3},{3,2},{4,5},{5,4},{6,7},{7,6},{8,9},{9,8},{10,11... | collective-permute-start | bytes 2727944 | tf_op jit(solution)/shard_map/ppermute | solution.py:475
  243.3 65.0 %collective-permute-start.48 = (bf16[2,192,1536]{2,1,0:T(8,128)(2,1)S(1)}, bf16[2,192,1536]{2,1,0:T(8,128)(2,1)S(1)}, u32[]{:S(2)}, u32[]{:S(2)}) collective-permute-start(bf16[2,192,1536]{2,1,0:T(8,128)(2,1)S(1)} %bitcast.134), channel_id=1, source_target_pairs={{0,2},{2,0},{1,3},{3,1},{4,6},{6,4},{5,7},{7,5},{8,10},{10,8},{9,1... | collective-permute-start | bytes 3538952 | tf_op jit(solution)/shard_map/ppermute | solution.py:475
  313.3 322.2 %reduce-scatter.6.cloned.1.call-start = ((), (), s32[]{:S(2)}) async-start(), calls=%async_computation.8 | async-start | bytes 11796480 | tf_op jit(solution)/shard_map/reduce_scatter | solution.py:591
  487.3 218.5 %reduce-scatter.8.cloned.1.call-start = ((), (), s32[]{:S(2)}) async-start(), calls=%async_computation.9 | async-start | bytes 11796480 | tf_op jit(solution)/shard_map/reduce_scatter | solution.py:591
  562.3 231.1 %reduce-scatter.10.cloned.1.call-start = ((), (), s32[]{:S(2)}) async-start(), calls=%async_computation.10 | async-start | bytes 3538944 | tf_op jit(solution)/shard_map/reduce_scatter | solution.py:674
  567.8 44.6 %collective-permute-start.76 = (bf16[1184,384]{1,0:T(8,128)(2,1)}, bf16[1184,384]{1,0:T(8,128)(2,1)}, u32[]{:S(2)}, u32[]{:S(2)}) collective-permute-start(bf16[1184,384]{1,0:T(8,128)(2,1)} %add_convert_fusion.6), channel_id=1, source_target_pairs={{0,1},{1,0},{2,3},{3,2},{4,5},{5,4},{6,7},{7,6},{8,9},{9,8},{10,11... | collective-permute-start | bytes 2727944 | tf_op jit(solution)/shard_map/ppermute | solution.py:475
  674.4 192.4 %reduce-scatter.14.cloned.1.call-start = ((), (), s32[]{:S(2)}) async-start(), calls=%async_computation.12 | async-start | bytes 3538944 | tf_op jit(solution)/shard_map/reduce_scatter | solution.py:674
  723.1 194.5 %reduce-scatter.12.cloned.1.call-start = ((), (), s32[]{:S(2)}) async-start(), calls=%async_computation.11 | async-start | bytes 2949120 | tf_op jit(solution)/shard_map/reduce_scatter | solution.py:591
  744.9 213.8 %collective-permute-start.86 = (bf16[1184,384]{1,0:T(8,128)(2,1)}, bf16[1184,384]{1,0:T(8,128)(2,1)}, u32[]{:S(2)}, u32[]{:S(2)}) collective-permute-start(bf16[1184,384]{1,0:T(8,128)(2,1)} %get-tuple-element.704), channel_id=1, source_target_pairs={{2,4},{4,2},{3,5},{5,3},{10,12},{12,10},{11,13},{13,11},{18,20},{2... | collective-permute-start | bytes 2727944 | tf_op jit(solution)/shard_map/ppermute | solution.py:466
  746.5 113.7 %collective-permute-start.90 = (bf16[1184,384]{1,0:T(8,128)(2,1)}, bf16[1184,384]{1,0:T(8,128)(2,1)}, u32[]{:S(2)}, u32[]{:S(2)}) collective-permute-start(bf16[1184,384]{1,0:T(8,128)(2,1)} %add_convert_fusion.3), channel_id=1, source_target_pairs={{0,1},{1,0},{2,3},{3,2},{4,5},{5,4},{6,7},{7,6},{8,9},{9,8},{10,11... | collective-permute-start | bytes 2727944 | tf_op jit(solution)/shard_map/ppermute | solution.py:475
  760.3 63.7 %collective-permute-start.97 = (bf16[1184,384]{1,0:T(8,128)(2,1)S(1)}, bf16[1184,384]{1,0:T(8,128)(2,1)S(1)}, u32[]{:S(2)}, u32[]{:S(2)}) collective-permute-start(bf16[1184,384]{1,0:T(8,128)(2,1)S(1)} %add_convert_fusion.2), channel_id=1, source_target_pairs={{0,1},{1,0},{2,3},{3,2},{4,5},{5,4},{6,7},{7,6},{8,9},{9,8},{10,11... | collective-permute-start | bytes 2727944 | tf_op jit(solution)/shard_map/ppermute | solution.py:475
  833.2 75.6 %collective-permute-start.103 = (bf16[1184,384]{1,0:T(8,128)(2,1)}, bf16[1184,384]{1,0:T(8,128)(2,1)}, u32[]{:S(2)}, u32[]{:S(2)}) collective-permute-start(bf16[1184,384]{1,0:T(8,128)(2,1)} %add_convert_fusion.1), channel_id=1, source_target_pairs={{0,1},{1,0},{2,3},{3,2},{4,5},{5,4},{6,7},{7,6},{8,9},{9,8},{10,11... | collective-permute-start | bytes 2727944 | tf_op jit(solution)/shard_map/ppermute | solution.py:475
  862.4 41.1 %collective-permute-start.105 = (bf16[2,384,1152]{2,1,0:T(8,128)(2,1)}, bf16[2,384,1152]{2,1,0:T(8,128)(2,1)}, u32[]{:S(2)}, u32[]{:S(2)}) collective-permute-start(bf16[2,384,1152]{2,1,0:T(8,128)(2,1)} %get-tuple-element.945), channel_id=1, source_target_pairs={{0,8},{8,0},{16,24},{24,16},{1,9},{9,1},{17,25},{25,17},{2,10},{10... | collective-permute-start | bytes 5308424 | tf_op jit(solution)/shard_map/ppermute | solution.py:479
  863.7 41.8 %collective-permute-start.104 = (bf16[2,384,1152]{2,1,0:T(8,128)(2,1)}, bf16[2,384,1152]{2,1,0:T(8,128)(2,1)}, u32[]{:S(2)}, u32[]{:S(2)}) collective-permute-start(bf16[2,384,1152]{2,1,0:T(8,128)(2,1)} %get-tuple-element.947), channel_id=1, source_target_pairs={{0,16},{8,24},{16,0},{24,8},{1,17},{9,25},{17,1},{25,9},{2,18},{10... | collective-permute-start | bytes 5308424 | tf_op jit(solution)/shard_map/ppermute | solution.py:479
  918.7 39.3 %collective-permute-start.107 = (bf16[2,192,384]{2,1,0:T(8,128)(2,1)S(1)}, bf16[2,192,384]{2,1,0:T(8,128)(2,1)S(1)}, u32[]{:S(2)}, u32[]{:S(2)}) collective-permute-start(bf16[2,192,384]{2,1,0:T(8,128)(2,1)S(1)} %get-tuple-element.973), channel_id=1, source_target_pairs={{0,4},{4,0},{1,5},{5,1},{2,6},{6,2},{3,7},{7,3},{8,12},{12,8},{9,1... | collective-permute-start | bytes 884744 | tf_op jit(solution)/shard_map/ppermute | solution.py:475
  960.3 81.3 %collective-permute-start.115 = (bf16[2,192,1152]{2,1,0:T(8,128)(2,1)S(1)}, bf16[2,192,1152]{2,1,0:T(8,128)(2,1)S(1)}, u32[]{:S(2)}, u32[]{:S(2)}) collective-permute-start(bf16[2,192,1152]{2,1,0:T(8,128)(2,1)S(1)} %get-tuple-element.961), channel_id=1, source_target_pairs={{0,2},{2,0},{1,3},{3,1},{4,6},{6,4},{5,7},{7,5},{8,10},{10,8},{9,1... | collective-permute-start | bytes 2654216 | tf_op jit(solution)/shard_map/ppermute | solution.py:475
  981.7 59.9 %collective-permute-start.116 = (bf16[2,192,384]{2,1,0:T(8,128)(2,1)}, bf16[2,192,384]{2,1,0:T(8,128)(2,1)}, u32[]{:S(2)}, u32[]{:S(2)}) collective-permute-start(bf16[2,192,384]{2,1,0:T(8,128)(2,1)} %get-tuple-element.971), channel_id=1, source_target_pairs={{0,2},{2,0},{1,3},{3,1},{4,6},{6,4},{5,7},{7,5},{8,10},{10,8},{9,1... | collective-permute-start | bytes 884744 | tf_op jit(solution)/shard_map/ppermute | solution.py:475
  (201 other events, 2279.5 us)
Sparse Core Ops, SparseCore 0:
  180.4 107.6 all-gather.2
  313.4 96.9 all-gather.4
  487.5 93.5 reduce-scatter.5
  584.0 95.0 reduce-scatter.7
  681.2 60.9 reduce-scatter.9
  744.9 77.9 reduce-scatter.13
  825.9 35.3 reduce-scatter.11

commit v3 on v2

--- a/solution.py
+++ b/solution.py
@@ -18,6 +18,8 @@
 SWAP = [(0, 1), (1, 0)]
 BLOCK = 256
 ROWS = 512
+FORWARD = 1280
+BACKWARD = 256
 LANES = 128
 
 
@@ -246,7 +248,7 @@
 
 
 def live_rows(values, length):
-    row = lax.broadcasted_iota(jnp.int32, values.shape, 0) + pl.program_id(1) * BLOCK
+    row = lax.broadcasted_iota(jnp.int32, values.shape, 0) + pl.program_id(1) * values.shape[0]
     return jnp.where(row < length, values, jnp.zeros_like(values))
 
 
@@ -261,7 +263,7 @@
     scores = [nt(keys_in, head_mask(queries, head)) for head in range(2)]
     found = []
     for head in range(2):
-        row = lax.broadcasted_iota(jnp.int32, (keys_in.shape[0] - cut, BLOCK), 0)
+        row = lax.broadcasted_iota(jnp.int32, (keys_in.shape[0] - cut, FORWARD), 0)
         body = scores[head][:cut]
         tail = jnp.where(row < length - cut, scores[head][cut:], -1e30)
         highest = jnp.maximum(
@@ -278,23 +280,23 @@
 
 def attend(joint, length):
     rows, width = joint.shape[0], joint.shape[1] // 3
-    pairs, blocks = width // LANES, pl.cdiv(rows, BLOCK)
+    pairs, blocks = width // LANES, pl.cdiv(rows, FORWARD)
     area = 2 * pairs * rows * rows
     return pl.pallas_call(
         functools.partial(attend_kernel, length),
         out_shape=(
             jax.ShapeDtypeStruct((rows, width), LOW),
-            jax.ShapeDtypeStruct((pairs, 8, blocks * BLOCK), FULL),
+            jax.ShapeDtypeStruct((pairs, 8, blocks * FORWARD), FULL),
         ),
         grid=(pairs, blocks),
         in_specs=[
-            pl.BlockSpec((BLOCK, LANES), lambda p, i: (i, p)),
+            pl.BlockSpec((FORWARD, LANES), lambda p, i: (i, p)),
             pl.BlockSpec((rows, LANES), lambda p, i: (0, pairs + p)),
             pl.BlockSpec((rows, LANES), lambda p, i: (0, 2 * pairs + p)),
         ],
         out_specs=(
-            pl.BlockSpec((BLOCK, LANES), lambda p, i: (i, p)),
-            pl.BlockSpec((1, 8, BLOCK), lambda p, i: (p, 0, i)),
+            pl.BlockSpec((FORWARD, LANES), lambda p, i: (i, p)),
+            pl.BlockSpec((1, 8, FORWARD), lambda p, i: (p, 0, i)),
         ),
         scratch_shapes=[pltpu.VMEM((LANES, rows), LOW)],
         compiler_params=pltpu.CompilerParams(
@@ -331,7 +333,7 @@
     for head in range(2):
         scores.append(nt(keys_in, masked[head]))
         grad_soft.append(nt(values_in, above[head]))
-    row = lax.broadcasted_iota(jnp.int32, (rows - cut, BLOCK), 0)
+    row = lax.broadcasted_iota(jnp.int32, (rows - cut, BACKWARD), 0)
     found = []
     for head in range(2):
         raised = jnp.exp(scores[head] - log_ref[0, head : head + 1, :])
@@ -343,14 +345,14 @@
         key_sum[...] += nn(grad_scores, masked[head])
         found.append(nn(turned[head * HEAD_DIM : (head + 1) * HEAD_DIM, :], grad_scores))
     first = pl.multiple_of(pair * LANES, LANES)
-    start = pl.multiple_of(block * BLOCK, BLOCK)
+    start = pl.multiple_of(block * BACKWARD, BACKWARD)
     grad_queries = (jnp.concatenate(found, 0).T * scale).astype(LOW)
     last = pl.num_programs(1) - 1
-    left = rows - rows // BLOCK * BLOCK
+    left = rows - rows // BACKWARD * BACKWARD
 
     @pl.when((block < last) if left else (block <= last))
     def _():
-        out_ref[pl.ds(start, BLOCK), pl.ds(first, LANES)] = grad_queries
+        out_ref[pl.ds(start, BACKWARD), pl.ds(first, LANES)] = grad_queries
 
     if left:
 
@@ -368,18 +370,18 @@
 
 def attend_back(joint, log_total, upstream, length):
     rows, width = joint.shape[0], joint.shape[1] // 3
-    pairs, blocks = width // LANES, pl.cdiv(rows, BLOCK)
+    pairs, blocks = width // LANES, pl.cdiv(rows, BACKWARD)
     area = 2 * pairs * rows * rows
     return pl.pallas_call(
         functools.partial(attend_back_kernel, length),
         out_shape=jax.ShapeDtypeStruct((rows, 3 * width), LOW),
         grid=(pairs, blocks),
         in_specs=[
-            pl.BlockSpec((BLOCK, LANES), lambda p, i: (i, p)),
+            pl.BlockSpec((BACKWARD, LANES), lambda p, i: (i, p)),
             pl.BlockSpec((rows, LANES), lambda p, i: (0, pairs + p)),
             pl.BlockSpec((rows, LANES), lambda p, i: (0, 2 * pairs + p)),
-            pl.BlockSpec((BLOCK, LANES), lambda p, i: (i, p)),
-            pl.BlockSpec((1, 8, BLOCK), lambda p, i: (p, 0, i)),
+            pl.BlockSpec((BACKWARD, LANES), lambda p, i: (i, p)),
+            pl.BlockSpec((1, 8, BACKWARD), lambda p, i: (p, 0, i)),
         ],
         out_specs=pl.BlockSpec((rows, 3 * width), lambda p, i: (0, 0)),
         scratch_shapes=[
@@ -1019,7 +1021,6 @@
     down_sum.swap()
     grad_one_full[0], grad_attended = proj_back_step(pieces[0])
     outs[0], gate_two[0] = output_step(0, part_c[0], middle[0])
-    line.wait(pieces[1][1])
     part_c[1] = fold(part_c[1])
     down_sum.cross()
     grad_joint[0] = line.run(

time: 1060 us -> 1050 us (level)
  Pallas kernels: 360 us -> 346 us
    pallas_call x2, Pallas kernels: 45 us -> 31.4 us  [attend(): pl.pallas_call(functools.partial(attend_kernel, length), out_shape=(jax.S...]
  transfers between devices with their start and end apart: 124 -> 124, of which waited for: 48 -> 47; matrix products, arithmetic and copies ran while one was open for 13% -> 13% of each run, Pallas kernels for 34% -> 33%
where the time goes in v3:
time: 1050 us; the launch traced here: 1040 us
  Pallas kernels  346 us (33%)
  waiting for transfers between devices  334 us (32%)
  starting transfers between devices  169 us (16%)
  other arithmetic  109 us (10%)
  local copies, waits for them, and re-layouts  53.1 us (5%)
  between operations  17.8 us (2%)
    ppermute x83, waiting for transfers between devices, over(): return lax.ppermute(values, axis, SWAP)  228 us
    pallas_call x16, Pallas kernels, rows_call(): pl.pallas_call(functools.partial(rows_kernel, kernel, split, rows - image...  180 us
    ppermute x83, starting transfers between devices, over(): return lax.ppermute(values, axis, SWAP)  131 us
    ppermute x20, waiting for transfers between devices, over_planes(): return lax.ppermute(values, 'yx', [(i, i ^ bit) for i in range(planes)])  105 us
    pallas_call x4, Pallas kernels, weight_grad(): pl.pallas_call(functools.partial(weight_kernel, image), grid=(width // BL...  71 us
    pallas_call x2, Pallas kernels, attend_back(): pl.pallas_call(functools.partial(attend_back_kernel, length), out_shape=j...  62.8 us
    pallas_call x2, Pallas kernels, attend(): pl.pallas_call(functools.partial(attend_kernel, length), out_shape=(jax.S...  31.4 us
    ppermute x20, starting transfers between devices, over_planes(): return lax.ppermute(values, 'yx', [(i, i ^ bit) for i in range(planes)])  25.9 us
  transfers between devices with their start and end apart: 124, of which 47 were waited for; matrix products, arithmetic and copies ran while one was open for 13% of the time, Pallas kernels for 33%

profile of v3, /device:TPU:0, one launch (start us, length us, event | category | flops | bytes accessed | tf_op | source)
XLA Modules:
  0.0 1043.6 jit_solution(16811502533957661910)
XLA Ops:
  30.7 32.0 %collective-permute-done.9 = bf16[2,192,1152]{2,1,0:T(8,128)(2,1)} collective-permute-done((bf16[2,192,1152]{2,1,0:T(8,128)(2,1)}, bf16[2,192,1152]{2,1,0:T(8,128)(2,1)}, u32[]{:S(2)}, u32[]{:S(2)}) %collective-permute-start.9) | collective-permute-done | bytes 884768 | tf_op jit(solution)/shard_map/ppermute | solution.py:477
  82.5 21.2 %collective-permute-start.28 = (bf16[2,192,384]{2,1,0:T(8,128)(2,1)S(1)}, bf16[2,192,384]{2,1,0:T(8,128)(2,1)S(1)}, u32[]{:S(2)}, u32[]{:S(2)}) collective-permute-start(bf16[2,192,384]{2,1,0:T(8,128)(2,1)S(1)} %bitcast.142), channel_id=1, source_target_pairs={{0,2},{2,0},{1,3},{3,1},{4,6},{6,4},{5,7},{7,5},{8,10},{10,8},{9,1... | collective-permute-start | bytes 884744 | tf_op jit(solution)/shard_map/ppermute | solution.py:477
  124.8 29.1 %collective-permute-done.27.refs_3_ = bf16[768,1152]{1,0:T(8,128)(2,1)S(1)} collective-permute-done((bf16[768,1152]{1,0:T(8,128)(2,1)S(1)}, bf16[768,1152]{1,0:T(8,128)(2,1)S(1)}, u32[]{:S(2)}, u32[]{:S(2)}) %collective-permute-start.27) | collective-permute-done | bytes 1769504 | tf_op jit(solution)/shard_map/ppermute | solution.py:481
  192.3 15.7 %attend.2 = (bf16[1184,384]{1,0:T(8,128)(2,1)}, f32[3,8,1280]{2,1,0:T(8,128)}) custom-call(bf16[1184,1152]{1,0:T(8,128)(2,1)} %get-tuple-element.618.q_ref.k_ref.v_ref, bf16[1184,1152]{1,0:T(8,128)(2,1)} %get-tuple-element.618.q_ref.k_ref.v_ref, bf16[1184,1152]{1,0:T(8,128)(2,1)} %get-tuple-element.618.q_ref.k_ref.v_ref), custom_call_target="tpu_custom_call" | custom-call | flops 21532508160 | bytes 4091904 | tf_op jit(solution)/shard_map/attend/pallas_call | solution.py:285
  239.2 16.1 %collective-permute-start.48 = (bf16[2,192,1536]{2,1,0:T(8,128)(2,1)S(1)}, bf16[2,192,1536]{2,1,0:T(8,128)(2,1)S(1)}, u32[]{:S(2)}, u32[]{:S(2)}) collective-permute-start(bf16[2,192,1536]{2,1,0:T(8,128)(2,1)S(1)} %bitcast.134), channel_id=1, source_target_pairs={{0,2},{2,0},{1,3},{3,1},{4,6},{6,4},{5,7},{7,5},{8,10},{10,8},{9,1... | collective-permute-start | bytes 3538952 | tf_op jit(solution)/shard_map/ppermute | solution.py:477
  281.4 15.7 %attend.3 = (bf16[1184,384]{1,0:T(8,128)(2,1)}, f32[3,8,1280]{2,1,0:T(8,128)}) custom-call(bf16[1184,1152]{1,0:T(8,128)(2,1)} %get-tuple-element.645.q_ref.k_ref.v_ref, bf16[1184,1152]{1,0:T(8,128)(2,1)} %get-tuple-element.645.q_ref.k_ref.v_ref, bf16[1184,1152]{1,0:T(8,128)(2,1)} %get-tuple-element.645.q_ref.k_ref.v_ref), custom_call_target="tpu_custom_call" | custom-call | flops 21532508160 | bytes 4091904 | tf_op jit(solution)/shard_map/attend/pallas_call | solution.py:285
  344.3 15.2 %up.2 = (bf16[1184,1536]{1,0:T(8,128)(2,1)}, f32[1184,1536]{1,0:T(8,128)}, bf16[1184,1536]{1,0:T(8,128)(2,1)}) custom-call(s32[2]{0:T(128)} %pad_add_fusion.here_ref, bf16[1184,384]{1,0:T(8,128)(2,1)} %copy-done.64, bf16[1184,384]{1,0:T(8,128)(2,1)} %copy-done.95, bf16[1184,384]{1,0:T(8,128)(2,1)} %copy-done.94, ...), custom_call_target="tpu_custom_call" | custom-call | flops 5586812928 | bytes 27635712 | tf_op jit(solution)/shard_map/up/pallas_call | solution.py:80
  377.0 20.7 %collective-permute-done.59.refs_1_ = bf16[1184,384]{1,0:T(8,128)(2,1)S(1)} collective-permute-done((bf16[1184,384]{1,0:T(8,128)(2,1)S(1)}, bf16[1184,384]{1,0:T(8,128)(2,1)S(1)}, u32[]{:S(2)}, u32[]{:S(2)}) %collective-permute-start.59) | collective-permute-done | bytes 909344 | tf_op jit(solution)/shard_map/ppermute | solution.py:477
  402.3 15.1 %up.3 = (bf16[1184,1536]{1,0:T(8,128)(2,1)}, f32[1184,1536]{1,0:T(8,128)}, bf16[1184,1536]{1,0:T(8,128)(2,1)}) custom-call(s32[2]{0:T(128)} %pad_add_fusion.here_ref, bf16[1184,384]{1,0:T(8,128)(2,1)} %copy-done.67, bf16[1184,384]{1,0:T(8,128)(2,1)} %copy-done.99, bf16[1184,384]{1,0:T(8,128)(2,1)} %copy-done.100, ...), custom_call_target="tpu_custom_call" | custom-call | flops 5586812928 | bytes 27635712 | tf_op jit(solution)/shard_map/up/pallas_call | solution.py:80
  417.5 14.2 %collective-permute-done.63.refs_1_ = bf16[1184,384]{1,0:T(8,128)(2,1)S(1)} collective-permute-done((bf16[1184,384]{1,0:T(8,128)(2,1)S(1)}, bf16[1184,384]{1,0:T(8,128)(2,1)S(1)}, u32[]{:S(2)}, u32[]{:S(2)}) %collective-permute-start.63) | collective-permute-done | bytes 909344 | tf_op jit(solution)/shard_map/ppermute | solution.py:477
  435.8 20.2 %collective-permute-done.64.refs_1_ = bf16[1184,384]{1,0:T(8,128)(2,1)S(1)} collective-permute-done((bf16[1184,384]{1,0:T(8,128)(2,1)S(1)}, bf16[1184,384]{1,0:T(8,128)(2,1)S(1)}, u32[]{:S(2)}, u32[]{:S(2)}) %collective-permute-start.64) | collective-permute-done | bytes 909344 | tf_op jit(solution)/shard_map/ppermute | solution.py:477
  467.2 20.6 %weight_grad.4 = (bf16[2,1536,1536]{2,1,0:T(8,128)(2,1)}, f32[2,1,1536]{2,1,0:T(1,128)}) custom-call(bf16[1184,1536]{1,0:T(8,128)(2,1)} %gather.2.left_zero.refs_0_, bf16[1184,1536]{1,0:T(8,128)(2,1)} %gather.3.left_one.refs_0_, bf16[1184,1536]{1,0:T(8,128)(2,1)} %get-tuple-element.567.right_zero.refs_0_, bf16[1184,1536]{1,0:T(8,128)(2,1)} %get-tuple-element.580.right_one.refs_0_), custom_call_target="tpu_custom_call" | custom-call | flops 11173625856 | bytes 23986176 | tf_op jit(solution)/shard_map/weight_grad/pallas_call | solution.py:220
  487.9 22.4 %mlp_back.2 = (bf16[1184,1536]{1,0:T(8,128)(2,1)}, bf16[1184,384]{1,0:T(8,128)(2,1)}, bf16[1184,384]{1,0:T(8,128)(2,1)}, bf16[1184,384]{1,0:T(8,128)(2,1)}, bf16[1184,384]{1,0:T(8,128)(2,1)}) custom-call(s32[2]{0:T(128)} %pad_add_fusion.here_ref, bf16[1184,1536]{1,0:T(8,128)(2,1)} %gather.2.left_zero.refs_0_, f32[1184,1536]{1,0:T(8,128)} %get-tuple-element.537.refs_1_, ...), custom_call_target="tpu_custom_call" | custom-call | flops 11173625856 | bytes 37060608 | tf_op jit(solution)/shard_map/mlp_back/pallas_call | solution.py:80
  515.8 22.4 %mlp_back.3 = (bf16[1184,1536]{1,0:T(8,128)(2,1)}, bf16[1184,384]{1,0:T(8,128)(2,1)}, bf16[1184,384]{1,0:T(8,128)(2,1)}, bf16[1184,384]{1,0:T(8,128)(2,1)}, bf16[1184,384]{1,0:T(8,128)(2,1)}) custom-call(s32[2]{0:T(128)} %pad_add_fusion.here_ref, bf16[1184,1536]{1,0:T(8,128)(2,1)} %gather.3.left_one.refs_0_, f32[1184,1536]{1,0:T(8,128)} %get-tuple-element.547.refs_1_, ...), custom_call_target="tpu_custom_call" | custom-call | flops 11173625856 | bytes 37060608 | tf_op jit(solution)/shard_map/mlp_back/pallas_call | solution.py:80
  541.9 20.8 %weight_grad.5 = (bf16[2,1536,1536]{2,1,0:T(8,128)(2,1)}, f32[2,1,1536]{2,1,0:T(1,128)}) custom-call(bf16[1184,1536]{1,0:T(8,128)(2,1)} %get-tuple-element.559.left_zero, bf16[1184,1536]{1,0:T(8,128)(2,1)} %get-tuple-element.560.left_one, bf16[1184,1536]{1,0:T(8,128)(2,1)} %get-tuple-element.561.right_zero, bf16[1184,1536]{1,0:T(8,128)(2,1)} %get-tuple-element.562.right_one), custom_call_target="tpu_custom_call" | custom-call | flops 11173625856 | bytes 23986176 | tf_op jit(solution)/shard_map/weight_grad/pallas_call | solution.py:220
  660.7 31.6 %attend_back.2.refs_0_.right_zero = bf16[1184,1152]{1,0:T(8,128)(2,1)} custom-call(bf16[1184,1152]{1,0:T(8,128)(2,1)} %get-tuple-element.618.q_ref.k_ref.v_ref, bf16[1184,1152]{1,0:T(8,128)(2,1)} %get-tuple-element.618.q_ref.k_ref.v_ref, bf16[1184,1152]{1,0:T(8,128)(2,1)} %get-tuple-element.618.q_ref.k_ref.v_ref, ...), custom_call_target="tpu_custom_call" | custom-call | flops 32298762240 | bytes 8183808 | tf_op jit(solution)/shard_map/attend_back/pallas_call | solution.py:375
  748.5 31.2 %attend_back.3.refs_0_.right_one = bf16[1184,1152]{1,0:T(8,128)(2,1)} custom-call(bf16[1184,1152]{1,0:T(8,128)(2,1)} %get-tuple-element.645.q_ref.k_ref.v_ref, bf16[1184,1152]{1,0:T(8,128)(2,1)} %get-tuple-element.645.q_ref.k_ref.v_ref, bf16[1184,1152]{1,0:T(8,128)(2,1)} %get-tuple-element.645.q_ref.k_ref.v_ref, ...), custom_call_target="tpu_custom_call" | custom-call | flops 32298762240 | bytes 8183808 | tf_op jit(solution)/shard_map/attend_back/pallas_call | solution.py:375
  792.9 22.0 %collective-permute-done.97 = bf16[1184,384]{1,0:T(8,128)(2,1)S(1)} collective-permute-done((bf16[1184,384]{1,0:T(8,128)(2,1)S(1)}, bf16[1184,384]{1,0:T(8,128)(2,1)S(1)}, u32[]{:S(2)}, u32[]{:S(2)}) %collective-permute-start.97) | collective-permute-done | bytes 909344 | tf_op jit(solution)/shard_map/ppermute | solution.py:477
  824.1 19.1 %weight_grad.7 = (bf16[2,1536,1152]{2,1,0:T(8,128)(2,1)}, f32[2,1,1152]{2,1,0:T(1,128)}) custom-call(bf16[1184,1536]{1,0:T(8,128)(2,1)} %get-tuple-element.662.left_zero, bf16[1184,1536]{1,0:T(8,128)(2,1)} %get-tuple-element.663.left_one, bf16[1184,1152]{1,0:T(8,128)(2,1)} %attend_back.2.refs_0_.right_zero, bf16[1184,1152]{1,0:T(8,128)(2,1)} %attend_back.3.refs_0_.right_one), custom_call_target="tpu_custom_call" | custom-call | flops 8380219392 | bytes 19808256 | tf_op jit(solution)/shard_map/weight_grad/pallas_call | solution.py:220
  861.2 33.9 %collective-permute-done.105 = bf16[2,384,1152]{2,1,0:T(8,128)(2,1)} collective-permute-done((bf16[2,384,1152]{2,1,0:T(8,128)(2,1)}, bf16[2,384,1152]{2,1,0:T(8,128)(2,1)}, u32[]{:S(2)}, u32[]{:S(2)}) %collective-permute-start.105) | collective-permute-done | bytes 1769504 | tf_op jit(solution)/shard_map/ppermute | solution.py:481
  922.4 15.7 %collective-permute-done.108 = bf16[384,1152]{1,0:T(8,128)(2,1)S(1)} collective-permute-done((bf16[384,1152]{1,0:T(8,128)(2,1)S(1)}, bf16[384,1152]{1,0:T(8,128)(2,1)S(1)}, u32[]{:S(2)}, u32[]{:S(2)}) %collective-permute-start.108) | collective-permute-done | bytes 884768 | tf_op jit(solution)/shard_map/ppermute | solution.py:481
  951.3 20.9 %collective-permute-start.115 = (bf16[2,192,1152]{2,1,0:T(8,128)(2,1)S(1)}, bf16[2,192,1152]{2,1,0:T(8,128)(2,1)S(1)}, u32[]{:S(2)}, u32[]{:S(2)}) collective-permute-start(bf16[2,192,1152]{2,1,0:T(8,128)(2,1)S(1)} %get-tuple-element.961), channel_id=1, source_target_pairs={{0,2},{2,0},{1,3},{3,1},{4,6},{6,4},{5,7},{7,5},{8,10},{10,8},{9,1... | collective-permute-start | bytes 2654216 | tf_op jit(solution)/shard_map/ppermute | solution.py:477
  974.6 58.3 %conditional.1 = (f32[2,1536]{1,0:T(2,128)S(1)}, f32[2,192,6,384]{3,1,2,0:T(8,128)}, f32[2,3072]{1,0:T(2,128)}, f32[2,768]{1,0:T(2,128)}, f32[2,384]{1,0:T(2,128...) conditional(s32[]{:T(128)} %bitcast.61, () %tuple.203, ...), branch_computations={%region_49.50_spmd, %region_50.52_spmd} | conditional | flops 58154508 | bytes 8399401 | solution.py:460
  1000.3 23.5 %collective-permute-done.3 = f32[2,1536]{1,0:T(2,128)S(1)} collective-permute-done((f32[2,1536]{1,0:T(2,128)S(1)}, f32[2,1536]{1,0:T(2,128)S(1)}, u32[]{:S(2)}, u32[]{:S(2)}) %collective-permute-start.3) | collective-permute-done | bytes 12320 | tf_op jit(solution)/shard_map/cond/branch_1_fun/ppermute | solution.py:477
  (770 shorter events, 526.6 us)
Async XLA Ops:
  7.2 337.1 %all-gather.3.cloned.1.call-start = ((), (), s32[]{:S(2)}) async-start(), calls=%async_computation.6 | async-start | bytes 11796480 | tf_op jit(solution)/shard_map/all_gather | solution.py:549
  23.2 39.4 %collective-permute-start.9 = (bf16[2,192,1152]{2,1,0:T(8,128)(2,1)}, bf16[2,192,1152]{2,1,0:T(8,128)(2,1)}, u32[]{:S(2)}, u32[]{:S(2)}) collective-permute-start(bf16[2,192,1152]{2,1,0:T(8,128)(2,1)} %bitcast.74), channel_id=1, source_target_pairs={{0,2},{2,0},{1,3},{3,1},{4,6},{6,4},{5,7},{7,5},{8,10},{10,8},{9,1... | collective-permute-start | bytes 2654216 | tf_op jit(solution)/shard_map/ppermute | solution.py:477
  28.0 39.9 %collective-permute-start.30 = (f32[2,2,384]{2,0,1:T(2,128)S(1)}, f32[2,2,384]{2,0,1:T(2,128)S(1)}, u32[]{:S(2)}, u32[]{:S(2)}) collective-permute-start(f32[2,2,384]{2,0,1:T(2,128)S(1)} %copy_convert_fusion), channel_id=1, source_target_pairs={{2,4},{4,2},{3,5},{5,3},{10,12},{12,10},{11,13},{13,11},{18,20},{2... | collective-permute-start | bytes 18440 | tf_op jit(solution)/shard_map/ppermute | solution.py:468
  72.4 47.9 %collective-permute-start.23 = (f32[2,2,2,768]{3,2,1,0:T(2,128)S(1)}, f32[2,2,2,768]{3,2,1,0:T(2,128)S(1)}, u32[]{:S(2)}, u32[]{:S(2)}) collective-permute-start(f32[2,2,2,768]{3,2,1,0:T(2,128)S(1)} %maximum_select_fusion.20), channel_id=1, source_target_pairs={{0,4},{4,0},{1,5},{5,1},{2,6},{6,2},{3,7},{7,3},{8,12},{12,8},{9,1... | collective-permute-start | bytes 73736 | tf_op jit(solution)/shard_map/ppermute | solution.py:477
  104.3 49.6 %collective-permute-start.26 = (bf16[768,1152]{1,0:T(8,128)(2,1)S(1)}, bf16[768,1152]{1,0:T(8,128)(2,1)S(1)}, u32[]{:S(2)}, u32[]{:S(2)}) collective-permute-start(bf16[768,1152]{1,0:T(8,128)(2,1)S(1)} %maximum_select_fusion.9.refs_0_), channel_id=1, source_target_pairs={{0,16},{8,24},{16,0},{24,8},{1,17},{9,25},{17,1},{25,9},{2,18},{10... | collective-permute-start | bytes 5308424 | tf_op jit(solution)/shard_map/ppermute | solution.py:481
  120.5 55.0 %collective-permute-start.33 = (bf16[2,192,1536]{2,1,0:T(8,128)(2,1)S(1)}, bf16[2,192,1536]{2,1,0:T(8,128)(2,1)S(1)}, u32[]{:S(2)}, u32[]{:S(2)}) collective-permute-start(bf16[2,192,1536]{2,1,0:T(8,128)(2,1)S(1)} %copy-done.46), channel_id=1, source_target_pairs={{0,2},{2,0},{1,3},{3,1},{4,6},{6,4},{5,7},{7,5},{8,10},{10,8},{9,1... | collective-permute-start | bytes 3538952 | tf_op jit(solution)/shard_map/ppermute | solution.py:477
  180.3 307.6 %all-gather.5.cloned.1.call-start = ((), (), s32[]{:S(2)}) async-start(), calls=%async_computation.7 | async-start | bytes 11796480 | tf_op jit(solution)/shard_map/all_gather | solution.py:549
  237.2 40.4 %collective-permute-start.40 = (bf16[1184,384]{1,0:T(8,128)(2,1)}, bf16[1184,384]{1,0:T(8,128)(2,1)}, u32[]{:S(2)}, u32[]{:S(2)}) collective-permute-start(bf16[1184,384]{1,0:T(8,128)(2,1)} %add_convert_fusion.11), channel_id=1, source_target_pairs={{0,1},{1,0},{2,3},{3,2},{4,5},{5,4},{6,7},{7,6},{8,9},{9,8},{10,11... | collective-permute-start | bytes 2727944 | tf_op jit(solution)/shard_map/ppermute | solution.py:477
  239.2 65.8 %collective-permute-start.48 = (bf16[2,192,1536]{2,1,0:T(8,128)(2,1)S(1)}, bf16[2,192,1536]{2,1,0:T(8,128)(2,1)S(1)}, u32[]{:S(2)}, u32[]{:S(2)}) collective-permute-start(bf16[2,192,1536]{2,1,0:T(8,128)(2,1)S(1)} %bitcast.134), channel_id=1, source_target_pairs={{0,2},{2,0},{1,3},{3,1},{4,6},{6,4},{5,7},{7,5},{8,10},{10,8},{9,1... | collective-permute-start | bytes 3538952 | tf_op jit(solution)/shard_map/ppermute | solution.py:477
  312.4 323.4 %reduce-scatter.6.cloned.1.call-start = ((), (), s32[]{:S(2)}) async-start(), calls=%async_computation.8 | async-start | bytes 11796480 | tf_op jit(solution)/shard_map/reduce_scatter | solution.py:593
  487.8 204.4 %reduce-scatter.8.cloned.1.call-start = ((), (), s32[]{:S(2)}) async-start(), calls=%async_computation.9 | async-start | bytes 11796480 | tf_op jit(solution)/shard_map/reduce_scatter | solution.py:593
  562.7 216.9 %reduce-scatter.10.cloned.1.call-start = ((), (), s32[]{:S(2)}) async-start(), calls=%async_computation.10 | async-start | bytes 3538944 | tf_op jit(solution)/shard_map/reduce_scatter | solution.py:676
  568.3 44.0 %collective-permute-start.76 = (bf16[1184,384]{1,0:T(8,128)(2,1)}, bf16[1184,384]{1,0:T(8,128)(2,1)}, u32[]{:S(2)}, u32[]{:S(2)}) collective-permute-start(bf16[1184,384]{1,0:T(8,128)(2,1)} %add_convert_fusion.6), channel_id=1, source_target_pairs={{0,1},{1,0},{2,3},{3,2},{4,5},{5,4},{6,7},{7,6},{8,9},{9,8},{10,11... | collective-permute-start | bytes 2727944 | tf_op jit(solution)/shard_map/ppermute | solution.py:477
  638.6 56.0 %collective-permute-start.92 = (bf16[1184,384]{1,0:T(8,128)(2,1)}, bf16[1184,384]{1,0:T(8,128)(2,1)}, u32[]{:S(2)}, u32[]{:S(2)}) collective-permute-start(bf16[1184,384]{1,0:T(8,128)(2,1)} %get-tuple-element.622.refs_0_), channel_id=1, source_target_pairs={{0,1},{1,0},{2,3},{3,2},{4,5},{5,4},{6,7},{7,6},{8,9},{9,8},{10,11... | collective-permute-start | bytes 2727944 | tf_op jit(solution)/shard_map/ppermute | solution.py:477
  660.6 197.4 %reduce-scatter.14.cloned.1.call-start = ((), (), s32[]{:S(2)}) async-start(), calls=%async_computation.12 | async-start | bytes 3538944 | tf_op jit(solution)/shard_map/reduce_scatter | solution.py:676
  709.8 198.8 %reduce-scatter.12.cloned.1.call-start = ((), (), s32[]{:S(2)}) async-start(), calls=%async_computation.11 | async-start | bytes 2949120 | tf_op jit(solution)/shard_map/reduce_scatter | solution.py:593
  731.4 119.9 %collective-permute-start.89 = (bf16[1184,384]{1,0:T(8,128)(2,1)}, bf16[1184,384]{1,0:T(8,128)(2,1)}, u32[]{:S(2)}, u32[]{:S(2)}) collective-permute-start(bf16[1184,384]{1,0:T(8,128)(2,1)} %add_convert_fusion.3), channel_id=1, source_target_pairs={{0,1},{1,0},{2,3},{3,2},{4,5},{5,4},{6,7},{7,6},{8,9},{9,8},{10,11... | collective-permute-start | bytes 2727944 | tf_op jit(solution)/shard_map/ppermute | solution.py:477
  732.3 217.5 %collective-permute-start.86 = (bf16[1184,384]{1,0:T(8,128)(2,1)}, bf16[1184,384]{1,0:T(8,128)(2,1)}, u32[]{:S(2)}, u32[]{:S(2)}) collective-permute-start(bf16[1184,384]{1,0:T(8,128)(2,1)} %get-tuple-element.704), channel_id=1, source_target_pairs={{2,4},{4,2},{3,5},{5,3},{10,12},{12,10},{11,13},{13,11},{18,20},{2... | collective-permute-start | bytes 2727944 | tf_op jit(solution)/shard_map/ppermute | solution.py:468
  747.1 67.7 %collective-permute-start.97 = (bf16[1184,384]{1,0:T(8,128)(2,1)S(1)}, bf16[1184,384]{1,0:T(8,128)(2,1)S(1)}, u32[]{:S(2)}, u32[]{:S(2)}) collective-permute-start(bf16[1184,384]{1,0:T(8,128)(2,1)S(1)} %add_convert_fusion.2), channel_id=1, source_target_pairs={{0,1},{1,0},{2,3},{3,2},{4,5},{5,4},{6,7},{7,6},{8,9},{9,8},{10,11... | collective-permute-start | bytes 2727944 | tf_op jit(solution)/shard_map/ppermute | solution.py:477
  824.1 74.2 %collective-permute-start.103 = (bf16[1184,384]{1,0:T(8,128)(2,1)}, bf16[1184,384]{1,0:T(8,128)(2,1)}, u32[]{:S(2)}, u32[]{:S(2)}) collective-permute-start(bf16[1184,384]{1,0:T(8,128)(2,1)} %add_convert_fusion.1), channel_id=1, source_target_pairs={{0,1},{1,0},{2,3},{3,2},{4,5},{5,4},{6,7},{7,6},{8,9},{9,8},{10,11... | collective-permute-start | bytes 2727944 | tf_op jit(solution)/shard_map/ppermute | solution.py:477
  853.5 41.5 %collective-permute-start.105 = (bf16[2,384,1152]{2,1,0:T(8,128)(2,1)}, bf16[2,384,1152]{2,1,0:T(8,128)(2,1)}, u32[]{:S(2)}, u32[]{:S(2)}) collective-permute-start(bf16[2,384,1152]{2,1,0:T(8,128)(2,1)} %get-tuple-element.945), channel_id=1, source_target_pairs={{0,8},{8,0},{16,24},{24,16},{1,9},{9,1},{17,25},{25,17},{2,10},{10... | collective-permute-start | bytes 5308424 | tf_op jit(solution)/shard_map/ppermute | solution.py:481
  855.0 40.1 %collective-permute-start.104 = (bf16[2,384,1152]{2,1,0:T(8,128)(2,1)}, bf16[2,384,1152]{2,1,0:T(8,128)(2,1)}, u32[]{:S(2)}, u32[]{:S(2)}) collective-permute-start(bf16[2,384,1152]{2,1,0:T(8,128)(2,1)} %get-tuple-element.947), channel_id=1, source_target_pairs={{0,16},{8,24},{16,0},{24,8},{1,17},{9,25},{17,1},{25,9},{2,18},{10... | collective-permute-start | bytes 5308424 | tf_op jit(solution)/shard_map/ppermute | solution.py:481
  951.3 81.7 %collective-permute-start.115 = (bf16[2,192,1152]{2,1,0:T(8,128)(2,1)S(1)}, bf16[2,192,1152]{2,1,0:T(8,128)(2,1)S(1)}, u32[]{:S(2)}, u32[]{:S(2)}) collective-permute-start(bf16[2,192,1152]{2,1,0:T(8,128)(2,1)S(1)} %get-tuple-element.961), channel_id=1, source_target_pairs={{0,2},{2,0},{1,3},{3,1},{4,6},{6,4},{5,7},{7,5},{8,10},{10,8},{9,1... | collective-permute-start | bytes 2654216 | tf_op jit(solution)/shard_map/ppermute | solution.py:477
  973.1 59.9 %collective-permute-start.116 = (bf16[2,192,384]{2,1,0:T(8,128)(2,1)}, bf16[2,192,384]{2,1,0:T(8,128)(2,1)}, u32[]{:S(2)}, u32[]{:S(2)}) collective-permute-start(bf16[2,192,384]{2,1,0:T(8,128)(2,1)} %get-tuple-element.971), channel_id=1, source_target_pairs={{0,2},{2,0},{1,3},{3,1},{4,6},{6,4},{5,7},{7,5},{8,10},{10,8},{9,1... | collective-permute-start | bytes 884744 | tf_op jit(solution)/shard_map/ppermute | solution.py:477
  (201 other events, 2264.9 us)
Sparse Core Ops, SparseCore 0:
  180.4 107.6 all-gather.2
  312.5 97.5 all-gather.4
  487.9 93.2 reduce-scatter.5
  584.2 95.0 reduce-scatter.7
  681.4 62.4 reduce-scatter.9
  746.7 69.2 reduce-scatter.13
  819.0 36.7 reduce-scatter.11
